TPU v7x, 256 devices: a whole 4x4x8 slice. The times are simulated.
256 devices in a mesh: branch: 2 (over x_lo), strip: 128 (over y, z, x_hi, core).
Axes of the slice: x: 4 (x_hi: 2, x_lo: 2; x = x_hi * 2 + x_lo), y: 4, z: 8, core: 2. Of those that a mesh axis runs over, the one named last changes fastest.
Arguments:
- image_feats: bfloat16 [32, 16384, 256], P(None, ('branch', 'strip')), may hold values from -6 to 6
- cam_weights: bfloat16 [3, 9, 256, 256], replicated, may hold values from -0.1875 to 0.1875
- depth_weight: bfloat16 [256, 118], replicated, may hold values from -1.5 to 1.5
- ray_bins: int32 [16384, 118], P(('branch', 'strip')), may hold values from 0 to 16383, as said below
- pillar_sums: bfloat16 [32, 2048, 128], P(None, ('branch', 'strip')), may hold values from -12 to 12
- pillar_counts: int32 [32, 2048], P(None, ('branch', 'strip')), may hold values from 0 to 8
- lidar_weight: bfloat16 [4, 128, 128], replicated, may hold values from -0.375 to 0.375
- merge_weight: bfloat16 [9, 384, 256], replicated, may hold values from -0.15625 to 0.15625
- out_cotangent: bfloat16 [16, 1024, 256], P(None, ('branch', 'strip')), may hold values from -6 to 6
Outputs:
- merged: bfloat16 [16, 1024, 256], P(None, ('branch', 'strip'))
- cam_grad: bfloat16 [32, 16384, 256], P(None, ('branch', 'strip'))
- lid_grad: bfloat16 [16, 1024, 128], P(None, ('branch', 'strip'))
Inputs may be any that keep to these rules, and one draw needn't show every extreme that they name: For a column j of sector s = j // 64, ray_bins[j, k] lies in sector s - 1, s or s + 1 taken modulo 256, in cycle k * 16 // 118.
All inputs are finite; a program needn't handle non-finite values.
Results may differ from a plain program's by a relative error of at most 0.014.
Values may be sent and summed in bfloat16 or wider, within the bound.
No kernel may reach another device: no remote copies, remote signals or barrier semaphores. Data moves between devices by JAX's collectives and lax.ppermute only.
A program may use at most 128 MiB of HBM per device.

v0:
```python
import jax
import jax.numpy as jnp
from jax import lax
from jax.experimental import pallas as pl
from jax.experimental.pallas import tpu as pltpu
from jax.sharding import PartitionSpec as P

AXES = ("branch", "strip")
ROWS = 32
COLS = 64
WIDE = 80
C = 256
CL = 128
BINS = 118
LANES = 128
LAYERS = 3
BR = 16
BA = 4
WIN = 16
REACH = 6
SLOTS = 12
BLOCK = 8
TILE_H = 4
TILE = TILE_H * COLS
F32 = jnp.float32
BF16 = jnp.bfloat16


def whole(memory_space=pltpu.VMEM):
    return pl.BlockSpec(memory_space=memory_space)


def iota(shape, dim):
    return lax.broadcasted_iota(jnp.int32, shape, dim)


def nt_dot(lhs, rhs):
    return lax.dot_general(lhs, rhs, (((1,), (1,)), ((), ())), preferred_element_type=F32)


def tn_dot(lhs, rhs):
    return lax.dot_general(lhs, rhs, (((0,), (0,)), ((), ())), preferred_element_type=F32)


def dot(lhs, rhs):
    return jnp.dot(lhs, rhs, preferred_element_type=F32)


def fill_spread(spread):
    bin_index = iota((LANES, WIN * BR), 0)
    column = iota((LANES, WIN * BR), 1)
    for slot in range(SLOTS):
        offset = (column - (slot + 2) * BR) * BINS
        hit = (offset <= bin_index * BR) & (bin_index * BR < offset + BINS)
        spread[slot * LANES : (slot + 1) * LANES, :] = hit.astype(F32).astype(BF16)


def front_kernel(
    me_ref, image, from_right, from_left, weights, depth, bins,
    feat_out, share_out, lifted_out, probs_out, gain_out, slot_out,
    first, second, depth_pad, spread, masks,
):
    first[0] = jnp.zeros((WIDE, C), BF16)
    first[ROWS + 1] = jnp.zeros((WIDE, C), BF16)
    second[0] = jnp.zeros((WIDE, C), BF16)
    second[ROWS + 1] = jnp.zeros((WIDE, C), BF16)
    first[1 : ROWS + 1, 0:COLS, :] = image[...]
    first[1 : ROWS + 1, COLS:WIDE, :] = jnp.concatenate(
        [from_right[...], from_left[...]], axis=1
    )
    depth_pad[...] = jnp.zeros((C, LANES), BF16)
    depth_pad[:, 0:BINS] = depth[...]
    fill_spread(spread)
    cells = bins[...]
    sector = cells // (BR * BA)
    step = sector - me_ref[0] + 1
    step = jnp.where(step < 0, step + 256, step)
    step = jnp.where(step > 255, step - 256, step)
    slot = step * BA + cells % BA
    slot_out[...] = jnp.full((COLS, LANES), -1, jnp.int32)
    slot_out[:, 0:BINS] = slot
    slot_map = slot_out[...]
    for index in range(SLOTS):
        masks[index] = (slot_map == index).astype(F32).astype(BF16)

    def layer(source, target, index):
        @pl.loop(0, ROWS // BLOCK)
        def _(block):
            top = block * BLOCK
            lhs = jnp.concatenate(
                [
                    source[pl.ds(top + down, BLOCK)].reshape(BLOCK * WIDE, C)
                    for down in range(3)
                ],
                axis=1,
            )
            out = None
            for right in range(3):
                kernel = jnp.concatenate(
                    [weights[index, 3 * down + right] for down in range(3)], axis=0
                )
                part = dot(lhs, kernel).reshape(BLOCK, WIDE, C)
                if right != 1:
                    part = pltpu.roll(part, (1 - right) % WIDE, 1)
                out = part if out is None else out + part
            target[pl.ds(top + 1, BLOCK)] = jnp.maximum(out, 0.0).astype(BF16)

    layer(first, second, 0)
    layer(second, first, 1)
    layer(first, second, 2)

    lifted_out[...] = jnp.zeros((WIN * BR, C), F32)
    lane_ok = iota((TILE, LANES), 1) < BINS

    @pl.loop(0, ROWS // TILE_H)
    def _(tile):
        top = tile * TILE_H
        block = second[pl.ds(top + 1, TILE_H), 0:COLS, :].reshape(TILE, C)
        feat_out[pl.ds(tile * TILE, TILE), :] = block
        logits = dot(block, depth_pad[...])
        decay = jnp.exp(-jnp.abs(logits))
        soft = jnp.maximum(logits, 0.0) + jnp.log(1.0 + decay) + 0.05
        soft = jnp.where(lane_ok, soft, 0.0)
        scale = 1.0 / jnp.sum(soft, axis=1, keepdims=True)
        probs = soft * scale
        gate = jnp.where(logits >= 0.0, 1.0, decay) / (1.0 + decay)
        probs_out[pl.ds(tile * TILE, TILE), :] = probs
        gain_out[pl.ds(tile * TILE, TILE), :] = gate * scale
        low = probs.astype(BF16).reshape(TILE_H, COLS, LANES)
        share = dot(
            jnp.concatenate(
                [
                    (low * masks[index][None]).reshape(TILE, LANES)
                    for index in range(SLOTS)
                ],
                axis=1,
            ),
            spread[...],
        ).astype(BF16)
        share_out[pl.ds(tile * TILE, TILE), :] = share
        lifted_out[...] += tn_dot(share, block)


def front(me, image, from_right, from_left, weights, depth, bins):
    total = ROWS * COLS
    return pl.pallas_call(
        front_kernel,
        out_shape=(
            jax.ShapeDtypeStruct((total, C), BF16),
            jax.ShapeDtypeStruct((total, WIN * BR), BF16),
            jax.ShapeDtypeStruct((WIN * BR, C), F32),
            jax.ShapeDtypeStruct((total, LANES), F32),
            jax.ShapeDtypeStruct((total, LANES), F32),
            jax.ShapeDtypeStruct((COLS, LANES), jnp.int32),
        ),
        in_specs=[whole(pltpu.SMEM)] + [whole()] * 6,
        out_specs=(whole(),) * 6,
        scratch_shapes=[
            pltpu.VMEM((ROWS + 2, WIDE, C), BF16),
            pltpu.VMEM((ROWS + 2, WIDE, C), BF16),
            pltpu.VMEM((C, LANES), BF16),
            pltpu.VMEM((SLOTS * LANES, WIN * BR), BF16),
            pltpu.VMEM((SLOTS, COLS, LANES), BF16),
        ],
        compiler_params=pltpu.CompilerParams(vmem_limit_bytes=48 * 2**20),
        name="front",
    )(me, image, from_right, from_left, weights, depth, bins)


def along_cycles(part, down):
    if down == 0:
        return part
    cycle = iota(part.shape, 1)
    moved = pltpu.roll(part, down % BR, 1)
    keep = cycle >= 1 if down == 1 else cycle < BR - 1
    return jnp.where(keep, moved, 0.0)


def back_kernel(
    cam_window, lid_window, cot_window, weights, feat, share, probs, gain, slots, depth,
    merged_out, cam_out, lid_out,
    table, spread, wide_table, depth_pad,
):
    depth_pad[...] = jnp.zeros((C, LANES), BF16)
    depth_pad[:, 0:BINS] = depth[...]
    fill_spread(spread)
    merged_in = jnp.concatenate([cam_window[...].astype(BF16), lid_window[...]], axis=2)
    span = WIN - 2
    joined = jnp.concatenate(
        [merged_in[right : right + span].reshape(span * BR, C + CL) for right in range(3)],
        axis=1,
    )
    pre = None
    for down in range(3):
        kernel = jnp.concatenate([weights[3 * down + right] for right in range(3)], axis=0)
        part = along_cycles(dot(joined, kernel).reshape(span, BR, C), 1 - down)
        pre = part if pre is None else pre + part
    gate = 1.0 / (1.0 + jnp.exp(-pre))
    merged = (pre * gate).astype(BF16)
    grad_pre = (cot_window[...].astype(F32) * (gate * (1.0 + pre * (1.0 - gate)))).astype(BF16)
    inner = span - 2
    total = None
    for down in range(3):
        part = None
        for right in range(3):
            piece = nt_dot(
                grad_pre[2 - right : 2 - right + inner].reshape(inner * BR, C),
                weights[3 * down + right],
            )
            part = piece if part is None else part + piece
        part = along_cycles(part.reshape(inner, BR, C + CL), down - 1)
        total = part if total is None else total + part
    table[...] = jnp.zeros((WIN * BR, C), BF16)
    table[2 * BR : (WIN - 2) * BR, :] = total[:, :, 0:C].astype(BF16).reshape(inner * BR, C)
    order = iota((BR * BA, BR * BA), 0)
    source = iota((BR * BA, BR * BA), 1)
    swap = ((order % BA) * BR + order // BA == source).astype(F32).astype(BF16)
    own = merged[REACH - 1 : REACH - 1 + BA].reshape(BA * BR, C)
    merged_out[...] = dot(swap, own).astype(BF16)
    own_lid = total[REACH - 2 : REACH - 2 + BA, :, C:].astype(BF16).reshape(BA * BR, CL)
    lid_out[...] = dot(swap, own_lid).astype(BF16)
    wide_table[...] = dot(spread[...], table[...]).astype(BF16)

    @pl.loop(0, ROWS // TILE_H)
    def _(tile):
        rows = pl.ds(tile * TILE, TILE)
        block = feat[rows, :]
        slot_map = slots[...]
        picked = jnp.zeros((TILE_H, COLS, LANES), F32)
        for pair in range(SLOTS // 2):
            both = nt_dot(block, wide_table[pair * 2 * LANES : (pair + 1) * 2 * LANES, :])
            for side in range(2):
                value = both[:, side * LANES : (side + 1) * LANES].reshape(
                    TILE_H, COLS, LANES
                )
                picked = jnp.where((slot_map == 2 * pair + side)[None], value, picked)
        picked = picked.reshape(TILE, LANES)
        mean = jnp.sum(picked * probs[rows, :], axis=1, keepdims=True)
        grad_logits = ((picked - mean) * gain[rows, :]).astype(BF16)
        out = dot(share[rows, :], table[...]) + nt_dot(grad_logits, depth_pad[...])
        cam_out[pl.ds(tile * TILE_H, TILE_H)] = out.astype(BF16).reshape(TILE_H, COLS, C)


def back(cam_window, lid_window, cot_window, weights, feat, share, probs, gain, slots, depth):
    return pl.pallas_call(
        back_kernel,
        out_shape=(
            jax.ShapeDtypeStruct((BR * BA, C), BF16),
            jax.ShapeDtypeStruct((ROWS, COLS, C), BF16),
            jax.ShapeDtypeStruct((BR * BA, CL), BF16),
        ),
        in_specs=[whole()] * 10,
        out_specs=(whole(),) * 3,
        scratch_shapes=[
            pltpu.VMEM((WIN * BR, C), BF16),
            pltpu.VMEM((SLOTS * LANES, WIN * BR), BF16),
            pltpu.VMEM((SLOTS * LANES, C), BF16),
            pltpu.VMEM((C, LANES), BF16),
        ],
        compiler_params=pltpu.CompilerParams(vmem_limit_bytes=48 * 2**20),
        name="back",
    )(cam_window, lid_window, cot_window, weights, feat, share, probs, gain, slots, depth)


def shifted(block, distance):
    count = lax.axis_size(AXES)
    return lax.ppermute(block, AXES, [((i - distance) % count, i) for i in range(count)])


def local(
    image_feats, cam_weights, depth_weight, ray_bins, pillar_sums, pillar_counts,
    lidar_weight, merge_weight, out_cotangent,
):
    me = lax.axis_index(AXES).reshape(1).astype(jnp.int32)
    from_right = shifted(image_feats[:, 0:8], -1)
    from_left = shifted(image_feats[:, COLS - 8 :], 1)

    occupied = (pillar_counts > 0).astype(F32)
    divisor = jnp.maximum(pillar_counts, 1).astype(F32)
    pillar_feat = (pillar_sums.astype(F32) * (occupied / divisor)[:, :, None]).astype(BF16)
    grouped = pillar_feat.reshape(BR, 2, BA, 2, CL).transpose(2, 0, 1, 3, 4)
    lid_own = jax.nn.relu(
        dot(grouped.reshape(BA * BR, 4 * CL), lidar_weight.reshape(4 * CL, CL))
    ).astype(BF16).reshape(BA, BR, CL)
    cot_own = out_cotangent.transpose(1, 0, 2)
    side = jnp.concatenate([cot_own, lid_own], axis=2)
    side_right = shifted(side, -1)
    side_left = shifted(side, 1)

    feat, share, lifted, probs, gain, slots = front(
        me, image_feats, from_right, from_left, cam_weights, depth_weight, ray_bins
    )
    lifted = lifted.reshape(WIN, BR, C)
    low = lifted.astype(BF16)
    near_right = shifted(low[2:12], -1)
    near_left = shifted(low[4:14], 1)
    far_right = jnp.concatenate(
        [low[2:8].reshape(6, BR, C), ], axis=0
    ).at[4:6].add(near_right[0:2])
    far_left = low[8:14].at[0:2].add(near_left[8:10])
    far_right = shifted(far_right, -2)
    far_left = shifted(far_left, 2)
    side_far_right = shifted(side[0:2], -2)
    side_far_left = shifted(side[2:4], 2)
    window = lifted
    zero = lambda n: jnp.zeros((n, BR, C), F32)
    window = window + jnp.concatenate([zero(6), near_right.astype(F32)], 0)
    window = window + jnp.concatenate([near_left.astype(F32), zero(6)], 0)
    window = window + jnp.concatenate([far_left.astype(F32), zero(4), far_right.astype(F32)], 0)
    side_window = jnp.concatenate([side_far_left, side_left, side, side_right, side_far_right], 0)
    cot_window = side_window[1:15, :, 0:C]
    lid_window = side_window[:, :, C:]
    merged, cam_grad, lid_grad = back(
        window, lid_window, cot_window, merge_weight, feat, share, probs, gain, slots,
        depth_weight,
    )
    return (
        merged.reshape(BR, BA, C),
        cam_grad,
        lid_grad.reshape(BR, BA, CL),
    )


def solution(mesh):
    columns = P(None, AXES, None)
    placed = (
        columns, P(), P(), P(AXES, None), columns, P(None, AXES), P(), P(), columns,
    )
    return jax.shard_map(
        local, mesh=mesh, in_specs=placed, out_specs=(columns,) * 3, check_vma=False
    )
```

profile of v0, /device:TPU:1, one launch (start us, length us, event | category | flops | bytes accessed | tf_op | source)
XLA Modules:
  0.0 82.4 jit_solution(10823487937041691667)
XLA Ops:
  0.6 0.0 copy-start
  0.6 0.7 convert_divide_fusion
  1.4 0.1 copy.18
  1.5 0.8 copy.24
  2.2 0.9 %multiply_convert_fusion = bf16[32,8,128]{2,1,0:T(8,128)(2,1)S(1)} fusion(bf16[32,8,128]{2,1,0:T(8,128)(2,1)} %param.17, f32[32,8]{1,0:T(8,128)S(1)} %copy.18), kind=kLoop, calls=%fused_computation.3 | loop fusion | flops 98304 | bytes 132096 | tf_op jit(solution)/shard_map/convert_element_type | solution.py:280
  3.3 0.0 copy-done
  3.3 0.2 fusion
  3.4 4.2 %collective-permute-start.7 = (bf16[4,16,384]{2,1,0:T(8,128)(2,1)S(1)}, bf16[4,16,384]{2,1,0:T(8,128)(2,1)S(1)}, u32[]{:S(2)}, u32[]{:S(2)}) collective-permute-start(bf16[4,16,384]{2,1,0:T(8,128)(2,1)S(1)} %pad_maximum_fusion), channel_id=1, source_target_pairs={{255,0},{0,1},{1,2},{2,3},{3,4},{4,5},{5,6},{6,7},{7,8},{8,9},{9,1... | collective-permute-start | bytes 147464 | tf_op jit(solution)/shard_map/ppermute | solution.py:267
  7.6 0.0 collective-permute-start.8
  7.7 7.7 %collective-permute-start.9 = (bf16[2,16,384]{2,1,0:T(8,128)(2,1)S(1)}, bf16[2,16,384]{2,1,0:T(8,128)(2,1)S(1)}, u32[]{:S(2)}, u32[]{:S(2)}) collective-permute-start(bf16[2,16,384]{2,1,0:T(8,128)(2,1)S(1)} %get-tuple-element.53), channel_id=1, source_target_pairs={{2,0},{3,1},{4,2},{5,3},{6,4},{7,5},{8,6},{9,7},{10,8},{11,9},{12,... | collective-permute-start | bytes 73736 | tf_op jit(solution)/shard_map/ppermute | solution.py:267
  15.3 0.0 collective-permute-start.6
  15.3 1.0 %fusion.5 = (bf16[32,8,256]{2,1,0:T(8,128)(2,1)S(1)}, bf16[32,8,256]{2,1,0:T(8,128)(2,1)S(1)}) fusion(bf16[32,64,256]{2,1,0:T(8,128)(2,1)} %image.1), kind=kLoop, calls=%fused_computation.23 | loop fusion | bytes 524288 | tf_op jit(solution)/shard_map/slice | solution.py:276
  16.3 2.9 %collective-permute-start.1 = (bf16[32,8,256]{2,1,0:T(8,128)(2,1)S(1)}, bf16[32,8,256]{2,1,0:T(8,128)(2,1)S(1)}, u32[]{:S(2)}, u32[]{:S(2)}) collective-permute-start(bf16[32,8,256]{2,1,0:T(8,128)(2,1)S(1)} %get-tuple-element.45), channel_id=1, source_target_pairs={{255,0},{0,1},{1,2},{2,3},{3,4},{4,5},{5,6},{6,7},{7,8},{8,9},{9,1... | collective-permute-start | bytes 393224 | tf_op jit(solution)/shard_map/ppermute | solution.py:267
  19.3 0.9 %copy.16.depth = bf16[256,118]{1,0:T(8,128)(2,1)S(1)} copy(bf16[256,118]{0,1:T(8,128)(2,1)} %param.15) | data formatting | bytes 120832 | tf_op args[2]
  20.2 0.1 pad.13.clone
  20.3 3.1 %collective-permute-done.6 = bf16[2,16,384]{2,1,0:T(8,128)(2,1)S(1)} collective-permute-done((bf16[2,16,384]{2,1,0:T(8,128)(2,1)S(1)}, bf16[2,16,384]{2,1,0:T(8,128)(2,1)S(1)}, u32[]{:S(2)}, u32[]{:S(2)}) %collective-permute-start.6) | collective-permute-done | bytes 24608 | tf_op jit(solution)/shard_map/ppermute | solution.py:267
  23.4 4.6 %collective-permute-start = (bf16[32,8,256]{2,1,0:T(8,128)(2,1)S(1)}, bf16[32,8,256]{2,1,0:T(8,128)(2,1)S(1)}, u32[]{:S(2)}, u32[]{:S(2)}) collective-permute-start(bf16[32,8,256]{2,1,0:T(8,128)(2,1)S(1)} %get-tuple-element.46), channel_id=1, source_target_pairs={{1,0},{2,1},{3,2},{4,3},{5,4},{6,5},{7,6},{8,7},{9,8},{10,9},{11,1... | collective-permute-start | bytes 393224 | tf_op jit(solution)/shard_map/ppermute | solution.py:267
  28.0 0.0 collective-permute-done.7
  28.1 0.0 collective-permute-done.8
  28.1 0.0 collective-permute-done.1.from_left
  28.1 1.2 %collective-permute-done.from_right = bf16[32,8,256]{2,1,0:T(8,128)(2,1)S(1)} collective-permute-done((bf16[32,8,256]{2,1,0:T(8,128)(2,1)S(1)}, bf16[32,8,256]{2,1,0:T(8,128)(2,1)S(1)}, u32[]{:S(2)}, u32[]{:S(2)}) %collective-permute-start) | collective-permute-done | bytes 131104 | tf_op jit(solution)/shard_map/ppermute | solution.py:267
  29.3 0.0 copy-start.1
  29.3 1.2 %copy-done.1 = bf16[32,64,256]{2,1,0:T(8,128)(2,1)S(1)} copy-done((bf16[32,64,256]{2,1,0:T(8,128)(2,1)S(1)}, bf16[32,64,256]{2,1,0:T(8,128)(2,1)}, u32[]{:S(2)}) %copy-start.1) | copy-done | bytes 1048600
  30.6 0.0 copy-start.2
  30.6 0.8 copy-done.2
  31.3 20.7 %front.1 = (bf16[2048,256]{1,0:T(8,128)(2,1)S(1)}, bf16[2048,256]{1,0:T(8,128)(2,1)S(1)}, f32[256,256]{1,0:T(8,128)S(1)}, f32[2048,128]{1,0:T(8,128)S(1)}, f32[2...) custom-call(s32[1]{0:T(128)} %bitcast.me_ref, bf16[32,64,256]{2,1,0:T(8,128)(2,1)S(1)} %copy-done.1, ...), custom_call_target="tpu_custom_call" | custom-call | tf_op jit(solution)/shard_map/front/pallas_call | solution.py:146
  52.1 0.1 collective-permute-start.3
  52.2 1.6 %collective-permute-start.2 = (bf16[10,16,256]{2,1,0:T(8,128)(2,1)S(1)}, bf16[10,16,256]{2,1,0:T(8,128)(2,1)S(1)}, u32[]{:S(2)}, u32[]{:S(2)}) collective-permute-start(bf16[10,16,256]{2,1,0:T(8,128)(2,1)S(1)} %get-tuple-element.50), channel_id=1, source_target_pairs={{1,0},{2,1},{3,2},{4,3},{5,4},{6,5},{7,6},{8,7},{9,8},{10,9},{11,1... | collective-permute-start | bytes 245768 | tf_op jit(solution)/shard_map/ppermute | solution.py:267
  53.8 0.7 collective-permute-done.3
  54.5 4.0 %collective-permute-done.2 = bf16[10,16,256]{2,1,0:T(8,128)(2,1)S(1)} collective-permute-done((bf16[10,16,256]{2,1,0:T(8,128)(2,1)S(1)}, bf16[10,16,256]{2,1,0:T(8,128)(2,1)S(1)}, u32[]{:S(2)}, u32[]{:S(2)}) %collective-permute-start.2) | collective-permute-done | bytes 81952 | tf_op jit(solution)/shard_map/ppermute | solution.py:267
  58.5 0.1 collective-permute-start.4
  58.6 11.3 %collective-permute-start.5 = (bf16[6,16,256]{2,1,0:T(8,128)(2,1)S(1)}, bf16[6,16,256]{2,1,0:T(8,128)(2,1)S(1)}, u32[]{:S(2)}, u32[]{:S(2)}) collective-permute-start(bf16[6,16,256]{2,1,0:T(8,128)(2,1)S(1)} %get-tuple-element.48), channel_id=1, source_target_pairs={{2,0},{3,1},{4,2},{5,3},{6,4},{7,5},{8,6},{9,7},{10,8},{11,9},{12,... | collective-permute-start | bytes 147464 | tf_op jit(solution)/shard_map/ppermute | solution.py:267
  70.0 0.0 collective-permute-done.9
  70.0 1.3 %collective-permute-done.4 = bf16[6,16,256]{2,1,0:T(8,128)(2,1)S(1)} collective-permute-done((bf16[6,16,256]{2,1,0:T(8,128)(2,1)S(1)}, bf16[6,16,256]{2,1,0:T(8,128)(2,1)S(1)}, u32[]{:S(2)}, u32[]{:S(2)}) %collective-permute-start.4) | collective-permute-done | bytes 49184 | tf_op jit(solution)/shard_map/ppermute | solution.py:267
  71.4 0.0 collective-permute-done.5
  71.4 0.1 maximum_add_fusion.cam_window
  71.5 10.3 %back.1 = (bf16[64,256]{1,0:T(8,128)(2,1)S(1)}, bf16[32,64,256]{2,1,0:T(8,128)(2,1)}, bf16[64,128]{1,0:T(8,128)(2,1)}) custom-call(f32[16,16,256]{2,1,0:T(8,128)S(1)} %maximum_add_fusion.cam_window, bf16[16,16,128]{2,1,0:T(8,128)(2,1)S(1)} %slice.112.lid_window, bf16[14,16,256]{2,1,0:T(8,128)(2,1)S(1)} %slice.113.cot_window, bf16[9,384,256]{2,1,0:T(8,128)(2,1)} %weights.3, ...), custom_call_target="tpu_custom_call" | custom-call | tf_op jit(solution)/shard_map/back/pallas_call | solution.py:245
  81.8 0.6 reshape.97
  (18 shorter events, 0.2 us)
Async XLA Ops:
  0.6 2.6 %copy-start = (bf16[4,128,128]{2,1,0:T(8,128)(2,1)S(1)}, bf16[4,128,128]{2,1,0:T(8,128)(2,1)}, u32[]{:S(2)}) copy-start(bf16[4,128,128]{2,1,0:T(8,128)(2,1)} %param.19) | copy-start | bytes 393220
  3.4 24.6 %collective-permute-start.7 = (bf16[4,16,384]{2,1,0:T(8,128)(2,1)S(1)}, bf16[4,16,384]{2,1,0:T(8,128)(2,1)S(1)}, u32[]{:S(2)}, u32[]{:S(2)}) collective-permute-start(bf16[4,16,384]{2,1,0:T(8,128)(2,1)S(1)} %pad_maximum_fusion), channel_id=1, source_target_pairs={{255,0},{0,1},{1,2},{2,3},{3,4},{4,5},{5,6},{6,7},{7,8},{8,9},{9,1... | collective-permute-start | bytes 147464 | tf_op jit(solution)/shard_map/ppermute | solution.py:267
  7.6 20.4 %collective-permute-start.8 = (bf16[4,16,384]{2,1,0:T(8,128)(2,1)S(1)}, bf16[4,16,384]{2,1,0:T(8,128)(2,1)S(1)}, u32[]{:S(2)}, u32[]{:S(2)}) collective-permute-start(bf16[4,16,384]{2,1,0:T(8,128)(2,1)S(1)} %pad_maximum_fusion), channel_id=1, source_target_pairs={{1,0},{2,1},{3,2},{4,3},{5,4},{6,5},{7,6},{8,7},{9,8},{10,9},{11,1... | collective-permute-start | bytes 147464 | tf_op jit(solution)/shard_map/ppermute | solution.py:267
  7.7 62.3 %collective-permute-start.9 = (bf16[2,16,384]{2,1,0:T(8,128)(2,1)S(1)}, bf16[2,16,384]{2,1,0:T(8,128)(2,1)S(1)}, u32[]{:S(2)}, u32[]{:S(2)}) collective-permute-start(bf16[2,16,384]{2,1,0:T(8,128)(2,1)S(1)} %get-tuple-element.53), channel_id=1, source_target_pairs={{2,0},{3,1},{4,2},{5,3},{6,4},{7,5},{8,6},{9,7},{10,8},{11,9},{12,... | collective-permute-start | bytes 73736 | tf_op jit(solution)/shard_map/ppermute | solution.py:267
  15.3 8.1 %collective-permute-start.6 = (bf16[2,16,384]{2,1,0:T(8,128)(2,1)S(1)}, bf16[2,16,384]{2,1,0:T(8,128)(2,1)S(1)}, u32[]{:S(2)}, u32[]{:S(2)}) collective-permute-start(bf16[2,16,384]{2,1,0:T(8,128)(2,1)S(1)} %get-tuple-element.54), channel_id=1, source_target_pairs={{254,0},{255,1},{0,2},{1,3},{2,4},{3,5},{4,6},{5,7},{6,8},{7,9},{8... | collective-permute-start | bytes 73736 | tf_op jit(solution)/shard_map/ppermute | solution.py:267
  16.3 11.8 %collective-permute-start.1 = (bf16[32,8,256]{2,1,0:T(8,128)(2,1)S(1)}, bf16[32,8,256]{2,1,0:T(8,128)(2,1)S(1)}, u32[]{:S(2)}, u32[]{:S(2)}) collective-permute-start(bf16[32,8,256]{2,1,0:T(8,128)(2,1)S(1)} %get-tuple-element.45), channel_id=1, source_target_pairs={{255,0},{0,1},{1,2},{2,3},{3,4},{4,5},{5,6},{6,7},{7,8},{8,9},{9,1... | collective-permute-start | bytes 393224 | tf_op jit(solution)/shard_map/ppermute | solution.py:267
  23.4 5.9 %collective-permute-start = (bf16[32,8,256]{2,1,0:T(8,128)(2,1)S(1)}, bf16[32,8,256]{2,1,0:T(8,128)(2,1)S(1)}, u32[]{:S(2)}, u32[]{:S(2)}) collective-permute-start(bf16[32,8,256]{2,1,0:T(8,128)(2,1)S(1)} %get-tuple-element.46), channel_id=1, source_target_pairs={{1,0},{2,1},{3,2},{4,3},{5,4},{6,5},{7,6},{8,7},{9,8},{10,9},{11,1... | collective-permute-start | bytes 393224 | tf_op jit(solution)/shard_map/ppermute | solution.py:267
  29.3 1.2 %copy-start.1 = (bf16[32,64,256]{2,1,0:T(8,128)(2,1)S(1)}, bf16[32,64,256]{2,1,0:T(8,128)(2,1)}, u32[]{:S(2)}) copy-start(bf16[32,64,256]{2,1,0:T(8,128)(2,1)} %image.1) | copy-start | bytes 3145732
  30.6 0.8 copy-start.2
  52.1 2.4 %collective-permute-start.3 = (bf16[10,16,256]{2,1,0:T(8,128)(2,1)S(1)}, bf16[10,16,256]{2,1,0:T(8,128)(2,1)S(1)}, u32[]{:S(2)}, u32[]{:S(2)}) collective-permute-start(bf16[10,16,256]{2,1,0:T(8,128)(2,1)S(1)} %get-tuple-element.49), channel_id=1, source_target_pairs={{255,0},{0,1},{1,2},{2,3},{3,4},{4,5},{5,6},{6,7},{7,8},{8,9},{9,1... | collective-permute-start | bytes 245768 | tf_op jit(solution)/shard_map/ppermute | solution.py:267
  52.2 6.3 %collective-permute-start.2 = (bf16[10,16,256]{2,1,0:T(8,128)(2,1)S(1)}, bf16[10,16,256]{2,1,0:T(8,128)(2,1)S(1)}, u32[]{:S(2)}, u32[]{:S(2)}) collective-permute-start(bf16[10,16,256]{2,1,0:T(8,128)(2,1)S(1)} %get-tuple-element.50), channel_id=1, source_target_pairs={{1,0},{2,1},{3,2},{4,3},{5,4},{6,5},{7,6},{8,7},{9,8},{10,9},{11,1... | collective-permute-start | bytes 245768 | tf_op jit(solution)/shard_map/ppermute | solution.py:267
  58.5 12.8 %collective-permute-start.4 = (bf16[6,16,256]{2,1,0:T(8,128)(2,1)S(1)}, bf16[6,16,256]{2,1,0:T(8,128)(2,1)S(1)}, u32[]{:S(2)}, u32[]{:S(2)}) collective-permute-start(bf16[6,16,256]{2,1,0:T(8,128)(2,1)S(1)} %get-tuple-element.47), channel_id=1, source_target_pairs={{254,0},{255,1},{0,2},{1,3},{2,4},{3,5},{4,6},{5,7},{6,8},{7,9},{8... | collective-permute-start | bytes 147464 | tf_op jit(solution)/shard_map/ppermute | solution.py:267
  58.6 12.8 %collective-permute-start.5 = (bf16[6,16,256]{2,1,0:T(8,128)(2,1)S(1)}, bf16[6,16,256]{2,1,0:T(8,128)(2,1)S(1)}, u32[]{:S(2)}, u32[]{:S(2)}) collective-permute-start(bf16[6,16,256]{2,1,0:T(8,128)(2,1)S(1)} %get-tuple-element.48), channel_id=1, source_target_pairs={{2,0},{3,1},{4,2},{5,3},{6,4},{7,5},{8,6},{9,7},{10,8},{11,9},{12,... | collective-permute-start | bytes 147464 | tf_op jit(solution)/shard_map/ppermute | solution.py:267
where the time goes:
time: 82.9 us; the launch traced here: 82.4 us
  starting transfers between devices  32.5 us (39%)
  Pallas kernels  31 us (37%)
  waiting for transfers between devices  10.4 us (13%)
  local copies, waits for them, and re-layouts  5.64 us (7%)
  other arithmetic  1.83 us (2%)
    ppermute x10, starting transfers between devices, shifted(): lax.ppermute(block, AXES, [((i - distance) % count, i) for i in range(cou...  32.5 us
    pallas_call x1, Pallas kernels, front(): pl.pallas_call(front_kernel, out_shape=(jax.ShapeDtypeStruct((total, C),...  20.7 us
    ppermute x10, waiting for transfers between devices, shifted(): lax.ppermute(block, AXES, [((i - distance) % count, i) for i in range(cou...  10.4 us
    pallas_call x1, Pallas kernels, back(): pl.pallas_call(back_kernel, out_shape=(jax.ShapeDtypeStruct((BR * BA, C),...  10.3 us
    unnamed x11, local copies, waits for them, and re-layouts  3.73 us
  transfers between devices with their start and end apart: 10, of which 5 were waited for; matrix products, arithmetic and copies ran while one was open for 3% of the time, Pallas kernels for 25%

commit v1 on v0

v1 whole, which is shorter than its diff:
```python
import jax
import jax.numpy as jnp
from jax import lax
from jax.experimental import pallas as pl
from jax.experimental.pallas import tpu as pltpu
from jax.sharding import PartitionSpec as P

AXES = ("branch", "strip")
ROWS = 32
COLS = 64
WIDE = 80
C = 256
CL = 128
BINS = 118
LANES = 128
LAYERS = 3
BR = 16
BA = 4
WIN = 16
REACH = 6
SLOTS = 12
BLOCK = 8
TILE_H = 4
TILE = TILE_H * COLS
FUSE = 2
SPREAD = 2
F32 = jnp.float32
BF16 = jnp.bfloat16


def whole(memory_space=pltpu.VMEM):
    return pl.BlockSpec(memory_space=memory_space)


def iota(shape, dim):
    return lax.broadcasted_iota(jnp.int32, shape, dim)


def nt_dot(lhs, rhs):
    return lax.dot_general(lhs, rhs, (((1,), (1,)), ((), ())), preferred_element_type=F32)


def tn_dot(lhs, rhs):
    return lax.dot_general(lhs, rhs, (((0,), (0,)), ((), ())), preferred_element_type=F32)


def dot(lhs, rhs):
    return jnp.dot(lhs, rhs, preferred_element_type=F32)


def fill_spread(spread):
    bin_index = iota((LANES, WIN * BR), 0)
    column = iota((LANES, WIN * BR), 1)
    for slot in range(SLOTS):
        offset = (column - (slot + 2) * BR) * BINS
        hit = (offset <= bin_index * BR) & (bin_index * BR < offset + BINS)
        spread[slot * LANES : (slot + 1) * LANES, :] = hit.astype(F32).astype(BF16)


def fill_side(side, pillars, counts, lidar, cotangent, flat):
    for cycle in range(BR):
        flat[BA * cycle : BA * (cycle + 1), :] = cotangent[cycle].astype(F32)
    order = iota((BA * BR, BR * BA), 0)
    source = iota((BA * BR, BR * BA), 1)
    swap = ((order % BR) * BA + order // BR == source).astype(F32).astype(BF16)
    side[0:BA] = dot(swap, flat[...].astype(BF16)).astype(BF16).reshape(BA, BR, C)
    cells = 4 * BR * BA
    row = iota((cells, 2 * BR), 0)
    pick = (row // (2 * BA) == iota((cells, 2 * BR), 1)).astype(F32).astype(BF16)
    spread = nt_dot(pick, counts[...].astype(F32).astype(BF16))
    here = iota((cells, 2 * BA), 0) % (2 * BA) == iota((cells, 2 * BA), 1)
    count = jnp.sum(jnp.where(here, spread, 0.0), axis=1, keepdims=True)
    scale = jnp.where(count > 0.0, 1.0, 0.0) / jnp.maximum(count, 1.0)
    feats = (pillars[...].astype(F32).reshape(cells, CL) * scale).astype(BF16)
    goal = iota((BA * BR, cells), 0)
    origin = iota((BA * BR, cells), 1)
    base = (goal % BR) * (4 * BA) + (goal // BR) * 2
    total = None
    for offset in range(4):
        step = (offset // 2) * 2 * BA + offset % 2
        chosen = dot((base + step == origin).astype(F32).astype(BF16), feats).astype(BF16)
        part = dot(chosen, lidar[offset])
        total = part if total is None else total + part
    lid = jnp.maximum(total, 0.0).astype(BF16)
    for pair in range(2):
        top = pair * 2 * BR
        side[BA + pair] = jnp.concatenate(
            [lid[top : top + BR], lid[top + BR : top + 2 * BR]], axis=1
        )


def front_kernel(
    me_ref, image, from_right, from_left, weights, depth, bins,
    pillars, counts, lidar, cotangent,
    feat_out, share_out, lifted_out, note_out, far_out, probs_out, gain_out, slot_out,
    first, second, held, depth_pad, spread, masks, flat, sems,
):
    image_copy = pltpu.make_async_copy(
        image, first.at[pl.ds(1, ROWS), pl.ds(0, COLS)], sems.at[LAYERS]
    )
    image_copy.start()
    weight_copies = [
        pltpu.make_async_copy(weights.at[index], held.at[index], sems.at[index])
        for index in range(LAYERS)
    ]
    for copy in weight_copies:
        copy.start()
    first[0] = jnp.zeros((WIDE, C), BF16)
    first[ROWS + 1] = jnp.zeros((WIDE, C), BF16)
    second[0] = jnp.zeros((WIDE, C), BF16)
    second[ROWS + 1] = jnp.zeros((WIDE, C), BF16)
    first[1 : ROWS + 1, COLS:WIDE, :] = jnp.concatenate(
        [from_right[...], from_left[...]], axis=1
    )
    depth_pad[BINS - 6 :, :] = jnp.zeros((LANES - BINS + 6, C), BF16)
    depth_pad[0:BINS, :] = depth[...]
    fill_spread(spread)
    fill_side(note_out.at[pl.ds(WIN, 6)], pillars, counts, lidar, cotangent, flat)
    cells = bins[...]
    sector = cells // (BR * BA)
    step = sector - me_ref[0] + 1
    step = jnp.where(step < 0, step + 256, step)
    step = jnp.where(step > 255, step - 256, step)
    slot = step * BA + cells % BA
    slot_out[...] = jnp.full((COLS, LANES), -1, jnp.int32)
    slot_out[:, 0:BINS] = slot
    slot_map = slot_out[...]
    for index in range(SLOTS):
        masks[index] = (slot_map == index).astype(F32).astype(BF16)

    def convolved(source, index, top, narrow):
        lhs = jnp.concatenate(
            [
                source[pl.ds(top + down, BLOCK)].reshape(BLOCK * WIDE, C)
                for down in range(3)
            ],
            axis=1,
        )
        out = None
        for right in (1, 0, 2):
            kernel = jnp.concatenate(
                [held[index, 3 * down + right] for down in range(3)], axis=0
            )
            if narrow and right == 1:
                part = dot(
                    lhs.reshape(BLOCK, WIDE, 3 * C)[:, 0:COLS].reshape(BLOCK * COLS, 3 * C),
                    kernel,
                ).reshape(BLOCK, COLS, C)
            else:
                part = dot(lhs, kernel).reshape(BLOCK, WIDE, C)
                if right != 1:
                    part = pltpu.roll(part, (1 - right) % WIDE, 1)
                if narrow:
                    part = part[:, 0:COLS]
            out = part if out is None else out + part
        return jnp.maximum(out, 0.0).astype(BF16)

    def layer(source, target, index):
        weight_copies[index].wait()

        @pl.loop(0, ROWS // BLOCK, unroll=True)
        def _(block):
            target[pl.ds(block * BLOCK + 1, BLOCK)] = convolved(
                source, index, block * BLOCK, False
            )

    image_copy.wait()
    layer(first, second, 0)
    layer(second, first, 1)
    weight_copies[2].wait()

    lifted_out[...] = jnp.zeros((WIN * BR, C), F32)
    lane_ok = iota((TILE, LANES), 1) < BINS

    def lift(block, tile):
        rows = pl.ds(pl.multiple_of(tile * TILE, TILE), TILE)
        feat_out[rows, :] = block
        logits = nt_dot(block, depth_pad[...])
        decay = jnp.exp(-jnp.abs(logits))
        tail = jnp.log(1.0 + decay)
        soft = jnp.maximum(logits, 0.0) + tail + 0.05
        soft = jnp.where(lane_ok, soft, 0.0)
        scale = 1.0 / jnp.sum(soft, axis=1, keepdims=True)
        probs = soft * scale
        gate = jnp.exp(jnp.minimum(logits, 0.0) - tail)
        probs_out[rows, :] = probs
        gain_out[rows, :] = gate * scale
        low = probs.astype(BF16).reshape(TILE_H, COLS, LANES)
        share = dot(
            jnp.concatenate(
                [
                    (low * masks[index][None]).reshape(TILE, LANES)
                    for index in range(SLOTS)
                ],
                axis=1,
            ),
            spread[...],
        ).astype(BF16)
        share_out[rows, :] = share
        lifted_out[...] += tn_dot(share, block)

    @pl.loop(0, ROWS // BLOCK, unroll=FUSE)
    def _(block):
        made = convolved(first, 2, block * BLOCK, True)
        for part in range(BLOCK // TILE_H):
            lift(
                made[part * TILE_H : (part + 1) * TILE_H].reshape(TILE, C),
                block * (BLOCK // TILE_H) + part,
            )

    note_out[0:WIN] = lifted_out[...].astype(BF16).reshape(WIN, BR, C)
    odd = lax.rem(me_ref[0], 2)

    @pl.when(odd == 1)
    def _():
        far_out[...] = note_out[12:14]

    @pl.when(odd == 0)
    def _():
        far_out[...] = note_out[2:4]


def front(me, image, from_right, from_left, weights, depth, bins, pillars, counts, lidar, cotangent):
    total = ROWS * COLS
    return pl.pallas_call(
        front_kernel,
        out_shape=(
            jax.ShapeDtypeStruct((total, C), BF16),
            jax.ShapeDtypeStruct((total, WIN * BR), BF16),
            jax.ShapeDtypeStruct((WIN * BR, C), F32),
            jax.ShapeDtypeStruct((WIN + 6, BR, C), BF16),
            jax.ShapeDtypeStruct((2, BR, C), BF16),
            jax.ShapeDtypeStruct((total, LANES), F32),
            jax.ShapeDtypeStruct((total, LANES), F32),
            jax.ShapeDtypeStruct((COLS, LANES), jnp.int32),
        ),
        in_specs=[
            whole(pltpu.SMEM), whole(pl.ANY), whole(), whole(), whole(pl.ANY),
            whole(), whole(), whole(), whole(), whole(), whole(),
        ],
        out_specs=(whole(),) * 8,
        scratch_shapes=[
            pltpu.VMEM((ROWS + 2, WIDE, C), BF16),
            pltpu.VMEM((ROWS + 2, WIDE, C), BF16),
            pltpu.VMEM((LAYERS, 9, C, C), BF16),
            pltpu.VMEM((LANES, C), BF16),
            pltpu.VMEM((SLOTS * LANES, WIN * BR), BF16),
            pltpu.VMEM((SLOTS, COLS, LANES), BF16),
            pltpu.VMEM((BR * BA, C), F32),
            pltpu.SemaphoreType.DMA((LAYERS + 1,)),
        ],
        compiler_params=pltpu.CompilerParams(vmem_limit_bytes=48 * 2**20),
        name="front",
    )(me, image, from_right, from_left, weights, depth, bins, pillars, counts, lidar, cotangent)


def along_cycles(part, down):
    if down == 0:
        return part
    cycle = iota(part.shape, 1)
    moved = pltpu.roll(part, down % BR, 1)
    keep = cycle >= 1 if down == 1 else cycle < BR - 1
    return jnp.where(keep, moved, 0.0)


def back_kernel(
    me_ref, lifted, note, partner, crossed, relayed, far, weights, feat, share, probs, gain,
    slots, depth,
    merged_out, cam_out, lid_out,
    cam, cot, lid, table, spread, wide_table, depth_pad,
):
    depth_pad[BINS - 6 :, :] = jnp.zeros((LANES - BINS + 6, C), BF16)
    depth_pad[0:BINS, :] = depth[...]
    fill_spread(spread)

    def put_lid(at, packed):
        lid[at] = packed[:, 0:CL]
        lid[at + 1] = packed[:, CL:]

    cam[...] = lifted[...].reshape(WIN, BR, C)
    cot[REACH : REACH + BA] = note[WIN : WIN + BA]
    put_lid(REACH, note[WIN + BA])
    put_lid(REACH + 2, note[WIN + BA + 1])
    cot[0] = jnp.zeros((BR, C), BF16)
    cot[WIN - 1] = jnp.zeros((BR, C), BF16)
    odd = lax.rem(me_ref[0], 2)

    def gather(low_side):
        near = 10 if low_side else 2
        other = 2 if low_side else 10
        cam[6:16] += (partner[2:12] if low_side else crossed[0:10]).astype(F32)
        cam[0:10] += (crossed[0:10] if low_side else partner[4:14]).astype(F32)
        start = 10 if low_side else 0
        cam[start : start + 6] += relayed[0:6].astype(F32)
        edge = 0 if low_side else 14
        cam[edge : edge + 2] += far[...].astype(F32)
        cot[near : near + 4] = partner[WIN : WIN + 4]
        cot[other : other + 4] = crossed[10:14]
        cot[1 if low_side else 14] = crossed[14]
        cot[14 if low_side else 1] = relayed[6]
        put_lid(near, partner[WIN + 4])
        put_lid(near + 2, partner[WIN + 5])
        put_lid(other, crossed[15])
        put_lid(other + 2, crossed[16])
        put_lid(0 if low_side else 14, crossed[17])
        put_lid(14 if low_side else 0, relayed[7])

    @pl.when(odd == 0)
    def _():
        gather(True)

    @pl.when(odd == 1)
    def _():
        gather(False)

    span = WIN - 2
    merged_in = jnp.concatenate([cam[...].astype(BF16), lid[...]], axis=2)
    joined = jnp.concatenate(
        [merged_in[right : right + span].reshape(span * BR, C + CL) for right in range(3)],
        axis=1,
    )
    pre = None
    for down in range(3):
        kernel = jnp.concatenate([weights[3 * down + right] for right in range(3)], axis=0)
        part = along_cycles(dot(joined, kernel).reshape(span, BR, C), 1 - down)
        pre = part if pre is None else pre + part
    gate = 1.0 / (1.0 + jnp.exp(-pre))
    merged = (pre * gate).astype(BF16)
    grad_pre = (
        cot[1 : WIN - 1].astype(F32) * (gate * (1.0 + pre * (1.0 - gate)))
    ).astype(BF16)
    inner = span - 2
    total = None
    for down in range(3):
        part = None
        for right in range(3):
            piece = nt_dot(
                grad_pre[2 - right : 2 - right + inner].reshape(inner * BR, C),
                weights[3 * down + right],
            )
            part = piece if part is None else part + piece
        part = along_cycles(part.reshape(inner, BR, C + CL), down - 1)
        total = part if total is None else total + part
    table[0 : 2 * BR, :] = jnp.zeros((2 * BR, C), BF16)
    table[(WIN - 2) * BR :, :] = jnp.zeros((2 * BR, C), BF16)
    table[2 * BR : (WIN - 2) * BR, :] = total[:, :, 0:C].astype(BF16).reshape(inner * BR, C)
    order = iota((BR * BA, BR * BA), 0)
    source = iota((BR * BA, BR * BA), 1)
    swap = ((order % BA) * BR + order // BA == source).astype(F32).astype(BF16)
    own = merged[REACH - 1 : REACH - 1 + BA].reshape(BA * BR, C)
    turned = dot(swap, own)
    for cycle in range(BR):
        merged_out[cycle] = turned[BA * cycle : BA * (cycle + 1)].astype(BF16)
    own_lid = total[REACH - 2 : REACH - 2 + BA, :, C:].astype(BF16).reshape(BA * BR, CL)
    lid_out[...] = dot(swap, own_lid).astype(BF16)
    wide_table[...] = dot(spread[...], table[...]).astype(BF16)

    @pl.loop(0, ROWS // TILE_H, unroll=SPREAD)
    def _(tile):
        rows = pl.ds(pl.multiple_of(tile * TILE, TILE), TILE)
        block = feat[rows, :]
        slot_map = slots[...]
        picked = jnp.zeros((TILE_H, COLS, LANES), F32)
        for pair in range(SLOTS // 2):
            both = nt_dot(block, wide_table[pair * 2 * LANES : (pair + 1) * 2 * LANES, :])
            for side in range(2):
                value = both[:, side * LANES : (side + 1) * LANES].reshape(
                    TILE_H, COLS, LANES
                )
                picked = jnp.where((slot_map == 2 * pair + side)[None], value, picked)
        picked = picked.reshape(TILE, LANES)
        mean = jnp.sum(picked * probs[rows, :], axis=1, keepdims=True)
        grad_logits = ((picked - mean) * gain[rows, :]).astype(BF16)
        out = dot(share[rows, :], table[...]) + dot(grad_logits, depth_pad[...])
        cam_out[pl.ds(tile * TILE_H, TILE_H)] = out.astype(BF16).reshape(TILE_H, COLS, C)


def back(*operands):
    return pl.pallas_call(
        back_kernel,
        out_shape=(
            jax.ShapeDtypeStruct((BR, BA, C), BF16),
            jax.ShapeDtypeStruct((ROWS, COLS, C), BF16),
            jax.ShapeDtypeStruct((BR * BA, CL), BF16),
        ),
        in_specs=[whole(pltpu.SMEM)] + [whole()] * 13,
        out_specs=(whole(),) * 3,
        scratch_shapes=[
            pltpu.VMEM((WIN, BR, C), F32),
            pltpu.VMEM((WIN, BR, C), BF16),
            pltpu.VMEM((WIN, BR, CL), BF16),
            pltpu.VMEM((WIN * BR, C), BF16),
            pltpu.VMEM((SLOTS * LANES, WIN * BR), BF16),
            pltpu.VMEM((SLOTS * LANES, C), BF16),
            pltpu.VMEM((LANES, C), BF16),
        ],
        compiler_params=pltpu.CompilerParams(vmem_limit_bytes=48 * 2**20),
        name="back",
    )(*operands)


def shifted(block, distance):
    count = lax.axis_size(AXES)
    return lax.ppermute(block, AXES, [((i - distance) % count, i) for i in range(count)])


def swapped(block, odd_step):
    count = lax.axis_size(AXES)
    route = [(i, (i + odd_step if i % 2 else i - odd_step) % count) for i in range(count)]
    return lax.ppermute(block, AXES, route)


def local(
    image_feats, cam_weights, depth_weight, ray_bins, pillar_sums, pillar_counts,
    lidar_weight, merge_weight, out_cotangent,
):
    me = lax.axis_index(AXES).astype(jnp.int32)
    odd = me % 2 == 1
    me = me.reshape(1)
    from_right = shifted(image_feats[:, 0:8], -1)
    from_left = shifted(image_feats[:, COLS - 8 :], 1)
    depth = depth_weight.T
    feat, share, lifted, note, far, probs, gain, slots = front(
        me, image_feats, from_right, from_left, cam_weights, depth, ray_bins,
        pillar_sums, pillar_counts.T, lidar_weight, out_cotangent,
    )
    partner = swapped(note, -1)
    far_got = swapped(far, 3)
    wide = lambda a: a.astype(F32)
    four = jnp.zeros((4, BR, C), F32)
    mine = lifted.reshape(WIN, BR, C)
    rise = mine[2:12] + jnp.concatenate([four, wide(partner[2:8])], 0)
    fall = mine[4:14] + jnp.concatenate([wide(partner[8:14]), four], 0)
    crossing = jnp.concatenate(
        [
            jnp.where(odd, fall, rise).astype(BF16),
            note[16:20],
            jnp.where(odd, partner[19:20], partner[16:17]),
            note[20:22],
            jnp.where(odd, partner[21:22], partner[20:21]),
        ],
        axis=0,
    )
    crossed = swapped(crossing, 1)
    relay = jnp.concatenate(
        [
            jnp.where(odd, crossed[0:6], crossed[4:10]),
            jnp.where(odd, crossed[10:11], crossed[13:14]),
            jnp.where(odd, crossed[15:16], crossed[16:17]),
        ],
        axis=0,
    )
    relayed = swapped(relay, -1)
    merged, cam_grad, lid_grad = back(
        me, lifted, note, partner, crossed, relayed, far_got, merge_weight, feat, share,
        probs, gain, slots, depth,
    )
    return merged, cam_grad, lid_grad.reshape(BR, BA, CL)


def solution(mesh):
    columns = P(None, AXES, None)
    placed = (
        columns, P(), P(), P(AXES, None), columns, P(None, AXES), P(), P(), columns,
    )
    return jax.shard_map(
        local, mesh=mesh, in_specs=placed, out_specs=(columns,) * 3, check_vma=False
    )
```

time: 82.9 us -> 67 us (0.81)
  the two profiles are of different devices: /device:TPU:1 before, /device:TPU:4 now
where the time goes in v1:
time: 67 us; the launch traced here: 66.6 us
  Pallas kernels  28.3 us (42%)
  starting transfers between devices  22.4 us (33%)
  waiting for transfers between devices  9.36 us (14%)
  local copies, waits for them, and re-layouts  5.8 us (9%)
  between operations  0.72 us (1%)
    ppermute x4, starting transfers between devices, swapped(): return lax.ppermute(block, AXES, route)  19 us
    pallas_call x1, Pallas kernels, front(): pl.pallas_call(front_kernel, out_shape=(jax.ShapeDtypeStruct((total, C),...  19 us
    pallas_call x1, Pallas kernels, back(): pl.pallas_call(back_kernel, out_shape=(jax.ShapeDtypeStruct((BR, BA, C),...  9.26 us
    ppermute x4, waiting for transfers between devices, swapped(): return lax.ppermute(block, AXES, route)  6.71 us
    unnamed x14, local copies, waits for them, and re-layouts  4.78 us
    ppermute x2, starting transfers between devices, shifted(): lax.ppermute(block, AXES, [((i - distance) % count, i) for i in range(cou...  3.32 us
    ppermute x2, waiting for transfers between devices, shifted(): lax.ppermute(block, AXES, [((i - distance) % count, i) for i in range(cou...  2.65 us
  transfers between devices with their start and end apart: 6, of which 4 were waited for; matrix products, arithmetic and copies ran while one was open for 0% of the time, Pallas kernels for 0%

profile of v1, /device:TPU:4, one launch (start us, length us, event | category | flops | bytes accessed | tf_op | source)
XLA Modules:
  0.0 66.6 jit_solution(17195842941712257048)
XLA Ops:
  0.6 1.0 %fusion.1 = (bf16[32,8,256]{2,1,0:T(8,128)(2,1)S(1)}, bf16[32,8,256]{2,1,0:T(8,128)(2,1)S(1)}) fusion(bf16[32,64,256]{2,1,0:T(8,128)(2,1)} %image.1), kind=kLoop, calls=%fused_computation.12 | loop fusion | bytes 524288 | tf_op jit(solution)/shard_map/slice | solution.py:421
  1.6 0.1 collective-permute-start.1
  1.7 3.2 %collective-permute-start = (bf16[32,8,256]{2,1,0:T(8,128)(2,1)S(1)}, bf16[32,8,256]{2,1,0:T(8,128)(2,1)S(1)}, u32[]{:S(2)}, u32[]{:S(2)}) collective-permute-start(bf16[32,8,256]{2,1,0:T(8,128)(2,1)S(1)} %get-tuple-element.26), channel_id=1, source_target_pairs={{1,0},{2,1},{3,2},{4,3},{5,4},{6,5},{7,6},{8,7},{9,8},{10,9},{11,1... | collective-permute-start | bytes 393224 | tf_op jit(solution)/shard_map/ppermute | solution.py:404
  5.0 2.6 %collective-permute-done.1.from_left = bf16[32,8,256]{2,1,0:T(8,128)(2,1)S(1)} collective-permute-done((bf16[32,8,256]{2,1,0:T(8,128)(2,1)S(1)}, bf16[32,8,256]{2,1,0:T(8,128)(2,1)S(1)}, u32[]{:S(2)}, u32[]{:S(2)}) %collective-permute-start.1) | collective-permute-done | bytes 131104 | tf_op jit(solution)/shard_map/ppermute | solution.py:404
  7.6 0.0 collective-permute-done.from_right
  7.6 0.0 copy-start
  7.6 0.8 %copy-done = bf16[256,118]{0,1:T(8,128)(2,1)S(1)} copy-done((bf16[256,118]{0,1:T(8,128)(2,1)S(1)}, bf16[256,118]{0,1:T(8,128)(2,1)}, u32[]{:S(2)}) %copy-start) | copy-done | bytes 60440
  8.4 0.0 copy-start.1
  8.4 0.9 %copy-done.1 = bf16[4,128,128]{2,1,0:T(8,128)(2,1)S(1)} copy-done((bf16[4,128,128]{2,1,0:T(8,128)(2,1)S(1)}, bf16[4,128,128]{2,1,0:T(8,128)(2,1)}, u32[]{:S(2)}) %copy-start.1) | copy-done | bytes 131096
  9.3 0.0 copy-start.2
  9.3 0.8 %copy-done.2 = bf16[32,8,128]{2,1,0:T(8,128)(2,1)S(1)} copy-done((bf16[32,8,128]{2,1,0:T(8,128)(2,1)S(1)}, bf16[32,8,128]{2,1,0:T(8,128)(2,1)}, u32[]{:S(2)}) %copy-start.2) | copy-done | bytes 65560
  10.2 0.0 copy-start.3
  10.2 0.8 %copy-done.3 = s32[64,118]{1,0:T(8,128)S(1)} copy-done((s32[64,118]{1,0:T(8,128)S(1)}, s32[64,118]{1,0:T(8,128)}, u32[]{:S(2)}) %copy-start.3) | copy-done | bytes 30232
  10.9 0.0 copy-start.4
  10.9 0.8 %copy-done.4 = bf16[16,4,256]{2,1,0:T(4,128)(2,1)S(1)} copy-done((bf16[16,4,256]{2,1,0:T(4,128)(2,1)S(1)}, bf16[16,4,256]{2,1,0:T(4,128)(2,1)}, u32[]{:S(2)}) %copy-start.4) | copy-done | bytes 32792
  11.7 0.0 copy-start.5
  11.7 0.7 %copy-done.5 = s32[32,8]{0,1:T(8,128)S(1)} copy-done((s32[32,8]{0,1:T(8,128)S(1)}, s32[32,8]{0,1:T(8,128)}, u32[]{:S(2)}) %copy-start.5) | copy-done | bytes 1048
  12.4 19.0 %front.1 = (bf16[2048,256]{1,0:T(8,128)(2,1)S(1)}, bf16[2048,256]{1,0:T(8,128)(2,1)S(1)}, f32[256,256]{1,0:T(8,128)S(1)}, bf16[22,16,256]{2,1,0:T(8,128)(2,1)S(1...) custom-call(s32[1]{0:T(128)} %bitcast.me_ref, ...), custom_call_target="tpu_custom_call" | custom-call | tf_op jit(solution)/shard_map/front/pallas_call | solution.py:225
  31.4 3.0 %collective-permute-start.2 = (bf16[22,16,256]{2,1,0:T(8,128)(2,1)S(1)}, bf16[22,16,256]{2,1,0:T(8,128)(2,1)S(1)}, u32[]{:S(2)}, u32[]{:S(2)}) collective-permute-start(bf16[22,16,256]{2,1,0:T(8,128)(2,1)S(1)} %get-tuple-element.15.note), channel_id=1, source_target_pairs={{0,1},{1,0},{2,3},{3,2},{4,5},{5,4},{6,7},{7,6},{8,9},{9,8},{10,11... | collective-permute-start | bytes 540680 | tf_op jit(solution)/shard_map/ppermute | solution.py:410
  34.4 1.0 %collective-permute-done.2.partner = bf16[22,16,256]{2,1,0:T(8,128)(2,1)S(1)} collective-permute-done((bf16[22,16,256]{2,1,0:T(8,128)(2,1)S(1)}, bf16[22,16,256]{2,1,0:T(8,128)(2,1)S(1)}, u32[]{:S(2)}, u32[]{:S(2)}) %collective-permute-start.2) | collective-permute-done | bytes 180256 | tf_op jit(solution)/shard_map/ppermute | solution.py:410
  35.5 5.0 %collective-permute-start.3 = (bf16[18,16,256]{2,1,0:T(8,128)(2,1)S(1)}, bf16[18,16,256]{2,1,0:T(8,128)(2,1)S(1)}, u32[]{:S(2)}, u32[]{:S(2)}) collective-permute-start(bf16[18,16,256]{2,1,0:T(8,128)(2,1)S(1)} %constant_dynamic-update-slice_fusion), channel_id=1, source_target_pairs={{0,255},{1,2},{2,1},{3,4},{4,3},{5,6},{6,5},{7,8},{8,7},{9,10},{10... | collective-permute-start | bytes 442376 | tf_op jit(solution)/shard_map/ppermute | solution.py:410
  40.5 4.2 %collective-permute-done.3.crossed = bf16[18,16,256]{2,1,0:T(8,128)(2,1)S(1)} collective-permute-done((bf16[18,16,256]{2,1,0:T(8,128)(2,1)S(1)}, bf16[18,16,256]{2,1,0:T(8,128)(2,1)S(1)}, u32[]{:S(2)}, u32[]{:S(2)}) %collective-permute-start.3) | collective-permute-done | bytes 147488 | tf_op jit(solution)/shard_map/ppermute | solution.py:410
  44.8 0.3 collective-permute-start.4
  45.1 10.8 %collective-permute-start.5 = (bf16[2,16,256]{2,1,0:T(8,128)(2,1)S(1)}, bf16[2,16,256]{2,1,0:T(8,128)(2,1)S(1)}, u32[]{:S(2)}, u32[]{:S(2)}) collective-permute-start(bf16[2,16,256]{2,1,0:T(8,128)(2,1)S(1)} %get-tuple-element.16), channel_id=1, source_target_pairs={{0,253},{1,4},{2,255},{3,6},{4,1},{5,8},{6,3},{7,10},{8,5},{9,12},... | collective-permute-start | bytes 49160 | tf_op jit(solution)/shard_map/ppermute | solution.py:410
  55.9 1.4 %collective-permute-done.5.far = bf16[2,16,256]{2,1,0:T(8,128)(2,1)S(1)} collective-permute-done((bf16[2,16,256]{2,1,0:T(8,128)(2,1)S(1)}, bf16[2,16,256]{2,1,0:T(8,128)(2,1)S(1)}, u32[]{:S(2)}, u32[]{:S(2)}) %collective-permute-start.5) | collective-permute-done | bytes 16416 | tf_op jit(solution)/shard_map/ppermute | solution.py:410
  57.4 0.0 collective-permute-done.4.relayed
  57.4 9.3 %back.1 = (bf16[16,4,256]{2,1,0:T(4,128)(2,1)}, bf16[32,64,256]{2,1,0:T(8,128)(2,1)}, bf16[64,128]{1,0:T(8,128)(2,1)}) custom-call(s32[1]{0:T(128)} %bitcast.me_ref, f32[256,256]{1,0:T(8,128)S(1)} %get-tuple-element.14.lifted, bf16[22,16,256]{2,1,0:T(8,128)(2,1)S(1)} %get-tuple-element.15.note, bf16[22,16,256]{2,1,0:T(8,128)(2,1)S(1)} %collective-permute-done.2.partner, ...), custom_call_target="tpu_custom_call" | custom-call | tf_op jit(solution)/shard_map/back/pallas_call | solution.py:379
  (10 shorter events, 0.1 us)
Async XLA Ops:
  1.6 6.0 %collective-permute-start.1 = (bf16[32,8,256]{2,1,0:T(8,128)(2,1)S(1)}, bf16[32,8,256]{2,1,0:T(8,128)(2,1)S(1)}, u32[]{:S(2)}, u32[]{:S(2)}) collective-permute-start(bf16[32,8,256]{2,1,0:T(8,128)(2,1)S(1)} %get-tuple-element.25), channel_id=1, source_target_pairs={{255,0},{0,1},{1,2},{2,3},{3,4},{4,5},{5,6},{6,7},{7,8},{8,9},{9,1... | collective-permute-start | bytes 393224 | tf_op jit(solution)/shard_map/ppermute | solution.py:404
  1.7 5.9 %collective-permute-start = (bf16[32,8,256]{2,1,0:T(8,128)(2,1)S(1)}, bf16[32,8,256]{2,1,0:T(8,128)(2,1)S(1)}, u32[]{:S(2)}, u32[]{:S(2)}) collective-permute-start(bf16[32,8,256]{2,1,0:T(8,128)(2,1)S(1)} %get-tuple-element.26), channel_id=1, source_target_pairs={{1,0},{2,1},{3,2},{4,3},{5,4},{6,5},{7,6},{8,7},{9,8},{10,9},{11,1... | collective-permute-start | bytes 393224 | tf_op jit(solution)/shard_map/ppermute | solution.py:404
  7.6 0.8 %copy-start = (bf16[256,118]{0,1:T(8,128)(2,1)S(1)}, bf16[256,118]{0,1:T(8,128)(2,1)}, u32[]{:S(2)}) copy-start(bf16[256,118]{0,1:T(8,128)(2,1)} %param.11) | copy-start | bytes 181252
  8.4 0.9 %copy-start.1 = (bf16[4,128,128]{2,1,0:T(8,128)(2,1)S(1)}, bf16[4,128,128]{2,1,0:T(8,128)(2,1)}, u32[]{:S(2)}) copy-start(bf16[4,128,128]{2,1,0:T(8,128)(2,1)} %lidar.1) | copy-start | bytes 393220
  9.3 0.8 %copy-start.2 = (bf16[32,8,128]{2,1,0:T(8,128)(2,1)S(1)}, bf16[32,8,128]{2,1,0:T(8,128)(2,1)}, u32[]{:S(2)}) copy-start(bf16[32,8,128]{2,1,0:T(8,128)(2,1)} %pillars.1) | copy-start | bytes 196612
  10.2 0.8 %copy-start.3 = (s32[64,118]{1,0:T(8,128)S(1)}, s32[64,118]{1,0:T(8,128)}, u32[]{:S(2)}) copy-start(s32[64,118]{1,0:T(8,128)} %bins.1) | copy-start | bytes 90628
  10.9 0.8 %copy-start.4 = (bf16[16,4,256]{2,1,0:T(4,128)(2,1)S(1)}, bf16[16,4,256]{2,1,0:T(4,128)(2,1)}, u32[]{:S(2)}) copy-start(bf16[16,4,256]{2,1,0:T(4,128)(2,1)} %cotangent.1) | copy-start | bytes 98308
  11.7 0.7 %copy-start.5 = (s32[32,8]{0,1:T(8,128)S(1)}, s32[32,8]{0,1:T(8,128)}, u32[]{:S(2)}) copy-start(s32[32,8]{0,1:T(8,128)} %param.14) | copy-start | bytes 3076
  31.4 4.0 %collective-permute-start.2 = (bf16[22,16,256]{2,1,0:T(8,128)(2,1)S(1)}, bf16[22,16,256]{2,1,0:T(8,128)(2,1)S(1)}, u32[]{:S(2)}, u32[]{:S(2)}) collective-permute-start(bf16[22,16,256]{2,1,0:T(8,128)(2,1)S(1)} %get-tuple-element.15.note), channel_id=1, source_target_pairs={{0,1},{1,0},{2,3},{3,2},{4,5},{5,4},{6,7},{7,6},{8,9},{9,8},{10,11... | collective-permute-start | bytes 540680 | tf_op jit(solution)/shard_map/ppermute | solution.py:410
  35.5 9.3 %collective-permute-start.3 = (bf16[18,16,256]{2,1,0:T(8,128)(2,1)S(1)}, bf16[18,16,256]{2,1,0:T(8,128)(2,1)S(1)}, u32[]{:S(2)}, u32[]{:S(2)}) collective-permute-start(bf16[18,16,256]{2,1,0:T(8,128)(2,1)S(1)} %constant_dynamic-update-slice_fusion), channel_id=1, source_target_pairs={{0,255},{1,2},{2,1},{3,4},{4,3},{5,6},{6,5},{7,8},{8,7},{9,10},{10... | collective-permute-start | bytes 442376 | tf_op jit(solution)/shard_map/ppermute | solution.py:410
  44.8 12.5 %collective-permute-start.4 = (bf16[8,16,256]{2,1,0:T(8,128)(2,1)S(1)}, bf16[8,16,256]{2,1,0:T(8,128)(2,1)S(1)}, u32[]{:S(2)}, u32[]{:S(2)}) collective-permute-start(bf16[8,16,256]{2,1,0:T(8,128)(2,1)S(1)} %pad_maximum_fusion), channel_id=1, source_target_pairs={{0,1},{1,0},{2,3},{3,2},{4,5},{5,4},{6,7},{7,6},{8,9},{9,8},{10,11... | collective-permute-start | bytes 196616 | tf_op jit(solution)/shard_map/ppermute | solution.py:410
  45.1 12.3 %collective-permute-start.5 = (bf16[2,16,256]{2,1,0:T(8,128)(2,1)S(1)}, bf16[2,16,256]{2,1,0:T(8,128)(2,1)S(1)}, u32[]{:S(2)}, u32[]{:S(2)}) collective-permute-start(bf16[2,16,256]{2,1,0:T(8,128)(2,1)S(1)} %get-tuple-element.16), channel_id=1, source_target_pairs={{0,253},{1,4},{2,255},{3,6},{4,1},{5,8},{6,3},{7,10},{8,5},{9,12},... | collective-permute-start | bytes 49160 | tf_op jit(solution)/shard_map/ppermute | solution.py:410

commit v2 on v1

--- a/solution.py
+++ b/solution.py
@@ -8,7 +8,8 @@
 AXES = ("branch", "strip")
 ROWS = 32
 COLS = 64
-WIDE = 80
+WIDE = 72
+HALO = (WIDE - COLS) // 2
 C = 256
 CL = 128
 BINS = 118
@@ -19,11 +20,12 @@
 WIN = 16
 REACH = 6
 SLOTS = 12
-BLOCK = 8
+BLOCK = 16
 TILE_H = 4
 TILE = TILE_H * COLS
-FUSE = 2
-SPREAD = 2
+UNROLL = 4
+TALL_H = 16
+TALL = TALL_H * COLS
 F32 = jnp.float32
 BF16 = jnp.bfloat16
 
@@ -89,44 +91,94 @@
         )
 
 
-def front_kernel(
-    me_ref, image, from_right, from_left, weights, depth, bins,
-    pillars, counts, lidar, cotangent,
-    feat_out, share_out, lifted_out, note_out, far_out, probs_out, gain_out, slot_out,
-    first, second, held, depth_pad, spread, masks, flat, sems,
+def prepare_kernel(
+    me_ref, image, weights, merging, depth_hbm, bins_hbm, pillars_hbm, counts_hbm, lidar_hbm,
+    cotangent_hbm,
+    padded, held, merge_held, spread, depth_pad, masks, slot_out, side,
+    depth, bins, pillars, counts, lidar, cotangent, flat, sems,
 ):
-    image_copy = pltpu.make_async_copy(
-        image, first.at[pl.ds(1, ROWS), pl.ds(0, COLS)], sems.at[LAYERS]
-    )
-    image_copy.start()
-    weight_copies = [
-        pltpu.make_async_copy(weights.at[index], held.at[index], sems.at[index])
-        for index in range(LAYERS)
+    copies = [
+        pltpu.make_async_copy(source, target, sems.at[index])
+        for index, (source, target) in enumerate(
+            [
+                (depth_hbm, depth),
+                (bins_hbm, bins),
+                (pillars_hbm, pillars),
+                (counts_hbm, counts),
+                (lidar_hbm, lidar),
+                (cotangent_hbm, cotangent),
+                (image, padded.at[pl.ds(1, ROWS), pl.ds(0, COLS)]),
+                (weights, held),
+                (merging, merge_held),
+            ]
+        )
     ]
-    for copy in weight_copies:
+    for copy in copies:
         copy.start()
-    first[0] = jnp.zeros((WIDE, C), BF16)
-    first[ROWS + 1] = jnp.zeros((WIDE, C), BF16)
-    second[0] = jnp.zeros((WIDE, C), BF16)
-    second[ROWS + 1] = jnp.zeros((WIDE, C), BF16)
-    first[1 : ROWS + 1, COLS:WIDE, :] = jnp.concatenate(
-        [from_right[...], from_left[...]], axis=1
-    )
+    padded[0] = jnp.zeros((WIDE, C), BF16)
+    padded[ROWS + 1] = jnp.zeros((WIDE, C), BF16)
+    fill_spread(spread)
+    for copy in copies[:6]:
+        copy.wait()
     depth_pad[BINS - 6 :, :] = jnp.zeros((LANES - BINS + 6, C), BF16)
     depth_pad[0:BINS, :] = depth[...]
-    fill_spread(spread)
-    fill_side(note_out.at[pl.ds(WIN, 6)], pillars, counts, lidar, cotangent, flat)
+    fill_side(side, pillars, counts, lidar, cotangent, flat)
     cells = bins[...]
     sector = cells // (BR * BA)
     step = sector - me_ref[0] + 1
     step = jnp.where(step < 0, step + 256, step)
     step = jnp.where(step > 255, step - 256, step)
-    slot = step * BA + cells % BA
     slot_out[...] = jnp.full((COLS, LANES), -1, jnp.int32)
-    slot_out[:, 0:BINS] = slot
+    slot_out[:, 0:BINS] = step * BA + cells % BA
     slot_map = slot_out[...]
     for index in range(SLOTS):
         masks[index] = (slot_map == index).astype(F32).astype(BF16)
+    for copy in copies[6:]:
+        copy.wait()
+
+
+def prepare(*operands):
+    return pl.pallas_call(
+        prepare_kernel,
+        out_shape=(
+            jax.ShapeDtypeStruct((ROWS + 2, WIDE, C), BF16),
+            jax.ShapeDtypeStruct((LAYERS, 9, C, C), BF16),
+            jax.ShapeDtypeStruct((9, C + CL, C), BF16),
+            jax.ShapeDtypeStruct((SLOTS * LANES, WIN * BR), BF16),
+            jax.ShapeDtypeStruct((LANES, C), BF16),
+            jax.ShapeDtypeStruct((SLOTS, COLS, LANES), BF16),
+            jax.ShapeDtypeStruct((COLS, LANES), jnp.int32),
+            jax.ShapeDtypeStruct((6, BR, C), BF16),
+        ),
+        in_specs=[whole(pltpu.SMEM)] + [whole(pltpu.HBM)] * 9,
+        out_specs=(whole(),) * 8,
+        scratch_shapes=[
+            pltpu.VMEM((BINS, C), BF16),
+            pltpu.VMEM((COLS, BINS), jnp.int32),
+            pltpu.VMEM((2 * BR, 2 * BA, CL), BF16),
+            pltpu.VMEM((2 * BA, 2 * BR), jnp.int32),
+            pltpu.VMEM((4, CL, CL), BF16),
+            pltpu.VMEM((BR, BA, C), BF16),
+            pltpu.VMEM((BR * BA, C), F32),
+            pltpu.SemaphoreType.DMA((9,)),
+        ],
+        compiler_params=pltpu.CompilerParams(vmem_limit_bytes=24 * 2**20),
+        cost_estimate=pl.CostEstimate(flops=10**8, bytes_accessed=8 * 2**20, transcendentals=0),
+        name="prepare",
+    )(*operands)
+
+
+def front_kernel(
+    me_ref, padded_in, from_right, from_left, held, depth_pad, spread, masks, side,
+    first, feat_out, share_out, lifted_out, note_out, far_out, probs_out, gain_out,
+    second,
+):
+    second[0] = jnp.zeros((WIDE, C), BF16)
+    second[ROWS + 1] = jnp.zeros((WIDE, C), BF16)
+    first[1 : ROWS + 1, COLS:WIDE, :] = jnp.concatenate(
+        [from_right[...].astype(F32), from_left[...].astype(F32)], axis=1
+    ).astype(BF16)
+    note_out[WIN : WIN + 6] = side[...]
 
     def convolved(source, index, top, narrow):
         lhs = jnp.concatenate(
@@ -155,27 +207,22 @@
             out = part if out is None else out + part
         return jnp.maximum(out, 0.0).astype(BF16)
 
-    def layer(source, target, index):
-        weight_copies[index].wait()
-
-        @pl.loop(0, ROWS // BLOCK, unroll=True)
-        def _(block):
-            target[pl.ds(block * BLOCK + 1, BLOCK)] = convolved(
+    for index, (source, target) in enumerate([(first, second), (second, first)]):
+        for block in range(ROWS // BLOCK):
+            target[block * BLOCK + 1 : (block + 1) * BLOCK + 1] = convolved(
                 source, index, block * BLOCK, False
             )
-
-    image_copy.wait()
-    layer(first, second, 0)
-    layer(second, first, 1)
-    weight_copies[2].wait()
-
-    lifted_out[...] = jnp.zeros((WIN * BR, C), F32)
+    for block in range(ROWS // BLOCK):
+        feat_out[block * BLOCK * COLS : (block + 1) * BLOCK * COLS, :] = convolved(
+            first, 2, block * BLOCK, True
+        ).reshape(BLOCK * COLS, C)
+
     lane_ok = iota((TILE, LANES), 1) < BINS
 
-    def lift(block, tile):
+    @pl.loop(0, ROWS // TILE_H, unroll=UNROLL)
+    def _(tile):
         rows = pl.ds(pl.multiple_of(tile * TILE, TILE), TILE)
-        feat_out[rows, :] = block
-        logits = nt_dot(block, depth_pad[...])
+        logits = nt_dot(feat_out[rows, :], depth_pad[...])
         decay = jnp.exp(-jnp.abs(logits))
         tail = jnp.log(1.0 + decay)
         soft = jnp.maximum(logits, 0.0) + tail + 0.05
@@ -186,7 +233,7 @@
         probs_out[rows, :] = probs
         gain_out[rows, :] = gate * scale
         low = probs.astype(BF16).reshape(TILE_H, COLS, LANES)
-        share = dot(
+        share_out[rows, :] = dot(
             jnp.concatenate(
                 [
                     (low * masks[index][None]).reshape(TILE, LANES)
@@ -196,19 +243,10 @@
             ),
             spread[...],
         ).astype(BF16)
-        share_out[rows, :] = share
-        lifted_out[...] += tn_dot(share, block)
-
-    @pl.loop(0, ROWS // BLOCK, unroll=FUSE)
-    def _(block):
-        made = convolved(first, 2, block * BLOCK, True)
-        for part in range(BLOCK // TILE_H):
-            lift(
-                made[part * TILE_H : (part + 1) * TILE_H].reshape(TILE, C),
-                block * (BLOCK // TILE_H) + part,
-            )
-
-    note_out[0:WIN] = lifted_out[...].astype(BF16).reshape(WIN, BR, C)
+
+    lifted = tn_dot(share_out[...], feat_out[...])
+    lifted_out[...] = lifted
+    note_out[0:WIN] = lifted.astype(BF16).reshape(WIN, BR, C)
     odd = lax.rem(me_ref[0], 2)
 
     @pl.when(odd == 1)
@@ -220,11 +258,12 @@
         far_out[...] = note_out[2:4]
 
 
-def front(me, image, from_right, from_left, weights, depth, bins, pillars, counts, lidar, cotangent):
+def front(*operands):
     total = ROWS * COLS
     return pl.pallas_call(
         front_kernel,
         out_shape=(
+            jax.ShapeDtypeStruct((ROWS + 2, WIDE, C), BF16),
             jax.ShapeDtypeStruct((total, C), BF16),
             jax.ShapeDtypeStruct((total, WIN * BR), BF16),
             jax.ShapeDtypeStruct((WIN * BR, C), F32),
@@ -232,26 +271,14 @@
             jax.ShapeDtypeStruct((2, BR, C), BF16),
             jax.ShapeDtypeStruct((total, LANES), F32),
             jax.ShapeDtypeStruct((total, LANES), F32),
-            jax.ShapeDtypeStruct((COLS, LANES), jnp.int32),
         ),
-        in_specs=[
-            whole(pltpu.SMEM), whole(pl.ANY), whole(), whole(), whole(pl.ANY),
-            whole(), whole(), whole(), whole(), whole(), whole(),
-        ],
+        in_specs=[whole(pltpu.SMEM)] + [whole()] * 8,
         out_specs=(whole(),) * 8,
-        scratch_shapes=[
-            pltpu.VMEM((ROWS + 2, WIDE, C), BF16),
-            pltpu.VMEM((ROWS + 2, WIDE, C), BF16),
-            pltpu.VMEM((LAYERS, 9, C, C), BF16),
-            pltpu.VMEM((LANES, C), BF16),
-            pltpu.VMEM((SLOTS * LANES, WIN * BR), BF16),
-            pltpu.VMEM((SLOTS, COLS, LANES), BF16),
-            pltpu.VMEM((BR * BA, C), F32),
-            pltpu.SemaphoreType.DMA((LAYERS + 1,)),
-        ],
-        compiler_params=pltpu.CompilerParams(vmem_limit_bytes=48 * 2**20),
+        scratch_shapes=[pltpu.VMEM((ROWS + 2, WIDE, C), BF16)],
+        input_output_aliases={1: 0},
+        compiler_params=pltpu.CompilerParams(vmem_limit_bytes=32 * 2**20),
         name="front",
-    )(me, image, from_right, from_left, weights, depth, bins, pillars, counts, lidar, cotangent)
+    )(*operands)
 
 
 def along_cycles(part, down):
@@ -265,13 +292,10 @@
 
 def back_kernel(
     me_ref, lifted, note, partner, crossed, relayed, far, weights, feat, share, probs, gain,
-    slots, depth,
+    slots, depth_pad, spread,
     merged_out, cam_out, lid_out,
-    cam, cot, lid, table, spread, wide_table, depth_pad,
+    cam, cot, lid, table, wide_table,
 ):
-    depth_pad[BINS - 6 :, :] = jnp.zeros((LANES - BINS + 6, C), BF16)
-    depth_pad[0:BINS, :] = depth[...]
-    fill_spread(spread)
 
     def put_lid(at, packed):
         lid[at] = packed[:, 0:CL]
@@ -355,24 +379,24 @@
     lid_out[...] = dot(swap, own_lid).astype(BF16)
     wide_table[...] = dot(spread[...], table[...]).astype(BF16)
 
-    @pl.loop(0, ROWS // TILE_H, unroll=SPREAD)
+    @pl.loop(0, ROWS // TALL_H, unroll=True)
     def _(tile):
-        rows = pl.ds(pl.multiple_of(tile * TILE, TILE), TILE)
+        rows = pl.ds(pl.multiple_of(tile * TALL, TALL), TALL)
         block = feat[rows, :]
         slot_map = slots[...]
-        picked = jnp.zeros((TILE_H, COLS, LANES), F32)
+        picked = jnp.zeros((TALL_H, COLS, LANES), F32)
         for pair in range(SLOTS // 2):
             both = nt_dot(block, wide_table[pair * 2 * LANES : (pair + 1) * 2 * LANES, :])
             for side in range(2):
                 value = both[:, side * LANES : (side + 1) * LANES].reshape(
-                    TILE_H, COLS, LANES
+                    TALL_H, COLS, LANES
                 )
                 picked = jnp.where((slot_map == 2 * pair + side)[None], value, picked)
-        picked = picked.reshape(TILE, LANES)
+        picked = picked.reshape(TALL, LANES)
         mean = jnp.sum(picked * probs[rows, :], axis=1, keepdims=True)
         grad_logits = ((picked - mean) * gain[rows, :]).astype(BF16)
         out = dot(share[rows, :], table[...]) + dot(grad_logits, depth_pad[...])
-        cam_out[pl.ds(tile * TILE_H, TILE_H)] = out.astype(BF16).reshape(TILE_H, COLS, C)
+        cam_out[pl.ds(tile * TALL_H, TALL_H)] = out.astype(BF16).reshape(TALL_H, COLS, C)
 
 
 def back(*operands):
@@ -383,18 +407,16 @@
             jax.ShapeDtypeStruct((ROWS, COLS, C), BF16),
             jax.ShapeDtypeStruct((BR * BA, CL), BF16),
         ),
-        in_specs=[whole(pltpu.SMEM)] + [whole()] * 13,
+        in_specs=[whole(pltpu.SMEM)] + [whole()] * 14,
         out_specs=(whole(),) * 3,
         scratch_shapes=[
             pltpu.VMEM((WIN, BR, C), F32),
             pltpu.VMEM((WIN, BR, C), BF16),
             pltpu.VMEM((WIN, BR, CL), BF16),
             pltpu.VMEM((WIN * BR, C), BF16),
-            pltpu.VMEM((SLOTS * LANES, WIN * BR), BF16),
             pltpu.VMEM((SLOTS * LANES, C), BF16),
-            pltpu.VMEM((LANES, C), BF16),
         ],
-        compiler_params=pltpu.CompilerParams(vmem_limit_bytes=48 * 2**20),
+        compiler_params=pltpu.CompilerParams(vmem_limit_bytes=32 * 2**20),
         name="back",
     )(*operands)
 
@@ -417,12 +439,20 @@
     me = lax.axis_index(AXES).astype(jnp.int32)
     odd = me % 2 == 1
     me = me.reshape(1)
-    from_right = shifted(image_feats[:, 0:8], -1)
-    from_left = shifted(image_feats[:, COLS - 8 :], 1)
-    depth = depth_weight.T
-    feat, share, lifted, note, far, probs, gain, slots = front(
-        me, image_feats, from_right, from_left, cam_weights, depth, ray_bins,
-        pillar_sums, pillar_counts.T, lidar_weight, out_cotangent,
+    from_right = shifted(image_feats[:, 0:HALO], -1)
+    from_left = shifted(image_feats[:, COLS - HALO :], 1)
+    padded, held, merge_held, spread, depth_pad, masks, slots, side = prepare(
+        me,
+        *[
+            pltpu.with_memory_space_constraint(value, pltpu.HBM)
+            for value in (
+                image_feats, cam_weights, merge_weight, depth_weight.T, ray_bins, pillar_sums,
+                pillar_counts.T, lidar_weight, out_cotangent,
+            )
+        ],
+    )
+    _, feat, share, lifted, note, far, probs, gain = front(
+        me, padded, from_right, from_left, held, depth_pad, spread, masks, side
     )
     partner = swapped(note, -1)
     far_got = swapped(far, 3)
@@ -452,8 +482,8 @@
     )
     relayed = swapped(relay, -1)
     merged, cam_grad, lid_grad = back(
-        me, lifted, note, partner, crossed, relayed, far_got, merge_weight, feat, share,
-        probs, gain, slots, depth,
+        me, lifted, note, partner, crossed, relayed, far_got, merge_held, feat, share,
+        probs, gain, slots, depth_pad, spread,
     )
     return merged, cam_grad, lid_grad.reshape(BR, BA, CL)
 

time: 67 us -> 56.5 us (0.84)
  the two profiles are of different devices: /device:TPU:4 before, /device:TPU:0 now
where the time goes in v2:
time: 56.5 us; the launch traced here: 56.4 us
  waiting for transfers between devices  23.5 us (42%)
  Pallas kernels  21 us (37%)
  starting transfers between devices  10.1 us (18%)
  local copies, waits for them, and re-layouts  1.07 us (2%)
  between operations  0.75 us (1%)
    ppermute x4, waiting for transfers between devices, swapped(): return lax.ppermute(block, AXES, route)  17.5 us
    pallas_call x1, Pallas kernels, front(): pl.pallas_call(front_kernel, out_shape=(jax.ShapeDtypeStruct((ROWS + 2, W...  12.2 us
    ppermute x2, starting transfers between devices, shifted(): lax.ppermute(block, AXES, [((i - distance) % count, i) for i in range(cou...  8.28 us
    ppermute x2, waiting for transfers between devices, shifted(): lax.ppermute(block, AXES, [((i - distance) % count, i) for i in range(cou...  5.97 us
    pallas_call x1, Pallas kernels, back(): pl.pallas_call(back_kernel, out_shape=(jax.ShapeDtypeStruct((BR, BA, C),...  5.69 us
    pallas_call x1, Pallas kernels, prepare(): pl.pallas_call(prepare_kernel, out_shape=(jax.ShapeDtypeStruct((ROWS + 2,...  3.14 us
    ppermute x4, starting transfers between devices, swapped(): return lax.ppermute(block, AXES, route)  1.77 us
  transfers between devices with their start and end apart: 6, of which 4 were waited for; matrix products, arithmetic and copies ran while one was open for 0% of the time, Pallas kernels for 6%

profile of v2, /device:TPU:0, one launch (start us, length us, event | category | flops | bytes accessed | tf_op | source)
XLA Modules:
  0.0 56.4 jit_solution(1295217923723830637)
XLA Ops:
  0.6 1.0 %fusion.1 = (bf16[32,4,256]{2,1,0:T(4,128)(2,1)S(1)}, bf16[32,4,256]{2,1,0:T(4,128)(2,1)S(1)}) fusion(bf16[32,64,256]{2,1,0:T(8,128)(2,1)} %image.1), kind=kLoop, calls=%fused_computation.12 | loop fusion | bytes 262144 | tf_op jit(solution)/shard_map/slice | solution.py:443
  1.7 8.3 %collective-permute-start = (bf16[32,4,256]{2,1,0:T(4,128)(2,1)S(1)}, bf16[32,4,256]{2,1,0:T(4,128)(2,1)S(1)}, u32[]{:S(2)}, u32[]{:S(2)}) collective-permute-start(bf16[32,4,256]{2,1,0:T(4,128)(2,1)S(1)} %get-tuple-element.40), channel_id=1, source_target_pairs={{1,0},{2,1},{3,2},{4,3},{5,4},{6,5},{7,6},{8,7},{9,8},{10,9},{11,1... | collective-permute-start | bytes 196616 | tf_op jit(solution)/shard_map/ppermute | solution.py:426
  9.9 0.0 collective-permute-start.1
  9.9 3.1 %prepare.1 = (bf16[34,72,256]{2,1,0:T(8,128)(2,1)S(1)}, bf16[3,9,256,256]{3,2,1,0:T(8,128)(2,1)S(1)}, bf16[9,384,256]{2,1,0:T(8,128)(2,1)S(1)}, bf16[1536,256]{1...) custom-call(s32[1]{0:T(128)} %bitcast.me_ref, ...), custom_call_target="tpu_custom_call" | custom-call | flops 100000000 | bytes 8388608 | tf_op jit(solution)/shard_map/prepare/pallas_call | solution.py:141
  13.1 0.0 collective-permute-done.from_right
  13.1 6.0 %collective-permute-done.1.from_left = bf16[32,4,256]{2,1,0:T(4,128)(2,1)S(1)} collective-permute-done((bf16[32,4,256]{2,1,0:T(4,128)(2,1)S(1)}, bf16[32,4,256]{2,1,0:T(4,128)(2,1)S(1)}, u32[]{:S(2)}, u32[]{:S(2)}) %collective-permute-start.1) | collective-permute-done | bytes 65568 | tf_op jit(solution)/shard_map/ppermute | solution.py:426
  19.1 12.2 %front.1 = (bf16[34,72,256]{2,1,0:T(8,128)(2,1)S(1)}, bf16[2048,256]{1,0:T(8,128)(2,1)S(1)}, bf16[2048,256]{1,0:T(8,128)(2,1)S(1)}, f32[256,256]{1,0:T(8,128)S(1...) custom-call(s32[1]{0:T(128)} %bitcast.me_ref, ...), custom_call_target="tpu_custom_call", output_to_operand_aliasing={{0}: (1, {})} | custom-call | tf_op jit(solution)/shard_map/front/pallas_call | solution.py:263
  31.2 0.1 collective-permute-start.2
  31.4 1.4 %collective-permute-done.2.partner = bf16[22,16,256]{2,1,0:T(8,128)(2,1)S(1)} collective-permute-done((bf16[22,16,256]{2,1,0:T(8,128)(2,1)S(1)}, bf16[22,16,256]{2,1,0:T(8,128)(2,1)S(1)}, u32[]{:S(2)}, u32[]{:S(2)}) %collective-permute-start.2) | collective-permute-done | bytes 180256 | tf_op jit(solution)/shard_map/ppermute | solution.py:432
  32.9 1.3 %collective-permute-start.3 = (bf16[18,16,256]{2,1,0:T(8,128)(2,1)S(1)}, bf16[18,16,256]{2,1,0:T(8,128)(2,1)S(1)}, u32[]{:S(2)}, u32[]{:S(2)}) collective-permute-start(bf16[18,16,256]{2,1,0:T(8,128)(2,1)S(1)} %constant_dynamic-update-slice_fusion), channel_id=1, source_target_pairs={{0,255},{1,2},{2,1},{3,4},{4,3},{5,6},{6,5},{7,8},{8,7},{9,10},{10... | collective-permute-start | bytes 442376 | tf_op jit(solution)/shard_map/ppermute | solution.py:432
  34.2 8.8 %collective-permute-done.3.crossed = bf16[18,16,256]{2,1,0:T(8,128)(2,1)S(1)} collective-permute-done((bf16[18,16,256]{2,1,0:T(8,128)(2,1)S(1)}, bf16[18,16,256]{2,1,0:T(8,128)(2,1)S(1)}, u32[]{:S(2)}, u32[]{:S(2)}) %collective-permute-start.3) | collective-permute-done | bytes 147488 | tf_op jit(solution)/shard_map/ppermute | solution.py:432
  43.0 0.1 collective-permute-start.4
  43.1 0.3 collective-permute-start.5
  43.4 7.4 %collective-permute-done.5.far = bf16[2,16,256]{2,1,0:T(8,128)(2,1)S(1)} collective-permute-done((bf16[2,16,256]{2,1,0:T(8,128)(2,1)S(1)}, bf16[2,16,256]{2,1,0:T(8,128)(2,1)S(1)}, u32[]{:S(2)}, u32[]{:S(2)}) %collective-permute-start.5) | collective-permute-done | bytes 16416 | tf_op jit(solution)/shard_map/ppermute | solution.py:432
  50.7 0.0 collective-permute-done.4.relayed
  50.8 5.7 %back.1 = (bf16[16,4,256]{2,1,0:T(4,128)(2,1)}, bf16[32,64,256]{2,1,0:T(8,128)(2,1)}, bf16[64,128]{1,0:T(8,128)(2,1)}) custom-call(s32[1]{0:T(128)} %bitcast.me_ref, f32[256,256]{1,0:T(8,128)S(1)} %get-tuple-element.27.lifted, bf16[22,16,256]{2,1,0:T(8,128)(2,1)S(1)} %get-tuple-element.28.note, bf16[22,16,256]{2,1,0:T(8,128)(2,1)S(1)} %collective-permute-done.2.partner, ...), custom_call_target="tpu_custom_call" | custom-call | tf_op jit(solution)/shard_map/back/pallas_call | solution.py:403
  (10 shorter events, 0.1 us)
Async XLA Ops:
  1.7 11.4 %collective-permute-start = (bf16[32,4,256]{2,1,0:T(4,128)(2,1)S(1)}, bf16[32,4,256]{2,1,0:T(4,128)(2,1)S(1)}, u32[]{:S(2)}, u32[]{:S(2)}) collective-permute-start(bf16[32,4,256]{2,1,0:T(4,128)(2,1)S(1)} %get-tuple-element.40), channel_id=1, source_target_pairs={{1,0},{2,1},{3,2},{4,3},{5,4},{6,5},{7,6},{8,7},{9,8},{10,9},{11,1... | collective-permute-start | bytes 196616 | tf_op jit(solution)/shard_map/ppermute | solution.py:426
  9.9 9.1 %collective-permute-start.1 = (bf16[32,4,256]{2,1,0:T(4,128)(2,1)S(1)}, bf16[32,4,256]{2,1,0:T(4,128)(2,1)S(1)}, u32[]{:S(2)}, u32[]{:S(2)}) collective-permute-start(bf16[32,4,256]{2,1,0:T(4,128)(2,1)S(1)} %get-tuple-element.39), channel_id=1, source_target_pairs={{255,0},{0,1},{1,2},{2,3},{3,4},{4,5},{5,6},{6,7},{7,8},{8,9},{9,1... | collective-permute-start | bytes 196616 | tf_op jit(solution)/shard_map/ppermute | solution.py:426
  31.2 1.5 %collective-permute-start.2 = (bf16[22,16,256]{2,1,0:T(8,128)(2,1)S(1)}, bf16[22,16,256]{2,1,0:T(8,128)(2,1)S(1)}, u32[]{:S(2)}, u32[]{:S(2)}) collective-permute-start(bf16[22,16,256]{2,1,0:T(8,128)(2,1)S(1)} %get-tuple-element.28.note), channel_id=1, source_target_pairs={{0,1},{1,0},{2,3},{3,2},{4,5},{5,4},{6,7},{7,6},{8,9},{9,8},{10,11... | collective-permute-start | bytes 540680 | tf_op jit(solution)/shard_map/ppermute | solution.py:432
  32.9 10.1 %collective-permute-start.3 = (bf16[18,16,256]{2,1,0:T(8,128)(2,1)S(1)}, bf16[18,16,256]{2,1,0:T(8,128)(2,1)S(1)}, u32[]{:S(2)}, u32[]{:S(2)}) collective-permute-start(bf16[18,16,256]{2,1,0:T(8,128)(2,1)S(1)} %constant_dynamic-update-slice_fusion), channel_id=1, source_target_pairs={{0,255},{1,2},{2,1},{3,4},{4,3},{5,6},{6,5},{7,8},{8,7},{9,10},{10... | collective-permute-start | bytes 442376 | tf_op jit(solution)/shard_map/ppermute | solution.py:432
  43.0 7.8 %collective-permute-start.4 = (bf16[8,16,256]{2,1,0:T(8,128)(2,1)S(1)}, bf16[8,16,256]{2,1,0:T(8,128)(2,1)S(1)}, u32[]{:S(2)}, u32[]{:S(2)}) collective-permute-start(bf16[8,16,256]{2,1,0:T(8,128)(2,1)S(1)} %pad_maximum_fusion), channel_id=1, source_target_pairs={{0,1},{1,0},{2,3},{3,2},{4,5},{5,4},{6,7},{7,6},{8,9},{9,8},{10,11... | collective-permute-start | bytes 196616 | tf_op jit(solution)/shard_map/ppermute | solution.py:432
  43.1 7.7 %collective-permute-start.5 = (bf16[2,16,256]{2,1,0:T(8,128)(2,1)S(1)}, bf16[2,16,256]{2,1,0:T(8,128)(2,1)S(1)}, u32[]{:S(2)}, u32[]{:S(2)}) collective-permute-start(bf16[2,16,256]{2,1,0:T(8,128)(2,1)S(1)} %get-tuple-element.29), channel_id=1, source_target_pairs={{0,253},{1,4},{2,255},{3,6},{4,1},{5,8},{6,3},{7,10},{8,5},{9,12},... | collective-permute-start | bytes 49160 | tf_op jit(solution)/shard_map/ppermute | solution.py:432

commit v3 on v2

--- a/solution.py
+++ b/solution.py
@@ -92,9 +92,9 @@
 
 
 def prepare_kernel(
-    me_ref, image, weights, merging, depth_hbm, bins_hbm, pillars_hbm, counts_hbm, lidar_hbm,
+    me_ref, image, weights, depth_hbm, bins_hbm, pillars_hbm, counts_hbm, lidar_hbm,
     cotangent_hbm,
-    padded, held, merge_held, spread, depth_pad, masks, slot_out, side,
+    padded, held, spread, depth_pad, masks, slot_out, side,
     depth, bins, pillars, counts, lidar, cotangent, flat, sems,
 ):
     copies = [
@@ -108,8 +108,7 @@
                 (lidar_hbm, lidar),
                 (cotangent_hbm, cotangent),
                 (image, padded.at[pl.ds(1, ROWS), pl.ds(0, COLS)]),
-                (weights, held),
-                (merging, merge_held),
+                (weights.at[0], held),
             ]
         )
     ]
@@ -142,16 +141,15 @@
         prepare_kernel,
         out_shape=(
             jax.ShapeDtypeStruct((ROWS + 2, WIDE, C), BF16),
-            jax.ShapeDtypeStruct((LAYERS, 9, C, C), BF16),
-            jax.ShapeDtypeStruct((9, C + CL, C), BF16),
+            jax.ShapeDtypeStruct((9, C, C), BF16),
             jax.ShapeDtypeStruct((SLOTS * LANES, WIN * BR), BF16),
             jax.ShapeDtypeStruct((LANES, C), BF16),
             jax.ShapeDtypeStruct((SLOTS, COLS, LANES), BF16),
             jax.ShapeDtypeStruct((COLS, LANES), jnp.int32),
             jax.ShapeDtypeStruct((6, BR, C), BF16),
         ),
-        in_specs=[whole(pltpu.SMEM)] + [whole(pltpu.HBM)] * 9,
-        out_specs=(whole(),) * 8,
+        in_specs=[whole(pltpu.SMEM)] + [whole(pltpu.HBM)] * 8,
+        out_specs=(whole(),) * 7,
         scratch_shapes=[
             pltpu.VMEM((BINS, C), BF16),
             pltpu.VMEM((COLS, BINS), jnp.int32),
@@ -160,7 +158,7 @@
             pltpu.VMEM((4, CL, CL), BF16),
             pltpu.VMEM((BR, BA, C), BF16),
             pltpu.VMEM((BR * BA, C), F32),
-            pltpu.SemaphoreType.DMA((9,)),
+            pltpu.SemaphoreType.DMA((8,)),
         ],
         compiler_params=pltpu.CompilerParams(vmem_limit_bytes=24 * 2**20),
         cost_estimate=pl.CostEstimate(flops=10**8, bytes_accessed=8 * 2**20, transcendentals=0),
@@ -169,18 +167,38 @@
 
 
 def front_kernel(
-    me_ref, padded_in, from_right, from_left, held, depth_pad, spread, masks, side,
-    first, feat_out, share_out, lifted_out, note_out, far_out, probs_out, gain_out,
-    second,
+    me_ref, padded_in, crossed, beside, held_first, depth_pad, spread, masks, side,
+    weights, merging,
+    first, feat_out, share_out, lifted_out, note_out, far_out, probs_out, gain_out, merge_held,
+    second, held_rest, sems,
 ):
+    copies = [
+        pltpu.make_async_copy(weights.at[1], held_rest.at[0], sems.at[0]),
+        pltpu.make_async_copy(weights.at[2], held_rest.at[1], sems.at[1]),
+        pltpu.make_async_copy(merging, merge_held, sems.at[2]),
+    ]
+    for copy in copies:
+        copy.start()
+    odd = lax.rem(me_ref[0], 2)
     second[0] = jnp.zeros((WIDE, C), BF16)
     second[ROWS + 1] = jnp.zeros((WIDE, C), BF16)
-    first[1 : ROWS + 1, COLS:WIDE, :] = jnp.concatenate(
-        [from_right[...].astype(F32), from_left[...].astype(F32)], axis=1
-    ).astype(BF16)
+
+    def put_halo(right, left):
+        first[1 : ROWS + 1, COLS:WIDE, :] = jnp.concatenate(
+            [right[...].astype(F32), left[...].astype(F32)], axis=1
+        ).astype(BF16)
+
+    @pl.when(odd == 1)
+    def _():
+        put_halo(crossed, beside)
+
+    @pl.when(odd == 0)
+    def _():
+        put_halo(beside, crossed)
+
     note_out[WIN : WIN + 6] = side[...]
 
-    def convolved(source, index, top, narrow):
+    def convolved(source, held, top, narrow):
         lhs = jnp.concatenate(
             [
                 source[pl.ds(top + down, BLOCK)].reshape(BLOCK * WIDE, C)
@@ -191,7 +209,7 @@
         out = None
         for right in (1, 0, 2):
             kernel = jnp.concatenate(
-                [held[index, 3 * down + right] for down in range(3)], axis=0
+                [held[3 * down + right] for down in range(3)], axis=0
             )
             if narrow and right == 1:
                 part = dot(
@@ -208,13 +226,17 @@
         return jnp.maximum(out, 0.0).astype(BF16)
 
     for index, (source, target) in enumerate([(first, second), (second, first)]):
+        if index == 1:
+            copies[0].wait()
+        held = held_first if index == 0 else held_rest.at[0]
         for block in range(ROWS // BLOCK):
             target[block * BLOCK + 1 : (block + 1) * BLOCK + 1] = convolved(
-                source, index, block * BLOCK, False
+                source, held, block * BLOCK, False
             )
+    copies[1].wait()
     for block in range(ROWS // BLOCK):
         feat_out[block * BLOCK * COLS : (block + 1) * BLOCK * COLS, :] = convolved(
-            first, 2, block * BLOCK, True
+            first, held_rest.at[1], block * BLOCK, True
         ).reshape(BLOCK * COLS, C)
 
     lane_ok = iota((TILE, LANES), 1) < BINS
@@ -247,7 +269,7 @@
     lifted = tn_dot(share_out[...], feat_out[...])
     lifted_out[...] = lifted
     note_out[0:WIN] = lifted.astype(BF16).reshape(WIN, BR, C)
-    odd = lax.rem(me_ref[0], 2)
+    copies[2].wait()
 
     @pl.when(odd == 1)
     def _():
@@ -271,10 +293,15 @@
             jax.ShapeDtypeStruct((2, BR, C), BF16),
             jax.ShapeDtypeStruct((total, LANES), F32),
             jax.ShapeDtypeStruct((total, LANES), F32),
+            jax.ShapeDtypeStruct((9, C + CL, C), BF16),
         ),
-        in_specs=[whole(pltpu.SMEM)] + [whole()] * 8,
-        out_specs=(whole(),) * 8,
-        scratch_shapes=[pltpu.VMEM((ROWS + 2, WIDE, C), BF16)],
+        in_specs=[whole(pltpu.SMEM)] + [whole()] * 8 + [whole(pltpu.HBM)] * 2,
+        out_specs=(whole(),) * 9,
+        scratch_shapes=[
+            pltpu.VMEM((ROWS + 2, WIDE, C), BF16),
+            pltpu.VMEM((LAYERS - 1, 9, C, C), BF16),
+            pltpu.SemaphoreType.DMA((3,)),
+        ],
         input_output_aliases={1: 0},
         compiler_params=pltpu.CompilerParams(vmem_limit_bytes=32 * 2**20),
         name="front",
@@ -421,11 +448,6 @@
     )(*operands)
 
 
-def shifted(block, distance):
-    count = lax.axis_size(AXES)
-    return lax.ppermute(block, AXES, [((i - distance) % count, i) for i in range(count)])
-
-
 def swapped(block, odd_step):
     count = lax.axis_size(AXES)
     route = [(i, (i + odd_step if i % 2 else i - odd_step) % count) for i in range(count)]
@@ -439,20 +461,24 @@
     me = lax.axis_index(AXES).astype(jnp.int32)
     odd = me % 2 == 1
     me = me.reshape(1)
-    from_right = shifted(image_feats[:, 0:HALO], -1)
-    from_left = shifted(image_feats[:, COLS - HALO :], 1)
-    padded, held, merge_held, spread, depth_pad, masks, slots, side = prepare(
+    left_edge = image_feats[:, 0:HALO]
+    right_edge = image_feats[:, COLS - HALO :]
+    beside = swapped(jnp.where(odd, left_edge, right_edge), -1)
+    across = swapped(jnp.where(odd, right_edge, left_edge), 1)
+    pinned = lambda value: pltpu.with_memory_space_constraint(value, pltpu.HBM)
+    padded, held, spread, depth_pad, masks, slots, side = prepare(
         me,
         *[
-            pltpu.with_memory_space_constraint(value, pltpu.HBM)
+            pinned(value)
             for value in (
-                image_feats, cam_weights, merge_weight, depth_weight.T, ray_bins, pillar_sums,
+                image_feats, cam_weights, depth_weight.T, ray_bins, pillar_sums,
                 pillar_counts.T, lidar_weight, out_cotangent,
             )
         ],
     )
-    _, feat, share, lifted, note, far, probs, gain = front(
-        me, padded, from_right, from_left, held, depth_pad, spread, masks, side
+    _, feat, share, lifted, note, far, probs, gain, merge_held = front(
+        me, padded, across, beside, held, depth_pad, spread, masks, side,
+        pinned(cam_weights), pinned(merge_weight),
     )
     partner = swapped(note, -1)
     far_got = swapped(far, 3)

time: 56.5 us -> 51.8 us (0.917)
  the two profiles are of different devices: /device:TPU:0 before, /device:TPU:4 now
where the time goes in v3:
time: 51.8 us; the launch traced here: 51.7 us
  starting transfers between devices  22 us (42%)
  Pallas kernels  20 us (39%)
  waiting for transfers between devices  7.78 us (15%)
  other arithmetic  1.13 us (2%)
  between operations  0.74 us (1%)
    ppermute x6, starting transfers between devices, swapped(): return lax.ppermute(block, AXES, route)  22 us
    pallas_call x1, Pallas kernels, front(): pl.pallas_call(front_kernel, out_shape=(jax.ShapeDtypeStruct((ROWS + 2, W...  12.5 us
    ppermute x6, waiting for transfers between devices, swapped(): return lax.ppermute(block, AXES, route)  7.78 us
    pallas_call x1, Pallas kernels, back(): pl.pallas_call(back_kernel, out_shape=(jax.ShapeDtypeStruct((BR, BA, C),...  5.69 us
    pallas_call x1, Pallas kernels, prepare(): pl.pallas_call(prepare_kernel, out_shape=(jax.ShapeDtypeStruct((ROWS + 2,...  1.85 us
    select_n x1, other arithmetic, local(): beside = swapped(jnp.where(odd, left_edge, right_edge), -1)  1.05 us
  transfers between devices with their start and end apart: 6, of which 4 were waited for; matrix products, arithmetic and copies ran while one was open for 0% of the time, Pallas kernels for 4%

profile of v3, /device:TPU:4, one launch (start us, length us, event | category | flops | bytes accessed | tf_op | source)
XLA Modules:
  0.0 51.7 jit_solution(11957357148766653940)
XLA Ops:
  0.6 1.0 %broadcast_select_fusion = (bf16[32,4,256]{2,1,0:T(4,128)(2,1)S(1)}, bf16[32,4,256]{2,1,0:T(4,128)(2,1)S(1)}) fusion(pred[]{:T(512)S(6)} %eq.5, bf16[32,64,256]{2,1,0:T(8,128)(2,1)} %image.1), kind=kLoop, calls=%fused_computation.3 | loop fusion | flops 65536 | bytes 262145 | tf_op jit(solution)/shard_map/jit(_where)/select_n | solution.py:466
  1.7 0.1 collective-permute-start.1
  1.8 2.3 %collective-permute-start = (bf16[32,4,256]{2,1,0:T(4,128)(2,1)S(1)}, bf16[32,4,256]{2,1,0:T(4,128)(2,1)S(1)}, u32[]{:S(2)}, u32[]{:S(2)}) collective-permute-start(bf16[32,4,256]{2,1,0:T(4,128)(2,1)S(1)} %get-tuple-element.40), channel_id=1, source_target_pairs={{0,255},{1,2},{2,1},{3,4},{4,3},{5,6},{6,5},{7,8},{8,7},{9,10},{10... | collective-permute-start | bytes 196616 | tf_op jit(solution)/shard_map/ppermute | solution.py:454
  4.1 1.8 %prepare.1 = (bf16[34,72,256]{2,1,0:T(8,128)(2,1)S(1)}, bf16[9,256,256]{2,1,0:T(8,128)(2,1)S(1)}, bf16[1536,256]{1,0:T(8,128)(2,1)S(1)}, bf16[128,256]{1,0:T(8,1...) custom-call(s32[1]{0:T(128)} %bitcast.me_ref, ...), custom_call_target="tpu_custom_call" | custom-call | flops 100000000 | bytes 8388608 | tf_op jit(solution)/shard_map/prepare/pallas_call | solution.py:140
  6.0 0.0 collective-permute-done.1.beside
  6.0 1.1 %collective-permute-done.crossed = bf16[32,4,256]{2,1,0:T(4,128)(2,1)S(1)} collective-permute-done((bf16[32,4,256]{2,1,0:T(4,128)(2,1)S(1)}, bf16[32,4,256]{2,1,0:T(4,128)(2,1)S(1)}, u32[]{:S(2)}, u32[]{:S(2)}) %collective-permute-start) | collective-permute-done | bytes 65568 | tf_op jit(solution)/shard_map/ppermute | solution.py:454
  7.1 12.5 %front.1 = (bf16[34,72,256]{2,1,0:T(8,128)(2,1)S(1)}, bf16[2048,256]{1,0:T(8,128)(2,1)S(1)}, bf16[2048,256]{1,0:T(8,128)(2,1)S(1)}, f32[256,256]{1,0:T(8,128)S(1...) custom-call(s32[1]{0:T(128)} %bitcast.me_ref, ...), custom_call_target="tpu_custom_call", output_to_operand_aliasing={{0}: (1, {})} | custom-call | tf_op jit(solution)/shard_map/front/pallas_call | solution.py:285
  19.6 1.4 %collective-permute-start.2 = (bf16[22,16,256]{2,1,0:T(8,128)(2,1)S(1)}, bf16[22,16,256]{2,1,0:T(8,128)(2,1)S(1)}, u32[]{:S(2)}, u32[]{:S(2)}) collective-permute-start(bf16[22,16,256]{2,1,0:T(8,128)(2,1)S(1)} %get-tuple-element.28.note), channel_id=1, source_target_pairs={{0,1},{1,0},{2,3},{3,2},{4,5},{5,4},{6,7},{7,6},{8,9},{9,8},{10,11... | collective-permute-start | bytes 540680 | tf_op jit(solution)/shard_map/ppermute | solution.py:454
  21.0 1.0 %collective-permute-done.2.partner = bf16[22,16,256]{2,1,0:T(8,128)(2,1)S(1)} collective-permute-done((bf16[22,16,256]{2,1,0:T(8,128)(2,1)S(1)}, bf16[22,16,256]{2,1,0:T(8,128)(2,1)S(1)}, u32[]{:S(2)}, u32[]{:S(2)}) %collective-permute-start.2) | collective-permute-done | bytes 180256 | tf_op jit(solution)/shard_map/ppermute | solution.py:454
  22.1 6.7 %collective-permute-start.3 = (bf16[18,16,256]{2,1,0:T(8,128)(2,1)S(1)}, bf16[18,16,256]{2,1,0:T(8,128)(2,1)S(1)}, u32[]{:S(2)}, u32[]{:S(2)}) collective-permute-start(bf16[18,16,256]{2,1,0:T(8,128)(2,1)S(1)} %constant_dynamic-update-slice_fusion), channel_id=1, source_target_pairs={{0,255},{1,2},{2,1},{3,4},{4,3},{5,6},{6,5},{7,8},{8,7},{9,10},{10... | collective-permute-start | bytes 442376 | tf_op jit(solution)/shard_map/ppermute | solution.py:454
  28.8 4.2 %collective-permute-done.3.crossed = bf16[18,16,256]{2,1,0:T(8,128)(2,1)S(1)} collective-permute-done((bf16[18,16,256]{2,1,0:T(8,128)(2,1)S(1)}, bf16[18,16,256]{2,1,0:T(8,128)(2,1)S(1)}, u32[]{:S(2)}, u32[]{:S(2)}) %collective-permute-start.3) | collective-permute-done | bytes 147488 | tf_op jit(solution)/shard_map/ppermute | solution.py:454
  33.1 0.1 collective-permute-start.4
  33.2 11.4 %collective-permute-start.5 = (bf16[2,16,256]{2,1,0:T(8,128)(2,1)S(1)}, bf16[2,16,256]{2,1,0:T(8,128)(2,1)S(1)}, u32[]{:S(2)}, u32[]{:S(2)}) collective-permute-start(bf16[2,16,256]{2,1,0:T(8,128)(2,1)S(1)} %get-tuple-element.29), channel_id=1, source_target_pairs={{0,253},{1,4},{2,255},{3,6},{4,1},{5,8},{6,3},{7,10},{8,5},{9,12},... | collective-permute-start | bytes 49160 | tf_op jit(solution)/shard_map/ppermute | solution.py:454
  44.6 1.4 %collective-permute-done.5.far = bf16[2,16,256]{2,1,0:T(8,128)(2,1)S(1)} collective-permute-done((bf16[2,16,256]{2,1,0:T(8,128)(2,1)S(1)}, bf16[2,16,256]{2,1,0:T(8,128)(2,1)S(1)}, u32[]{:S(2)}, u32[]{:S(2)}) %collective-permute-start.5) | collective-permute-done | bytes 16416 | tf_op jit(solution)/shard_map/ppermute | solution.py:454
  46.0 0.0 collective-permute-done.4.relayed
  46.0 5.7 %back.1 = (bf16[16,4,256]{2,1,0:T(4,128)(2,1)}, bf16[32,64,256]{2,1,0:T(8,128)(2,1)}, bf16[64,128]{1,0:T(8,128)(2,1)}) custom-call(s32[1]{0:T(128)} %bitcast.me_ref, f32[256,256]{1,0:T(8,128)S(1)} %get-tuple-element.27.lifted, bf16[22,16,256]{2,1,0:T(8,128)(2,1)S(1)} %get-tuple-element.28.note, bf16[22,16,256]{2,1,0:T(8,128)(2,1)S(1)} %collective-permute-done.2.partner, ...), custom_call_target="tpu_custom_call" | custom-call | tf_op jit(solution)/shard_map/back/pallas_call | solution.py:430
  (10 shorter events, 0.1 us)
Async XLA Ops:
  1.7 4.3 %collective-permute-start.1 = (bf16[32,4,256]{2,1,0:T(4,128)(2,1)S(1)}, bf16[32,4,256]{2,1,0:T(4,128)(2,1)S(1)}, u32[]{:S(2)}, u32[]{:S(2)}) collective-permute-start(bf16[32,4,256]{2,1,0:T(4,128)(2,1)S(1)} %get-tuple-element.39), channel_id=1, source_target_pairs={{0,1},{1,0},{2,3},{3,2},{4,5},{5,4},{6,7},{7,6},{8,9},{9,8},{10,11... | collective-permute-start | bytes 196616 | tf_op jit(solution)/shard_map/ppermute | solution.py:454
  1.8 5.3 %collective-permute-start = (bf16[32,4,256]{2,1,0:T(4,128)(2,1)S(1)}, bf16[32,4,256]{2,1,0:T(4,128)(2,1)S(1)}, u32[]{:S(2)}, u32[]{:S(2)}) collective-permute-start(bf16[32,4,256]{2,1,0:T(4,128)(2,1)S(1)} %get-tuple-element.40), channel_id=1, source_target_pairs={{0,255},{1,2},{2,1},{3,4},{4,3},{5,6},{6,5},{7,8},{8,7},{9,10},{10... | collective-permute-start | bytes 196616 | tf_op jit(solution)/shard_map/ppermute | solution.py:454
  19.6 2.4 %collective-permute-start.2 = (bf16[22,16,256]{2,1,0:T(8,128)(2,1)S(1)}, bf16[22,16,256]{2,1,0:T(8,128)(2,1)S(1)}, u32[]{:S(2)}, u32[]{:S(2)}) collective-permute-start(bf16[22,16,256]{2,1,0:T(8,128)(2,1)S(1)} %get-tuple-element.28.note), channel_id=1, source_target_pairs={{0,1},{1,0},{2,3},{3,2},{4,5},{5,4},{6,7},{7,6},{8,9},{9,8},{10,11... | collective-permute-start | bytes 540680 | tf_op jit(solution)/shard_map/ppermute | solution.py:454
  22.1 10.9 %collective-permute-start.3 = (bf16[18,16,256]{2,1,0:T(8,128)(2,1)S(1)}, bf16[18,16,256]{2,1,0:T(8,128)(2,1)S(1)}, u32[]{:S(2)}, u32[]{:S(2)}) collective-permute-start(bf16[18,16,256]{2,1,0:T(8,128)(2,1)S(1)} %constant_dynamic-update-slice_fusion), channel_id=1, source_target_pairs={{0,255},{1,2},{2,1},{3,4},{4,3},{5,6},{6,5},{7,8},{8,7},{9,10},{10... | collective-permute-start | bytes 442376 | tf_op jit(solution)/shard_map/ppermute | solution.py:454
  33.1 12.9 %collective-permute-start.4 = (bf16[8,16,256]{2,1,0:T(8,128)(2,1)S(1)}, bf16[8,16,256]{2,1,0:T(8,128)(2,1)S(1)}, u32[]{:S(2)}, u32[]{:S(2)}) collective-permute-start(bf16[8,16,256]{2,1,0:T(8,128)(2,1)S(1)} %pad_maximum_fusion), channel_id=1, source_target_pairs={{0,1},{1,0},{2,3},{3,2},{4,5},{5,4},{6,7},{7,6},{8,9},{9,8},{10,11... | collective-permute-start | bytes 196616 | tf_op jit(solution)/shard_map/ppermute | solution.py:454
  33.2 12.8 %collective-permute-start.5 = (bf16[2,16,256]{2,1,0:T(8,128)(2,1)S(1)}, bf16[2,16,256]{2,1,0:T(8,128)(2,1)S(1)}, u32[]{:S(2)}, u32[]{:S(2)}) collective-permute-start(bf16[2,16,256]{2,1,0:T(8,128)(2,1)S(1)} %get-tuple-element.29), channel_id=1, source_target_pairs={{0,253},{1,4},{2,255},{3,6},{4,1},{5,8},{6,3},{7,10},{8,5},{9,12},... | collective-permute-start | bytes 49160 | tf_op jit(solution)/shard_map/ppermute | solution.py:454

commit v4 on v3

--- a/solution.py
+++ b/solution.py
@@ -169,7 +169,8 @@
 def front_kernel(
     me_ref, padded_in, crossed, beside, held_first, depth_pad, spread, masks, side,
     weights, merging,
-    first, feat_out, share_out, lifted_out, note_out, far_out, probs_out, gain_out, merge_held,
+    first, feat_out, share_out, lifted_out, beside_out, across_out, edge_out, probs_out,
+    gain_out, merge_held,
     second, held_rest, sems,
 ):
     copies = [
@@ -196,7 +197,6 @@
     def _():
         put_halo(beside, crossed)
 
-    note_out[WIN : WIN + 6] = side[...]
 
     def convolved(source, held, top, narrow):
         lhs = jnp.concatenate(
@@ -268,16 +268,27 @@
 
     lifted = tn_dot(share_out[...], feat_out[...])
     lifted_out[...] = lifted
-    note_out[0:WIN] = lifted.astype(BF16).reshape(WIN, BR, C)
     copies[2].wait()
+    low = lifted[2 * BR : 8 * BR].reshape(6, BR, C)
+    high = lifted[8 * BR : 14 * BR].reshape(6, BR, C)
 
     @pl.when(odd == 1)
     def _():
-        far_out[...] = note_out[12:14]
+        beside_out[0:6] = low.astype(BF16)
+        beside_out[6] = side[0]
+        beside_out[7] = side[BA]
+        across_out[...] = high
+        edge_out[0] = side[BA - 1]
+        edge_out[1] = side[BA + 1]
 
     @pl.when(odd == 0)
     def _():
-        far_out[...] = note_out[2:4]
+        beside_out[0:6] = high.astype(BF16)
+        beside_out[6] = side[BA - 1]
+        beside_out[7] = side[BA + 1]
+        across_out[...] = low
+        edge_out[0] = side[0]
+        edge_out[1] = side[BA]
 
 
 def front(*operands):
@@ -289,14 +300,15 @@
             jax.ShapeDtypeStruct((total, C), BF16),
             jax.ShapeDtypeStruct((total, WIN * BR), BF16),
             jax.ShapeDtypeStruct((WIN * BR, C), F32),
-            jax.ShapeDtypeStruct((WIN + 6, BR, C), BF16),
+            jax.ShapeDtypeStruct((8, BR, C), BF16),
+            jax.ShapeDtypeStruct((6, BR, C), F32),
             jax.ShapeDtypeStruct((2, BR, C), BF16),
             jax.ShapeDtypeStruct((total, LANES), F32),
             jax.ShapeDtypeStruct((total, LANES), F32),
             jax.ShapeDtypeStruct((9, C + CL, C), BF16),
         ),
         in_specs=[whole(pltpu.SMEM)] + [whole()] * 8 + [whole(pltpu.HBM)] * 2,
-        out_specs=(whole(),) * 9,
+        out_specs=(whole(),) * 10,
         scratch_shapes=[
             pltpu.VMEM((ROWS + 2, WIDE, C), BF16),
             pltpu.VMEM((LAYERS - 1, 9, C, C), BF16),
@@ -317,54 +329,39 @@
     return jnp.where(keep, moved, 0.0)
 
 
-def back_kernel(
-    me_ref, lifted, note, partner, crossed, relayed, far, weights, feat, share, probs, gain,
-    slots, depth_pad, spread,
-    merged_out, cam_out, lid_out,
-    cam, cot, lid, table, wide_table,
+def middle_kernel(
+    me_ref, lifted, side, partner, crossed, relayed, weights,
+    merged_out, lid_out, table_out,
+    cam, cot, lid,
 ):
-
     def put_lid(at, packed):
         lid[at] = packed[:, 0:CL]
         lid[at + 1] = packed[:, CL:]
 
-    cam[...] = lifted[...].reshape(WIN, BR, C)
-    cot[REACH : REACH + BA] = note[WIN : WIN + BA]
-    put_lid(REACH, note[WIN + BA])
-    put_lid(REACH + 2, note[WIN + BA + 1])
-    cot[0] = jnp.zeros((BR, C), BF16)
-    cot[WIN - 1] = jnp.zeros((BR, C), BF16)
+    cam[...] = lifted[4 * BR : 12 * BR].reshape(2 * BA, BR, C)
+    cot[1 : 1 + BA] = side[0:BA]
+    put_lid(2, side[BA])
+    put_lid(4, side[BA + 1])
     odd = lax.rem(me_ref[0], 2)
 
-    def gather(low_side):
-        near = 10 if low_side else 2
-        other = 2 if low_side else 10
-        cam[6:16] += (partner[2:12] if low_side else crossed[0:10]).astype(F32)
-        cam[0:10] += (crossed[0:10] if low_side else partner[4:14]).astype(F32)
-        start = 10 if low_side else 0
-        cam[start : start + 6] += relayed[0:6].astype(F32)
-        edge = 0 if low_side else 14
-        cam[edge : edge + 2] += far[...].astype(F32)
-        cot[near : near + 4] = partner[WIN : WIN + 4]
-        cot[other : other + 4] = crossed[10:14]
-        cot[1 if low_side else 14] = crossed[14]
-        cot[14 if low_side else 1] = relayed[6]
-        put_lid(near, partner[WIN + 4])
-        put_lid(near + 2, partner[WIN + 5])
-        put_lid(other, crossed[15])
-        put_lid(other + 2, crossed[16])
-        put_lid(0 if low_side else 14, crossed[17])
-        put_lid(14 if low_side else 0, relayed[7])
+    def gather(left, right, at):
+        cam[2:8] += right[0:6].astype(F32)
+        cam[0:6] += left[0:6].astype(F32)
+        cam[at : at + 2] += relayed[...].astype(F32)
+        cot[0] = left[6]
+        cot[BA + 1] = right[6]
+        put_lid(0, left[7])
+        put_lid(6, right[7])
 
     @pl.when(odd == 0)
     def _():
-        gather(True)
+        gather(crossed, partner, 6)
 
     @pl.when(odd == 1)
     def _():
-        gather(False)
-
-    span = WIN - 2
+        gather(partner, crossed, 0)
+
+    span = BA + 2
     merged_in = jnp.concatenate([cam[...].astype(BF16), lid[...]], axis=2)
     joined = jnp.concatenate(
         [merged_in[right : right + span].reshape(span * BR, C + CL) for right in range(3)],
@@ -378,7 +375,7 @@
     gate = 1.0 / (1.0 + jnp.exp(-pre))
     merged = (pre * gate).astype(BF16)
     grad_pre = (
-        cot[1 : WIN - 1].astype(F32) * (gate * (1.0 + pre * (1.0 - gate)))
+        cot[...].astype(F32) * (gate * (1.0 + pre * (1.0 - gate)))
     ).astype(BF16)
     inner = span - 2
     total = None
@@ -392,18 +389,63 @@
             part = piece if part is None else part + piece
         part = along_cycles(part.reshape(inner, BR, C + CL), down - 1)
         total = part if total is None else total + part
-    table[0 : 2 * BR, :] = jnp.zeros((2 * BR, C), BF16)
-    table[(WIN - 2) * BR :, :] = jnp.zeros((2 * BR, C), BF16)
-    table[2 * BR : (WIN - 2) * BR, :] = total[:, :, 0:C].astype(BF16).reshape(inner * BR, C)
+    table_out[...] = total[:, :, 0:C].astype(BF16)
     order = iota((BR * BA, BR * BA), 0)
     source = iota((BR * BA, BR * BA), 1)
     swap = ((order % BA) * BR + order // BA == source).astype(F32).astype(BF16)
-    own = merged[REACH - 1 : REACH - 1 + BA].reshape(BA * BR, C)
+    own = merged[1 : 1 + BA].reshape(BA * BR, C)
     turned = dot(swap, own)
     for cycle in range(BR):
         merged_out[cycle] = turned[BA * cycle : BA * (cycle + 1)].astype(BF16)
-    own_lid = total[REACH - 2 : REACH - 2 + BA, :, C:].astype(BF16).reshape(BA * BR, CL)
+    own_lid = total[:, :, C:].astype(BF16).reshape(BA * BR, CL)
     lid_out[...] = dot(swap, own_lid).astype(BF16)
+
+
+def middle(*operands):
+    return pl.pallas_call(
+        middle_kernel,
+        out_shape=(
+            jax.ShapeDtypeStruct((BR, BA, C), BF16),
+            jax.ShapeDtypeStruct((BR * BA, CL), BF16),
+            jax.ShapeDtypeStruct((BA, BR, C), BF16),
+        ),
+        in_specs=[whole(pltpu.SMEM)] + [whole()] * 6,
+        out_specs=(whole(),) * 3,
+        scratch_shapes=[
+            pltpu.VMEM((2 * BA, BR, C), F32),
+            pltpu.VMEM((BA + 2, BR, C), BF16),
+            pltpu.VMEM((2 * BA, BR, CL), BF16),
+        ],
+        compiler_params=pltpu.CompilerParams(vmem_limit_bytes=24 * 2**20),
+        name="middle",
+    )(*operands)
+
+
+def back_kernel(
+    me_ref, own_table, partner_table, across_table, feat, share, probs, gain, slots, depth_pad,
+    spread,
+    cam_out,
+    table, wide_table,
+):
+    odd = lax.rem(me_ref[0], 2)
+    table[0 : 2 * BR, :] = jnp.zeros((2 * BR, C), BF16)
+    table[(WIN - 2) * BR :, :] = jnp.zeros((2 * BR, C), BF16)
+
+    def put(at, value):
+        table[at * BR : (at + BA) * BR, :] = value[...].reshape(BA * BR, C)
+
+    put(REACH, own_table)
+
+    @pl.when(odd == 0)
+    def _():
+        put(REACH - BA, across_table)
+        put(REACH + BA, partner_table)
+
+    @pl.when(odd == 1)
+    def _():
+        put(REACH - BA, partner_table)
+        put(REACH + BA, across_table)
+
     wide_table[...] = dot(spread[...], table[...]).astype(BF16)
 
     @pl.loop(0, ROWS // TALL_H, unroll=True)
@@ -429,17 +471,10 @@
 def back(*operands):
     return pl.pallas_call(
         back_kernel,
-        out_shape=(
-            jax.ShapeDtypeStruct((BR, BA, C), BF16),
-            jax.ShapeDtypeStruct((ROWS, COLS, C), BF16),
-            jax.ShapeDtypeStruct((BR * BA, CL), BF16),
-        ),
-        in_specs=[whole(pltpu.SMEM)] + [whole()] * 14,
-        out_specs=(whole(),) * 3,
+        out_shape=jax.ShapeDtypeStruct((ROWS, COLS, C), BF16),
+        in_specs=[whole(pltpu.SMEM)] + [whole()] * 10,
+        out_specs=whole(),
         scratch_shapes=[
-            pltpu.VMEM((WIN, BR, C), F32),
-            pltpu.VMEM((WIN, BR, C), BF16),
-            pltpu.VMEM((WIN, BR, CL), BF16),
             pltpu.VMEM((WIN * BR, C), BF16),
             pltpu.VMEM((SLOTS * LANES, C), BF16),
         ],
@@ -466,7 +501,7 @@
     beside = swapped(jnp.where(odd, left_edge, right_edge), -1)
     across = swapped(jnp.where(odd, right_edge, left_edge), 1)
     pinned = lambda value: pltpu.with_memory_space_constraint(value, pltpu.HBM)
-    padded, held, spread, depth_pad, masks, slots, side = prepare(
+    image_held, held, spread, depth_pad, masks, slots, side = prepare(
         me,
         *[
             pinned(value)
@@ -476,40 +511,28 @@
             )
         ],
     )
-    _, feat, share, lifted, note, far, probs, gain, merge_held = front(
-        me, padded, across, beside, held, depth_pad, spread, masks, side,
+    _, feat, share, lifted, aside, sums, edge, probs, gain, merge_held = front(
+        me, image_held, across, beside, held, depth_pad, spread, masks, side,
         pinned(cam_weights), pinned(merge_weight),
     )
-    partner = swapped(note, -1)
-    far_got = swapped(far, 3)
-    wide = lambda a: a.astype(F32)
+    partner = swapped(aside, -1)
     four = jnp.zeros((4, BR, C), F32)
-    mine = lifted.reshape(WIN, BR, C)
-    rise = mine[2:12] + jnp.concatenate([four, wide(partner[2:8])], 0)
-    fall = mine[4:14] + jnp.concatenate([wide(partner[8:14]), four], 0)
-    crossing = jnp.concatenate(
-        [
-            jnp.where(odd, fall, rise).astype(BF16),
-            note[16:20],
-            jnp.where(odd, partner[19:20], partner[16:17]),
-            note[20:22],
-            jnp.where(odd, partner[21:22], partner[20:21]),
-        ],
-        axis=0,
-    )
-    crossed = swapped(crossing, 1)
-    relay = jnp.concatenate(
-        [
-            jnp.where(odd, crossed[0:6], crossed[4:10]),
-            jnp.where(odd, crossed[10:11], crossed[13:14]),
-            jnp.where(odd, crossed[15:16], crossed[16:17]),
-        ],
-        axis=0,
-    )
-    relayed = swapped(relay, -1)
-    merged, cam_grad, lid_grad = back(
-        me, lifted, note, partner, crossed, relayed, far_got, merge_held, feat, share,
-        probs, gain, slots, depth_pad, spread,
+    wide = partner.astype(F32)
+    added = jnp.where(
+        odd,
+        jnp.concatenate([wide[4:6], four], axis=0),
+        jnp.concatenate([four, wide[0:2]], axis=0),
+    )
+    crossed = swapped(jnp.concatenate([(sums + added).astype(BF16), edge], axis=0), 1)
+    relayed = swapped(jnp.where(odd, crossed[0:2], crossed[4:6]), -1)
+    merged, lid_grad, own_table = middle(
+        me, lifted, side, partner, crossed, relayed, merge_held
+    )
+    partner_table = swapped(own_table, -1)
+    across_table = swapped(own_table, 1)
+    cam_grad = back(
+        me, own_table, partner_table, across_table, feat, share, probs, gain, slots,
+        depth_pad, spread,
     )
     return merged, cam_grad, lid_grad.reshape(BR, BA, CL)
 

time: 51.8 us -> 54.4 us (1.050)
  the two profiles are of different devices: /device:TPU:4 before, /device:TPU:1 now
where the time goes in v4:
time: 54.4 us; the launch traced here: 54.3 us
  starting transfers between devices  21.2 us (39%)
  Pallas kernels  20.4 us (38%)
  waiting for transfers between devices  10.8 us (20%)
  other arithmetic  1.08 us (2%)
  between operations  0.7 us (1%)
    ppermute x7, starting transfers between devices, swapped(): return lax.ppermute(block, AXES, route)  21.2 us
    pallas_call x1, Pallas kernels, front(): pl.pallas_call(front_kernel, out_shape=(jax.ShapeDtypeStruct((ROWS + 2, W...  12.5 us
    ppermute x7, waiting for transfers between devices, swapped(): return lax.ppermute(block, AXES, route)  10.8 us
    pallas_call x1, Pallas kernels, back(): pl.pallas_call(back_kernel, out_shape=jax.ShapeDtypeStruct((ROWS, COLS, C...  4.08 us
    pallas_call x1, Pallas kernels, middle(): pl.pallas_call(middle_kernel, out_shape=(jax.ShapeDtypeStruct((BR, BA, C)...  2 us
    pallas_call x1, Pallas kernels, prepare(): pl.pallas_call(prepare_kernel, out_shape=(jax.ShapeDtypeStruct((ROWS + 2,...  1.85 us
  transfers between devices with their start and end apart: 7, of which 5 were waited for; matrix products, arithmetic and copies ran while one was open for 0% of the time, Pallas kernels for 3%

profile of v4, /device:TPU:1, one launch (start us, length us, event | category | flops | bytes accessed | tf_op | source)
XLA Modules:
  0.0 54.3 jit_solution(4542894981856369907)
XLA Ops:
  0.6 1.0 %broadcast_select_fusion = (bf16[32,4,256]{2,1,0:T(4,128)(2,1)S(1)}, bf16[32,4,256]{2,1,0:T(4,128)(2,1)S(1)}) fusion(pred[]{:T(512)S(6)} %eq.5, bf16[32,64,256]{2,1,0:T(8,128)(2,1)} %image.1), kind=kLoop, calls=%fused_computation.2 | loop fusion | flops 65536 | bytes 262145 | tf_op jit(solution)/shard_map/jit(_where)/select_n | solution.py:501
  1.7 3.3 %collective-permute-start.1 = (bf16[32,4,256]{2,1,0:T(4,128)(2,1)S(1)}, bf16[32,4,256]{2,1,0:T(4,128)(2,1)S(1)}, u32[]{:S(2)}, u32[]{:S(2)}) collective-permute-start(bf16[32,4,256]{2,1,0:T(4,128)(2,1)S(1)} %get-tuple-element.41), channel_id=1, source_target_pairs={{0,1},{1,0},{2,3},{3,2},{4,5},{5,4},{6,7},{7,6},{8,9},{9,8},{10,11... | collective-permute-start | bytes 196616 | tf_op jit(solution)/shard_map/ppermute | solution.py:489
  5.0 1.0 %collective-permute-start = (bf16[32,4,256]{2,1,0:T(4,128)(2,1)S(1)}, bf16[32,4,256]{2,1,0:T(4,128)(2,1)S(1)}, u32[]{:S(2)}, u32[]{:S(2)}) collective-permute-start(bf16[32,4,256]{2,1,0:T(4,128)(2,1)S(1)} %get-tuple-element.42), channel_id=1, source_target_pairs={{0,255},{1,2},{2,1},{3,4},{4,3},{5,6},{6,5},{7,8},{8,7},{9,10},{10... | collective-permute-start | bytes 196616 | tf_op jit(solution)/shard_map/ppermute | solution.py:489
  6.0 1.8 %prepare.1 = (bf16[34,72,256]{2,1,0:T(8,128)(2,1)S(1)}, bf16[9,256,256]{2,1,0:T(8,128)(2,1)S(1)}, bf16[1536,256]{1,0:T(8,128)(2,1)S(1)}, bf16[128,256]{1,0:T(8,1...) custom-call(s32[1]{0:T(128)} %bitcast.me_ref, ...), custom_call_target="tpu_custom_call" | custom-call | flops 100000000 | bytes 8388608 | tf_op jit(solution)/shard_map/prepare/pallas_call | solution.py:140
  7.9 0.0 collective-permute-done.1.beside
  7.9 2.3 %collective-permute-done.crossed = bf16[32,4,256]{2,1,0:T(4,128)(2,1)S(1)} collective-permute-done((bf16[32,4,256]{2,1,0:T(4,128)(2,1)S(1)}, bf16[32,4,256]{2,1,0:T(4,128)(2,1)S(1)}, u32[]{:S(2)}, u32[]{:S(2)}) %collective-permute-start) | collective-permute-done | bytes 65568 | tf_op jit(solution)/shard_map/ppermute | solution.py:489
  10.2 12.5 %front.1 = (bf16[34,72,256]{2,1,0:T(8,128)(2,1)S(1)}, bf16[2048,256]{1,0:T(8,128)(2,1)S(1)}, bf16[2048,256]{1,0:T(8,128)(2,1)S(1)}, f32[256,256]{1,0:T(8,128)S(1...) custom-call(s32[1]{0:T(128)} %bitcast.me_ref, ...), custom_call_target="tpu_custom_call", output_to_operand_aliasing={{0}: (1, {})} | custom-call | tf_op jit(solution)/shard_map/front/pallas_call | solution.py:296
  22.7 5.7 %collective-permute-start.2 = (bf16[8,16,256]{2,1,0:T(8,128)(2,1)S(1)}, bf16[8,16,256]{2,1,0:T(8,128)(2,1)S(1)}, u32[]{:S(2)}, u32[]{:S(2)}) collective-permute-start(bf16[8,16,256]{2,1,0:T(8,128)(2,1)S(1)} %get-tuple-element.29), channel_id=1, source_target_pairs={{0,1},{1,0},{2,3},{3,2},{4,5},{5,4},{6,7},{7,6},{8,9},{9,8},{10,11... | collective-permute-start | bytes 196616 | tf_op jit(solution)/shard_map/ppermute | solution.py:489
  28.4 0.9 %collective-permute-done.2.partner = bf16[8,16,256]{2,1,0:T(8,128)(2,1)S(1)} collective-permute-done((bf16[8,16,256]{2,1,0:T(8,128)(2,1)S(1)}, bf16[8,16,256]{2,1,0:T(8,128)(2,1)S(1)}, u32[]{:S(2)}, u32[]{:S(2)}) %collective-permute-start.2) | collective-permute-done | bytes 65568 | tf_op jit(solution)/shard_map/ppermute | solution.py:489
  29.4 0.1 collective-permute-start.3
  29.5 5.9 %collective-permute-done.3.crossed = bf16[8,16,256]{2,1,0:T(8,128)(2,1)S(1)} collective-permute-done((bf16[8,16,256]{2,1,0:T(8,128)(2,1)S(1)}, bf16[8,16,256]{2,1,0:T(8,128)(2,1)S(1)}, u32[]{:S(2)}, u32[]{:S(2)}) %collective-permute-start.3) | collective-permute-done | bytes 65568 | tf_op jit(solution)/shard_map/ppermute | solution.py:489
  35.4 3.6 %collective-permute-start.4 = (bf16[2,16,256]{2,1,0:T(8,128)(2,1)S(1)}, bf16[2,16,256]{2,1,0:T(8,128)(2,1)S(1)}, u32[]{:S(2)}, u32[]{:S(2)}) collective-permute-start(bf16[2,16,256]{2,1,0:T(8,128)(2,1)S(1)} %slice_select_fusion), channel_id=1, source_target_pairs={{0,1},{1,0},{2,3},{3,2},{4,5},{5,4},{6,7},{7,6},{8,9},{9,8},{10,11... | collective-permute-start | bytes 49160 | tf_op jit(solution)/shard_map/ppermute | solution.py:489
  39.0 0.8 %collective-permute-done.4.relayed = bf16[2,16,256]{2,1,0:T(8,128)(2,1)S(1)} collective-permute-done((bf16[2,16,256]{2,1,0:T(8,128)(2,1)S(1)}, bf16[2,16,256]{2,1,0:T(8,128)(2,1)S(1)}, u32[]{:S(2)}, u32[]{:S(2)}) %collective-permute-start.4) | collective-permute-done | bytes 16416 | tf_op jit(solution)/shard_map/ppermute | solution.py:489
  39.8 2.0 %middle.1 = (bf16[16,4,256]{2,1,0:T(4,128)(2,1)}, bf16[64,128]{1,0:T(8,128)(2,1)}, bf16[4,16,256]{2,1,0:T(8,128)(2,1)S(1)}) custom-call(s32[1]{0:T(128)} %bitcast.me_ref, f32[256,256]{1,0:T(8,128)S(1)} %get-tuple-element.28.lifted, bf16[6,16,256]{2,1,0:T(8,128)(2,1)S(1)} %get-tuple-element.27.side, bf16[8,16,256]{2,1,0:T(8,128)(2,1)S(1)} %collective-permute-done.2.partner, ...), custom_call_target="tpu_custom_call" | custom-call | tf_op jit(solution)/shard_map/middle/pallas_call | solution.py:405
  41.8 0.0 collective-permute-start.6
  41.8 7.5 %collective-permute-start.5 = (bf16[4,16,256]{2,1,0:T(8,128)(2,1)S(1)}, bf16[4,16,256]{2,1,0:T(8,128)(2,1)S(1)}, u32[]{:S(2)}, u32[]{:S(2)}) collective-permute-start(bf16[4,16,256]{2,1,0:T(8,128)(2,1)S(1)} %get-tuple-element.34.own_table), channel_id=1, source_target_pairs={{0,1},{1,0},{2,3},{3,2},{4,5},{5,4},{6,7},{7,6},{8,9},{9,8},{10,11... | collective-permute-start | bytes 98312 | tf_op jit(solution)/shard_map/ppermute | solution.py:489
  49.3 0.0 collective-permute-done.6.across_table
  49.3 0.9 %collective-permute-done.5.partner_table = bf16[4,16,256]{2,1,0:T(8,128)(2,1)S(1)} collective-permute-done((bf16[4,16,256]{2,1,0:T(8,128)(2,1)S(1)}, bf16[4,16,256]{2,1,0:T(8,128)(2,1)S(1)}, u32[]{:S(2)}, u32[]{:S(2)}) %collective-permute-start.5) | collective-permute-done | bytes 32800 | tf_op jit(solution)/shard_map/ppermute | solution.py:489
  50.2 4.1 %back.1 = bf16[32,64,256]{2,1,0:T(8,128)(2,1)} custom-call(s32[1]{0:T(128)} %bitcast.me_ref, bf16[4,16,256]{2,1,0:T(8,128)(2,1)S(1)} %get-tuple-element.34.own_table, bf16[4,16,256]{2,1,0:T(8,128)(2,1)S(1)} %collective-permute-done.5.partner_table, bf16[4,16,256]{2,1,0:T(8,128)(2,1)S(1)} %collective-permute-done.6.across_table, ...), custom_call_target="tpu_custom_call" | custom-call | tf_op jit(solution)/shard_map/back/pallas_call | solution.py:472
  (4 shorter events, 0.0 us)
Async XLA Ops:
  1.7 6.2 %collective-permute-start.1 = (bf16[32,4,256]{2,1,0:T(4,128)(2,1)S(1)}, bf16[32,4,256]{2,1,0:T(4,128)(2,1)S(1)}, u32[]{:S(2)}, u32[]{:S(2)}) collective-permute-start(bf16[32,4,256]{2,1,0:T(4,128)(2,1)S(1)} %get-tuple-element.41), channel_id=1, source_target_pairs={{0,1},{1,0},{2,3},{3,2},{4,5},{5,4},{6,7},{7,6},{8,9},{9,8},{10,11... | collective-permute-start | bytes 196616 | tf_op jit(solution)/shard_map/ppermute | solution.py:489
  5.0 5.2 %collective-permute-start = (bf16[32,4,256]{2,1,0:T(4,128)(2,1)S(1)}, bf16[32,4,256]{2,1,0:T(4,128)(2,1)S(1)}, u32[]{:S(2)}, u32[]{:S(2)}) collective-permute-start(bf16[32,4,256]{2,1,0:T(4,128)(2,1)S(1)} %get-tuple-element.42), channel_id=1, source_target_pairs={{0,255},{1,2},{2,1},{3,4},{4,3},{5,6},{6,5},{7,8},{8,7},{9,10},{10... | collective-permute-start | bytes 196616 | tf_op jit(solution)/shard_map/ppermute | solution.py:489
  22.7 6.6 %collective-permute-start.2 = (bf16[8,16,256]{2,1,0:T(8,128)(2,1)S(1)}, bf16[8,16,256]{2,1,0:T(8,128)(2,1)S(1)}, u32[]{:S(2)}, u32[]{:S(2)}) collective-permute-start(bf16[8,16,256]{2,1,0:T(8,128)(2,1)S(1)} %get-tuple-element.29), channel_id=1, source_target_pairs={{0,1},{1,0},{2,3},{3,2},{4,5},{5,4},{6,7},{7,6},{8,9},{9,8},{10,11... | collective-permute-start | bytes 196616 | tf_op jit(solution)/shard_map/ppermute | solution.py:489
  29.4 6.0 %collective-permute-start.3 = (bf16[8,16,256]{2,1,0:T(8,128)(2,1)S(1)}, bf16[8,16,256]{2,1,0:T(8,128)(2,1)S(1)}, u32[]{:S(2)}, u32[]{:S(2)}) collective-permute-start(bf16[8,16,256]{2,1,0:T(8,128)(2,1)S(1)} %pad_maximum_fusion), channel_id=1, source_target_pairs={{0,255},{1,2},{2,1},{3,4},{4,3},{5,6},{6,5},{7,8},{8,7},{9,10},{10... | collective-permute-start | bytes 196616 | tf_op jit(solution)/shard_map/ppermute | solution.py:489
  35.4 4.4 %collective-permute-start.4 = (bf16[2,16,256]{2,1,0:T(8,128)(2,1)S(1)}, bf16[2,16,256]{2,1,0:T(8,128)(2,1)S(1)}, u32[]{:S(2)}, u32[]{:S(2)}) collective-permute-start(bf16[2,16,256]{2,1,0:T(8,128)(2,1)S(1)} %slice_select_fusion), channel_id=1, source_target_pairs={{0,1},{1,0},{2,3},{3,2},{4,5},{5,4},{6,7},{7,6},{8,9},{9,8},{10,11... | collective-permute-start | bytes 49160 | tf_op jit(solution)/shard_map/ppermute | solution.py:489
  41.8 7.5 %collective-permute-start.6 = (bf16[4,16,256]{2,1,0:T(8,128)(2,1)S(1)}, bf16[4,16,256]{2,1,0:T(8,128)(2,1)S(1)}, u32[]{:S(2)}, u32[]{:S(2)}) collective-permute-start(bf16[4,16,256]{2,1,0:T(8,128)(2,1)S(1)} %get-tuple-element.34.own_table), channel_id=1, source_target_pairs={{0,255},{1,2},{2,1},{3,4},{4,3},{5,6},{6,5},{7,8},{8,7},{9,10},{10... | collective-permute-start | bytes 98312 | tf_op jit(solution)/shard_map/ppermute | solution.py:489
  41.8 8.4 %collective-permute-start.5 = (bf16[4,16,256]{2,1,0:T(8,128)(2,1)S(1)}, bf16[4,16,256]{2,1,0:T(8,128)(2,1)S(1)}, u32[]{:S(2)}, u32[]{:S(2)}) collective-permute-start(bf16[4,16,256]{2,1,0:T(8,128)(2,1)S(1)} %get-tuple-element.34.own_table), channel_id=1, source_target_pairs={{0,1},{1,0},{2,3},{3,2},{4,5},{5,4},{6,7},{7,6},{8,9},{9,8},{10,11... | collective-permute-start | bytes 98312 | tf_op jit(solution)/shard_map/ppermute | solution.py:489

commit v5 on v3

--- a/solution.py
+++ b/solution.py
@@ -506,6 +506,7 @@
         ],
         axis=0,
     )
+    relay, far_got = lax.optimization_barrier((relay, far_got))
     relayed = swapped(relay, -1)
     merged, cam_grad, lid_grad = back(
         me, lifted, note, partner, crossed, relayed, far_got, merge_held, feat, share,

time: 51.8 us -> 51.3 us (level)
  the two profiles are of different devices: /device:TPU:4 before, /device:TPU:1 now
where the time goes in v5:
time: 51.3 us; the launch traced here: 51.2 us
  Pallas kernels  20 us (39%)
  starting transfers between devices  17.5 us (34%)
  waiting for transfers between devices  11.8 us (23%)
  other arithmetic  1.13 us (2%)
  between operations  0.75 us (1%)
    ppermute x6, starting transfers between devices, swapped(): return lax.ppermute(block, AXES, route)  17.5 us
    pallas_call x1, Pallas kernels, front(): pl.pallas_call(front_kernel, out_shape=(jax.ShapeDtypeStruct((ROWS + 2, W...  12.5 us
    ppermute x6, waiting for transfers between devices, swapped(): return lax.ppermute(block, AXES, route)  11.8 us
    pallas_call x1, Pallas kernels, back(): pl.pallas_call(back_kernel, out_shape=(jax.ShapeDtypeStruct((BR, BA, C),...  5.69 us
    pallas_call x1, Pallas kernels, prepare(): pl.pallas_call(prepare_kernel, out_shape=(jax.ShapeDtypeStruct((ROWS + 2,...  1.85 us
    select_n x1, other arithmetic, local(): beside = swapped(jnp.where(odd, left_edge, right_edge), -1)  1.05 us
  transfers between devices with their start and end apart: 6, of which 4 were waited for; matrix products, arithmetic and copies ran while one was open for 0% of the time, Pallas kernels for 4%

profile of v5, /device:TPU:1, one launch (start us, length us, event | category | flops | bytes accessed | tf_op | source)
XLA Modules:
  0.0 51.2 jit_solution(15420271805353356282)
XLA Ops:
  0.6 1.0 %broadcast_select_fusion = (bf16[32,4,256]{2,1,0:T(4,128)(2,1)S(1)}, bf16[32,4,256]{2,1,0:T(4,128)(2,1)S(1)}) fusion(pred[]{:T(512)S(6)} %eq.5, bf16[32,64,256]{2,1,0:T(8,128)(2,1)} %image.1), kind=kLoop, calls=%fused_computation.3 | loop fusion | flops 65536 | bytes 262145 | tf_op jit(solution)/shard_map/jit(_where)/select_n | solution.py:466
  1.7 3.3 %collective-permute-start.1 = (bf16[32,4,256]{2,1,0:T(4,128)(2,1)S(1)}, bf16[32,4,256]{2,1,0:T(4,128)(2,1)S(1)}, u32[]{:S(2)}, u32[]{:S(2)}) collective-permute-start(bf16[32,4,256]{2,1,0:T(4,128)(2,1)S(1)} %get-tuple-element.43), channel_id=1, source_target_pairs={{0,1},{1,0},{2,3},{3,2},{4,5},{5,4},{6,7},{7,6},{8,9},{9,8},{10,11... | collective-permute-start | bytes 196616 | tf_op jit(solution)/shard_map/ppermute | solution.py:454
  5.0 1.0 %collective-permute-start = (bf16[32,4,256]{2,1,0:T(4,128)(2,1)S(1)}, bf16[32,4,256]{2,1,0:T(4,128)(2,1)S(1)}, u32[]{:S(2)}, u32[]{:S(2)}) collective-permute-start(bf16[32,4,256]{2,1,0:T(4,128)(2,1)S(1)} %get-tuple-element.44), channel_id=1, source_target_pairs={{0,255},{1,2},{2,1},{3,4},{4,3},{5,6},{6,5},{7,8},{8,7},{9,10},{10... | collective-permute-start | bytes 196616 | tf_op jit(solution)/shard_map/ppermute | solution.py:454
  6.0 1.8 %prepare.1 = (bf16[34,72,256]{2,1,0:T(8,128)(2,1)S(1)}, bf16[9,256,256]{2,1,0:T(8,128)(2,1)S(1)}, bf16[1536,256]{1,0:T(8,128)(2,1)S(1)}, bf16[128,256]{1,0:T(8,1...) custom-call(s32[1]{0:T(128)} %bitcast.me_ref, ...), custom_call_target="tpu_custom_call" | custom-call | flops 100000000 | bytes 8388608 | tf_op jit(solution)/shard_map/prepare/pallas_call | solution.py:140
  7.9 0.0 collective-permute-done.1.beside
  7.9 2.3 %collective-permute-done.crossed = bf16[32,4,256]{2,1,0:T(4,128)(2,1)S(1)} collective-permute-done((bf16[32,4,256]{2,1,0:T(4,128)(2,1)S(1)}, bf16[32,4,256]{2,1,0:T(4,128)(2,1)S(1)}, u32[]{:S(2)}, u32[]{:S(2)}) %collective-permute-start) | collective-permute-done | bytes 65568 | tf_op jit(solution)/shard_map/ppermute | solution.py:454
  10.2 12.5 %front.1 = (bf16[34,72,256]{2,1,0:T(8,128)(2,1)S(1)}, bf16[2048,256]{1,0:T(8,128)(2,1)S(1)}, bf16[2048,256]{1,0:T(8,128)(2,1)S(1)}, f32[256,256]{1,0:T(8,128)S(1...) custom-call(s32[1]{0:T(128)} %bitcast.me_ref, ...), custom_call_target="tpu_custom_call", output_to_operand_aliasing={{0}: (1, {})} | custom-call | tf_op jit(solution)/shard_map/front/pallas_call | solution.py:285
  22.7 5.7 %collective-permute-start.2 = (bf16[22,16,256]{2,1,0:T(8,128)(2,1)S(1)}, bf16[22,16,256]{2,1,0:T(8,128)(2,1)S(1)}, u32[]{:S(2)}, u32[]{:S(2)}) collective-permute-start(bf16[22,16,256]{2,1,0:T(8,128)(2,1)S(1)} %get-tuple-element.30.note), channel_id=1, source_target_pairs={{0,1},{1,0},{2,3},{3,2},{4,5},{5,4},{6,7},{7,6},{8,9},{9,8},{10,11... | collective-permute-start | bytes 540680 | tf_op jit(solution)/shard_map/ppermute | solution.py:454
  28.5 1.0 %collective-permute-done.2.partner = bf16[22,16,256]{2,1,0:T(8,128)(2,1)S(1)} collective-permute-done((bf16[22,16,256]{2,1,0:T(8,128)(2,1)S(1)}, bf16[22,16,256]{2,1,0:T(8,128)(2,1)S(1)}, u32[]{:S(2)}, u32[]{:S(2)}) %collective-permute-start.2) | collective-permute-done | bytes 180256 | tf_op jit(solution)/shard_map/ppermute | solution.py:454
  29.6 0.1 collective-permute-start.3
  29.7 0.1 collective-permute-start.4
  29.8 7.5 %collective-permute-done.3.crossed = bf16[18,16,256]{2,1,0:T(8,128)(2,1)S(1)} collective-permute-done((bf16[18,16,256]{2,1,0:T(8,128)(2,1)S(1)}, bf16[18,16,256]{2,1,0:T(8,128)(2,1)S(1)}, u32[]{:S(2)}, u32[]{:S(2)}) %collective-permute-start.3) | collective-permute-done | bytes 147488 | tf_op jit(solution)/shard_map/ppermute | solution.py:454
  37.4 0.0 collective-permute-done.4.far
  37.4 7.2 %collective-permute-start.5 = (bf16[8,16,256]{2,1,0:T(8,128)(2,1)S(1)}, bf16[8,16,256]{2,1,0:T(8,128)(2,1)S(1)}, u32[]{:S(2)}, u32[]{:S(2)}) collective-permute-start(bf16[8,16,256]{2,1,0:T(8,128)(2,1)S(1)} %pad_maximum_fusion), channel_id=1, source_target_pairs={{0,1},{1,0},{2,3},{3,2},{4,5},{5,4},{6,7},{7,6},{8,9},{9,8},{10,11... | collective-permute-start | bytes 196616 | tf_op jit(solution)/shard_map/ppermute | solution.py:454
  44.6 0.9 %collective-permute-done.5.relayed = bf16[8,16,256]{2,1,0:T(8,128)(2,1)S(1)} collective-permute-done((bf16[8,16,256]{2,1,0:T(8,128)(2,1)S(1)}, bf16[8,16,256]{2,1,0:T(8,128)(2,1)S(1)}, u32[]{:S(2)}, u32[]{:S(2)}) %collective-permute-start.5) | collective-permute-done | bytes 65568 | tf_op jit(solution)/shard_map/ppermute | solution.py:454
  45.5 5.7 %back.1 = (bf16[16,4,256]{2,1,0:T(4,128)(2,1)}, bf16[32,64,256]{2,1,0:T(8,128)(2,1)}, bf16[64,128]{1,0:T(8,128)(2,1)}) custom-call(s32[1]{0:T(128)} %bitcast.me_ref, f32[256,256]{1,0:T(8,128)S(1)} %get-tuple-element.29.lifted, bf16[22,16,256]{2,1,0:T(8,128)(2,1)S(1)} %get-tuple-element.30.note, bf16[22,16,256]{2,1,0:T(8,128)(2,1)S(1)} %collective-permute-done.2.partner, ...), custom_call_target="tpu_custom_call" | custom-call | tf_op jit(solution)/shard_map/back/pallas_call | solution.py:430
  (10 shorter events, 0.1 us)
Async XLA Ops:
  1.7 6.2 %collective-permute-start.1 = (bf16[32,4,256]{2,1,0:T(4,128)(2,1)S(1)}, bf16[32,4,256]{2,1,0:T(4,128)(2,1)S(1)}, u32[]{:S(2)}, u32[]{:S(2)}) collective-permute-start(bf16[32,4,256]{2,1,0:T(4,128)(2,1)S(1)} %get-tuple-element.43), channel_id=1, source_target_pairs={{0,1},{1,0},{2,3},{3,2},{4,5},{5,4},{6,7},{7,6},{8,9},{9,8},{10,11... | collective-permute-start | bytes 196616 | tf_op jit(solution)/shard_map/ppermute | solution.py:454
  5.0 5.2 %collective-permute-start = (bf16[32,4,256]{2,1,0:T(4,128)(2,1)S(1)}, bf16[32,4,256]{2,1,0:T(4,128)(2,1)S(1)}, u32[]{:S(2)}, u32[]{:S(2)}) collective-permute-start(bf16[32,4,256]{2,1,0:T(4,128)(2,1)S(1)} %get-tuple-element.44), channel_id=1, source_target_pairs={{0,255},{1,2},{2,1},{3,4},{4,3},{5,6},{6,5},{7,8},{8,7},{9,10},{10... | collective-permute-start | bytes 196616 | tf_op jit(solution)/shard_map/ppermute | solution.py:454
  22.7 6.8 %collective-permute-start.2 = (bf16[22,16,256]{2,1,0:T(8,128)(2,1)S(1)}, bf16[22,16,256]{2,1,0:T(8,128)(2,1)S(1)}, u32[]{:S(2)}, u32[]{:S(2)}) collective-permute-start(bf16[22,16,256]{2,1,0:T(8,128)(2,1)S(1)} %get-tuple-element.30.note), channel_id=1, source_target_pairs={{0,1},{1,0},{2,3},{3,2},{4,5},{5,4},{6,7},{7,6},{8,9},{9,8},{10,11... | collective-permute-start | bytes 540680 | tf_op jit(solution)/shard_map/ppermute | solution.py:454
  29.6 7.7 %collective-permute-start.3 = (bf16[18,16,256]{2,1,0:T(8,128)(2,1)S(1)}, bf16[18,16,256]{2,1,0:T(8,128)(2,1)S(1)}, u32[]{:S(2)}, u32[]{:S(2)}) collective-permute-start(bf16[18,16,256]{2,1,0:T(8,128)(2,1)S(1)} %constant_dynamic-update-slice_fusion), channel_id=1, source_target_pairs={{0,255},{1,2},{2,1},{3,4},{4,3},{5,6},{6,5},{7,8},{8,7},{9,10},{10... | collective-permute-start | bytes 442376 | tf_op jit(solution)/shard_map/ppermute | solution.py:454
  29.7 7.7 %collective-permute-start.4 = (bf16[2,16,256]{2,1,0:T(8,128)(2,1)S(1)}, bf16[2,16,256]{2,1,0:T(8,128)(2,1)S(1)}, u32[]{:S(2)}, u32[]{:S(2)}) collective-permute-start(bf16[2,16,256]{2,1,0:T(8,128)(2,1)S(1)} %get-tuple-element.31), channel_id=1, source_target_pairs={{0,253},{1,4},{2,255},{3,6},{4,1},{5,8},{6,3},{7,10},{8,5},{9,12},... | collective-permute-start | bytes 49160 | tf_op jit(solution)/shard_map/ppermute | solution.py:454
  37.4 8.1 %collective-permute-start.5 = (bf16[8,16,256]{2,1,0:T(8,128)(2,1)S(1)}, bf16[8,16,256]{2,1,0:T(8,128)(2,1)S(1)}, u32[]{:S(2)}, u32[]{:S(2)}) collective-permute-start(bf16[8,16,256]{2,1,0:T(8,128)(2,1)S(1)} %pad_maximum_fusion), channel_id=1, source_target_pairs={{0,1},{1,0},{2,3},{3,2},{4,5},{5,4},{6,7},{7,6},{8,9},{9,8},{10,11... | collective-permute-start | bytes 196616 | tf_op jit(solution)/shard_map/ppermute | solution.py:454

commit v6 on v3

--- a/solution.py
+++ b/solution.py
@@ -481,7 +481,7 @@
         pinned(cam_weights), pinned(merge_weight),
     )
     partner = swapped(note, -1)
-    far_got = swapped(far, 3)
+    far_got = swapped(jnp.concatenate([far, note[0:6]], 0), 3)[0:2]
     wide = lambda a: a.astype(F32)
     four = jnp.zeros((4, BR, C), F32)
     mine = lifted.reshape(WIN, BR, C)

time: 51.8 us -> 47.8 us (0.923)
  the two profiles are of different devices: /device:TPU:4 before, /device:TPU:0 now
where the time goes in v6:
time: 47.8 us; the launch traced here: 47.7 us
  Pallas kernels  20 us (42%)
  starting transfers between devices  17.3 us (36%)
  waiting for transfers between devices  8.45 us (18%)
  other arithmetic  1.14 us (2%)
  between operations  0.76 us (2%)
    ppermute x6, starting transfers between devices, swapped(): return lax.ppermute(block, AXES, route)  17.3 us
    pallas_call x1, Pallas kernels, front(): pl.pallas_call(front_kernel, out_shape=(jax.ShapeDtypeStruct((ROWS + 2, W...  12.5 us
    ppermute x6, waiting for transfers between devices, swapped(): return lax.ppermute(block, AXES, route)  8.45 us
    pallas_call x1, Pallas kernels, back(): pl.pallas_call(back_kernel, out_shape=(jax.ShapeDtypeStruct((BR, BA, C),...  5.69 us
    pallas_call x1, Pallas kernels, prepare(): pl.pallas_call(prepare_kernel, out_shape=(jax.ShapeDtypeStruct((ROWS + 2,...  1.85 us
    select_n x1, other arithmetic, local(): beside = swapped(jnp.where(odd, left_edge, right_edge), -1)  1.05 us
  transfers between devices with their start and end apart: 6, of which 4 were waited for; matrix products, arithmetic and copies ran while one was open for 0% of the time, Pallas kernels for 4%

profile of v6, /device:TPU:0, one launch (start us, length us, event | category | flops | bytes accessed | tf_op | source)
XLA Modules:
  0.0 47.7 jit_solution(9640436958933295764)
XLA Ops:
  0.6 1.0 %broadcast_select_fusion = (bf16[32,4,256]{2,1,0:T(4,128)(2,1)S(1)}, bf16[32,4,256]{2,1,0:T(4,128)(2,1)S(1)}) fusion(pred[]{:T(512)S(6)} %eq.5, bf16[32,64,256]{2,1,0:T(8,128)(2,1)} %image.1), kind=kLoop, calls=%fused_computation.4 | loop fusion | flops 65536 | bytes 262145 | tf_op jit(solution)/shard_map/jit(_where)/select_n | solution.py:466
  1.7 0.1 collective-permute-start.1
  1.8 8.9 %collective-permute-start = (bf16[32,4,256]{2,1,0:T(4,128)(2,1)S(1)}, bf16[32,4,256]{2,1,0:T(4,128)(2,1)S(1)}, u32[]{:S(2)}, u32[]{:S(2)}) collective-permute-start(bf16[32,4,256]{2,1,0:T(4,128)(2,1)S(1)} %get-tuple-element.40), channel_id=1, source_target_pairs={{0,255},{1,2},{2,1},{3,4},{4,3},{5,6},{6,5},{7,8},{8,7},{9,10},{10... | collective-permute-start | bytes 196616 | tf_op jit(solution)/shard_map/ppermute | solution.py:454
  10.7 1.8 %prepare.1 = (bf16[34,72,256]{2,1,0:T(8,128)(2,1)S(1)}, bf16[9,256,256]{2,1,0:T(8,128)(2,1)S(1)}, bf16[1536,256]{1,0:T(8,128)(2,1)S(1)}, bf16[128,256]{1,0:T(8,1...) custom-call(s32[1]{0:T(128)} %bitcast.me_ref, ...), custom_call_target="tpu_custom_call" | custom-call | flops 100000000 | bytes 8388608 | tf_op jit(solution)/shard_map/prepare/pallas_call | solution.py:140
  12.5 0.0 collective-permute-done.1.beside
  12.5 0.1 collective-permute-done.crossed
  12.6 12.5 %front.1 = (bf16[34,72,256]{2,1,0:T(8,128)(2,1)S(1)}, bf16[2048,256]{1,0:T(8,128)(2,1)S(1)}, bf16[2048,256]{1,0:T(8,128)(2,1)S(1)}, f32[256,256]{1,0:T(8,128)S(1...) custom-call(s32[1]{0:T(128)} %bitcast.me_ref, ...), custom_call_target="tpu_custom_call", output_to_operand_aliasing={{0}: (1, {})} | custom-call | tf_op jit(solution)/shard_map/front/pallas_call | solution.py:285
  25.1 0.1 collective-permute-start.2
  25.2 1.4 %collective-permute-done.2.partner = bf16[22,16,256]{2,1,0:T(8,128)(2,1)S(1)} collective-permute-done((bf16[22,16,256]{2,1,0:T(8,128)(2,1)S(1)}, bf16[22,16,256]{2,1,0:T(8,128)(2,1)S(1)}, u32[]{:S(2)}, u32[]{:S(2)}) %collective-permute-start.2) | collective-permute-done | bytes 180256 | tf_op jit(solution)/shard_map/ppermute | solution.py:454
  26.7 7.3 %collective-permute-start.3 = (bf16[18,16,256]{2,1,0:T(8,128)(2,1)S(1)}, bf16[18,16,256]{2,1,0:T(8,128)(2,1)S(1)}, u32[]{:S(2)}, u32[]{:S(2)}) collective-permute-start(bf16[18,16,256]{2,1,0:T(8,128)(2,1)S(1)} %constant_dynamic-update-slice_fusion), channel_id=1, source_target_pairs={{0,255},{1,2},{2,1},{3,4},{4,3},{5,6},{6,5},{7,8},{8,7},{9,10},{10... | collective-permute-start | bytes 442376 | tf_op jit(solution)/shard_map/ppermute | solution.py:454
  34.0 0.7 %collective-permute-start.5 = (bf16[8,16,256]{2,1,0:T(8,128)(2,1)S(1)}, bf16[8,16,256]{2,1,0:T(8,128)(2,1)S(1)}, u32[]{:S(2)}, u32[]{:S(2)}) collective-permute-start(bf16[8,16,256]{2,1,0:T(8,128)(2,1)S(1)} %pad_maximum_fusion.1), channel_id=1, source_target_pairs={{0,253},{1,4},{2,255},{3,6},{4,1},{5,8},{6,3},{7,10},{8,5},{9,12},... | collective-permute-start | bytes 196616 | tf_op jit(solution)/shard_map/ppermute | solution.py:454
  34.7 2.1 %collective-permute-done.3.crossed = bf16[18,16,256]{2,1,0:T(8,128)(2,1)S(1)} collective-permute-done((bf16[18,16,256]{2,1,0:T(8,128)(2,1)S(1)}, bf16[18,16,256]{2,1,0:T(8,128)(2,1)S(1)}, u32[]{:S(2)}, u32[]{:S(2)}) %collective-permute-start.3) | collective-permute-done | bytes 147488 | tf_op jit(solution)/shard_map/ppermute | solution.py:454
  36.9 0.3 collective-permute-start.4
  37.1 4.9 %collective-permute-done.5 = bf16[8,16,256]{2,1,0:T(8,128)(2,1)S(1)} collective-permute-done((bf16[8,16,256]{2,1,0:T(8,128)(2,1)S(1)}, bf16[8,16,256]{2,1,0:T(8,128)(2,1)S(1)}, u32[]{:S(2)}, u32[]{:S(2)}) %collective-permute-start.5) | collective-permute-done | bytes 65568 | tf_op jit(solution)/shard_map/ppermute | solution.py:454
  42.0 0.0 collective-permute-done.4.relayed
  42.0 5.7 %back.1 = (bf16[16,4,256]{2,1,0:T(4,128)(2,1)}, bf16[32,64,256]{2,1,0:T(8,128)(2,1)}, bf16[64,128]{1,0:T(8,128)(2,1)}) custom-call(s32[1]{0:T(128)} %bitcast.me_ref, f32[256,256]{1,0:T(8,128)S(1)} %get-tuple-element.27.lifted, bf16[22,16,256]{2,1,0:T(8,128)(2,1)S(1)} %get-tuple-element.28.note, bf16[22,16,256]{2,1,0:T(8,128)(2,1)S(1)} %collective-permute-done.2.partner, ...), custom_call_target="tpu_custom_call" | custom-call | tf_op jit(solution)/shard_map/back/pallas_call | solution.py:430
  (13 shorter events, 0.1 us)
Async XLA Ops:
  1.7 10.8 %collective-permute-start.1 = (bf16[32,4,256]{2,1,0:T(4,128)(2,1)S(1)}, bf16[32,4,256]{2,1,0:T(4,128)(2,1)S(1)}, u32[]{:S(2)}, u32[]{:S(2)}) collective-permute-start(bf16[32,4,256]{2,1,0:T(4,128)(2,1)S(1)} %get-tuple-element.39), channel_id=1, source_target_pairs={{0,1},{1,0},{2,3},{3,2},{4,5},{5,4},{6,7},{7,6},{8,9},{9,8},{10,11... | collective-permute-start | bytes 196616 | tf_op jit(solution)/shard_map/ppermute | solution.py:454
  1.8 10.8 %collective-permute-start = (bf16[32,4,256]{2,1,0:T(4,128)(2,1)S(1)}, bf16[32,4,256]{2,1,0:T(4,128)(2,1)S(1)}, u32[]{:S(2)}, u32[]{:S(2)}) collective-permute-start(bf16[32,4,256]{2,1,0:T(4,128)(2,1)S(1)} %get-tuple-element.40), channel_id=1, source_target_pairs={{0,255},{1,2},{2,1},{3,4},{4,3},{5,6},{6,5},{7,8},{8,7},{9,10},{10... | collective-permute-start | bytes 196616 | tf_op jit(solution)/shard_map/ppermute | solution.py:454
  25.1 1.5 %collective-permute-start.2 = (bf16[22,16,256]{2,1,0:T(8,128)(2,1)S(1)}, bf16[22,16,256]{2,1,0:T(8,128)(2,1)S(1)}, u32[]{:S(2)}, u32[]{:S(2)}) collective-permute-start(bf16[22,16,256]{2,1,0:T(8,128)(2,1)S(1)} %get-tuple-element.28.note), channel_id=1, source_target_pairs={{0,1},{1,0},{2,3},{3,2},{4,5},{5,4},{6,7},{7,6},{8,9},{9,8},{10,11... | collective-permute-start | bytes 540680 | tf_op jit(solution)/shard_map/ppermute | solution.py:454
  26.7 10.1 %collective-permute-start.3 = (bf16[18,16,256]{2,1,0:T(8,128)(2,1)S(1)}, bf16[18,16,256]{2,1,0:T(8,128)(2,1)S(1)}, u32[]{:S(2)}, u32[]{:S(2)}) collective-permute-start(bf16[18,16,256]{2,1,0:T(8,128)(2,1)S(1)} %constant_dynamic-update-slice_fusion), channel_id=1, source_target_pairs={{0,255},{1,2},{2,1},{3,4},{4,3},{5,6},{6,5},{7,8},{8,7},{9,10},{10... | collective-permute-start | bytes 442376 | tf_op jit(solution)/shard_map/ppermute | solution.py:454
  34.0 8.0 %collective-permute-start.5 = (bf16[8,16,256]{2,1,0:T(8,128)(2,1)S(1)}, bf16[8,16,256]{2,1,0:T(8,128)(2,1)S(1)}, u32[]{:S(2)}, u32[]{:S(2)}) collective-permute-start(bf16[8,16,256]{2,1,0:T(8,128)(2,1)S(1)} %pad_maximum_fusion.1), channel_id=1, source_target_pairs={{0,253},{1,4},{2,255},{3,6},{4,1},{5,8},{6,3},{7,10},{8,5},{9,12},... | collective-permute-start | bytes 196616 | tf_op jit(solution)/shard_map/ppermute | solution.py:454
  36.9 5.2 %collective-permute-start.4 = (bf16[8,16,256]{2,1,0:T(8,128)(2,1)S(1)}, bf16[8,16,256]{2,1,0:T(8,128)(2,1)S(1)}, u32[]{:S(2)}, u32[]{:S(2)}) collective-permute-start(bf16[8,16,256]{2,1,0:T(8,128)(2,1)S(1)} %pad_maximum_fusion), channel_id=1, source_target_pairs={{0,1},{1,0},{2,3},{3,2},{4,5},{5,4},{6,7},{7,6},{8,9},{9,8},{10,11... | collective-permute-start | bytes 196616 | tf_op jit(solution)/shard_map/ppermute | solution.py:454

commit v7 on v6

--- a/solution.py
+++ b/solution.py
@@ -21,9 +21,9 @@
 REACH = 6
 SLOTS = 12
 BLOCK = 16
-TILE_H = 4
+TILE_H = 16
 TILE = TILE_H * COLS
-UNROLL = 4
+UNROLL = 2
 TALL_H = 16
 TALL = TALL_H * COLS
 F32 = jnp.float32

time: 47.8 us -> 46.9 us (0.981)
  Pallas kernels: 20 us -> 19 us
    pallas_call x1, Pallas kernels: 12.5 us -> 11.4 us  [front(): pl.pallas_call(front_kernel, out_shape=(jax.ShapeDtypeStruct((ROWS + 2, W...]
where the time goes in v7:
time: 46.9 us; the launch traced here: 46.8 us
  Pallas kernels  19 us (41%)
  starting transfers between devices  17.3 us (37%)
  waiting for transfers between devices  8.63 us (18%)
  other arithmetic  1.14 us (2%)
  between operations  0.76 us (2%)
    ppermute x6, starting transfers between devices, swapped(): return lax.ppermute(block, AXES, route)  17.3 us
    pallas_call x1, Pallas kernels, front(): pl.pallas_call(front_kernel, out_shape=(jax.ShapeDtypeStruct((ROWS + 2, W...  11.4 us
    ppermute x6, waiting for transfers between devices, swapped(): return lax.ppermute(block, AXES, route)  8.63 us
    pallas_call x1, Pallas kernels, back(): pl.pallas_call(back_kernel, out_shape=(jax.ShapeDtypeStruct((BR, BA, C),...  5.69 us
    pallas_call x1, Pallas kernels, prepare(): pl.pallas_call(prepare_kernel, out_shape=(jax.ShapeDtypeStruct((ROWS + 2,...  1.85 us
    select_n x1, other arithmetic, local(): beside = swapped(jnp.where(odd, left_edge, right_edge), -1)  1.05 us
  transfers between devices with their start and end apart: 6, of which 4 were waited for; matrix products, arithmetic and copies ran while one was open for 0% of the time, Pallas kernels for 4%

profile of v7, /device:TPU:0, one launch (start us, length us, event | category | flops | bytes accessed | tf_op | source)
XLA Modules:
  0.0 46.8 jit_solution(11965808709892845598)
XLA Ops:
  0.6 1.0 %broadcast_select_fusion = (bf16[32,4,256]{2,1,0:T(4,128)(2,1)S(1)}, bf16[32,4,256]{2,1,0:T(4,128)(2,1)S(1)}) fusion(pred[]{:T(512)S(6)} %eq.5, bf16[32,64,256]{2,1,0:T(8,128)(2,1)} %image.1), kind=kLoop, calls=%fused_computation.4 | loop fusion | flops 65536 | bytes 262145 | tf_op jit(solution)/shard_map/jit(_where)/select_n | solution.py:466
  1.7 0.1 collective-permute-start.1
  1.8 8.9 %collective-permute-start = (bf16[32,4,256]{2,1,0:T(4,128)(2,1)S(1)}, bf16[32,4,256]{2,1,0:T(4,128)(2,1)S(1)}, u32[]{:S(2)}, u32[]{:S(2)}) collective-permute-start(bf16[32,4,256]{2,1,0:T(4,128)(2,1)S(1)} %get-tuple-element.40), channel_id=1, source_target_pairs={{0,255},{1,2},{2,1},{3,4},{4,3},{5,6},{6,5},{7,8},{8,7},{9,10},{10... | collective-permute-start | bytes 196616 | tf_op jit(solution)/shard_map/ppermute | solution.py:454
  10.7 1.8 %prepare.1 = (bf16[34,72,256]{2,1,0:T(8,128)(2,1)S(1)}, bf16[9,256,256]{2,1,0:T(8,128)(2,1)S(1)}, bf16[1536,256]{1,0:T(8,128)(2,1)S(1)}, bf16[128,256]{1,0:T(8,1...) custom-call(s32[1]{0:T(128)} %bitcast.me_ref, ...), custom_call_target="tpu_custom_call" | custom-call | flops 100000000 | bytes 8388608 | tf_op jit(solution)/shard_map/prepare/pallas_call | solution.py:140
  12.5 0.0 collective-permute-done.1.beside
  12.5 0.1 collective-permute-done.crossed
  12.6 11.4 %front.1 = (bf16[34,72,256]{2,1,0:T(8,128)(2,1)S(1)}, bf16[2048,256]{1,0:T(8,128)(2,1)S(1)}, bf16[2048,256]{1,0:T(8,128)(2,1)S(1)}, f32[256,256]{1,0:T(8,128)S(1...) custom-call(s32[1]{0:T(128)} %bitcast.me_ref, ...), custom_call_target="tpu_custom_call", output_to_operand_aliasing={{0}: (1, {})} | custom-call | tf_op jit(solution)/shard_map/front/pallas_call | solution.py:285
  24.0 0.1 collective-permute-start.2
  24.2 1.4 %collective-permute-done.2.partner = bf16[22,16,256]{2,1,0:T(8,128)(2,1)S(1)} collective-permute-done((bf16[22,16,256]{2,1,0:T(8,128)(2,1)S(1)}, bf16[22,16,256]{2,1,0:T(8,128)(2,1)S(1)}, u32[]{:S(2)}, u32[]{:S(2)}) %collective-permute-start.2) | collective-permute-done | bytes 180256 | tf_op jit(solution)/shard_map/ppermute | solution.py:454
  25.6 7.3 %collective-permute-start.3 = (bf16[18,16,256]{2,1,0:T(8,128)(2,1)S(1)}, bf16[18,16,256]{2,1,0:T(8,128)(2,1)S(1)}, u32[]{:S(2)}, u32[]{:S(2)}) collective-permute-start(bf16[18,16,256]{2,1,0:T(8,128)(2,1)S(1)} %constant_dynamic-update-slice_fusion), channel_id=1, source_target_pairs={{0,255},{1,2},{2,1},{3,4},{4,3},{5,6},{6,5},{7,8},{8,7},{9,10},{10... | collective-permute-start | bytes 442376 | tf_op jit(solution)/shard_map/ppermute | solution.py:454
  32.9 0.9 %collective-permute-start.5 = (bf16[8,16,256]{2,1,0:T(8,128)(2,1)S(1)}, bf16[8,16,256]{2,1,0:T(8,128)(2,1)S(1)}, u32[]{:S(2)}, u32[]{:S(2)}) collective-permute-start(bf16[8,16,256]{2,1,0:T(8,128)(2,1)S(1)} %pad_maximum_fusion.1), channel_id=1, source_target_pairs={{0,253},{1,4},{2,255},{3,6},{4,1},{5,8},{6,3},{7,10},{8,5},{9,12},... | collective-permute-start | bytes 196616 | tf_op jit(solution)/shard_map/ppermute | solution.py:454
  33.8 1.9 %collective-permute-done.3.crossed = bf16[18,16,256]{2,1,0:T(8,128)(2,1)S(1)} collective-permute-done((bf16[18,16,256]{2,1,0:T(8,128)(2,1)S(1)}, bf16[18,16,256]{2,1,0:T(8,128)(2,1)S(1)}, u32[]{:S(2)}, u32[]{:S(2)}) %collective-permute-start.3) | collective-permute-done | bytes 147488 | tf_op jit(solution)/shard_map/ppermute | solution.py:454
  35.8 0.1 collective-permute-start.4
  35.9 5.2 %collective-permute-done.5 = bf16[8,16,256]{2,1,0:T(8,128)(2,1)S(1)} collective-permute-done((bf16[8,16,256]{2,1,0:T(8,128)(2,1)S(1)}, bf16[8,16,256]{2,1,0:T(8,128)(2,1)S(1)}, u32[]{:S(2)}, u32[]{:S(2)}) %collective-permute-start.5) | collective-permute-done | bytes 65568 | tf_op jit(solution)/shard_map/ppermute | solution.py:454
  41.1 0.0 collective-permute-done.4.relayed
  41.1 5.7 %back.1 = (bf16[16,4,256]{2,1,0:T(4,128)(2,1)}, bf16[32,64,256]{2,1,0:T(8,128)(2,1)}, bf16[64,128]{1,0:T(8,128)(2,1)}) custom-call(s32[1]{0:T(128)} %bitcast.me_ref, f32[256,256]{1,0:T(8,128)S(1)} %get-tuple-element.27.lifted, bf16[22,16,256]{2,1,0:T(8,128)(2,1)S(1)} %get-tuple-element.28.note, bf16[22,16,256]{2,1,0:T(8,128)(2,1)S(1)} %collective-permute-done.2.partner, ...), custom_call_target="tpu_custom_call" | custom-call | tf_op jit(solution)/shard_map/back/pallas_call | solution.py:430
  (13 shorter events, 0.1 us)
Async XLA Ops:
  1.7 10.8 %collective-permute-start.1 = (bf16[32,4,256]{2,1,0:T(4,128)(2,1)S(1)}, bf16[32,4,256]{2,1,0:T(4,128)(2,1)S(1)}, u32[]{:S(2)}, u32[]{:S(2)}) collective-permute-start(bf16[32,4,256]{2,1,0:T(4,128)(2,1)S(1)} %get-tuple-element.39), channel_id=1, source_target_pairs={{0,1},{1,0},{2,3},{3,2},{4,5},{5,4},{6,7},{7,6},{8,9},{9,8},{10,11... | collective-permute-start | bytes 196616 | tf_op jit(solution)/shard_map/ppermute | solution.py:454
  1.8 10.8 %collective-permute-start = (bf16[32,4,256]{2,1,0:T(4,128)(2,1)S(1)}, bf16[32,4,256]{2,1,0:T(4,128)(2,1)S(1)}, u32[]{:S(2)}, u32[]{:S(2)}) collective-permute-start(bf16[32,4,256]{2,1,0:T(4,128)(2,1)S(1)} %get-tuple-element.40), channel_id=1, source_target_pairs={{0,255},{1,2},{2,1},{3,4},{4,3},{5,6},{6,5},{7,8},{8,7},{9,10},{10... | collective-permute-start | bytes 196616 | tf_op jit(solution)/shard_map/ppermute | solution.py:454
  24.0 1.5 %collective-permute-start.2 = (bf16[22,16,256]{2,1,0:T(8,128)(2,1)S(1)}, bf16[22,16,256]{2,1,0:T(8,128)(2,1)S(1)}, u32[]{:S(2)}, u32[]{:S(2)}) collective-permute-start(bf16[22,16,256]{2,1,0:T(8,128)(2,1)S(1)} %get-tuple-element.28.note), channel_id=1, source_target_pairs={{0,1},{1,0},{2,3},{3,2},{4,5},{5,4},{6,7},{7,6},{8,9},{9,8},{10,11... | collective-permute-start | bytes 540680 | tf_op jit(solution)/shard_map/ppermute | solution.py:454
  25.6 10.1 %collective-permute-start.3 = (bf16[18,16,256]{2,1,0:T(8,128)(2,1)S(1)}, bf16[18,16,256]{2,1,0:T(8,128)(2,1)S(1)}, u32[]{:S(2)}, u32[]{:S(2)}) collective-permute-start(bf16[18,16,256]{2,1,0:T(8,128)(2,1)S(1)} %constant_dynamic-update-slice_fusion), channel_id=1, source_target_pairs={{0,255},{1,2},{2,1},{3,4},{4,3},{5,6},{6,5},{7,8},{8,7},{9,10},{10... | collective-permute-start | bytes 442376 | tf_op jit(solution)/shard_map/ppermute | solution.py:454
  32.9 8.2 %collective-permute-start.5 = (bf16[8,16,256]{2,1,0:T(8,128)(2,1)S(1)}, bf16[8,16,256]{2,1,0:T(8,128)(2,1)S(1)}, u32[]{:S(2)}, u32[]{:S(2)}) collective-permute-start(bf16[8,16,256]{2,1,0:T(8,128)(2,1)S(1)} %pad_maximum_fusion.1), channel_id=1, source_target_pairs={{0,253},{1,4},{2,255},{3,6},{4,1},{5,8},{6,3},{7,10},{8,5},{9,12},... | collective-permute-start | bytes 196616 | tf_op jit(solution)/shard_map/ppermute | solution.py:454
  35.8 5.3 %collective-permute-start.4 = (bf16[8,16,256]{2,1,0:T(8,128)(2,1)S(1)}, bf16[8,16,256]{2,1,0:T(8,128)(2,1)S(1)}, u32[]{:S(2)}, u32[]{:S(2)}) collective-permute-start(bf16[8,16,256]{2,1,0:T(8,128)(2,1)S(1)} %pad_maximum_fusion), channel_id=1, source_target_pairs={{0,1},{1,0},{2,3},{3,2},{4,5},{5,4},{6,7},{7,6},{8,9},{9,8},{10,11... | collective-permute-start | bytes 196616 | tf_op jit(solution)/shard_map/ppermute | solution.py:454

commit v8 on v7

--- a/solution.py
+++ b/solution.py
@@ -24,7 +24,7 @@
 TILE_H = 16
 TILE = TILE_H * COLS
 UNROLL = 2
-TALL_H = 16
+TALL_H = 8
 TALL = TALL_H * COLS
 F32 = jnp.float32
 BF16 = jnp.bfloat16

time: 46.9 us -> 46.8 us (level)
  no operation moved by 1% of the time
where the time goes in v8:
time: 46.8 us; the launch traced here: 46.7 us
  Pallas kernels  18.8 us (40%)
  starting transfers between devices  17.3 us (37%)
  waiting for transfers between devices  8.63 us (18%)
  other arithmetic  1.14 us (2%)
  between operations  0.76 us (2%)
    ppermute x6, starting transfers between devices, swapped(): return lax.ppermute(block, AXES, route)  17.3 us
    pallas_call x1, Pallas kernels, front(): pl.pallas_call(front_kernel, out_shape=(jax.ShapeDtypeStruct((ROWS + 2, W...  11.4 us
    ppermute x6, waiting for transfers between devices, swapped(): return lax.ppermute(block, AXES, route)  8.63 us
    pallas_call x1, Pallas kernels, back(): pl.pallas_call(back_kernel, out_shape=(jax.ShapeDtypeStruct((BR, BA, C),...  5.55 us
    pallas_call x1, Pallas kernels, prepare(): pl.pallas_call(prepare_kernel, out_shape=(jax.ShapeDtypeStruct((ROWS + 2,...  1.85 us
    select_n x1, other arithmetic, local(): beside = swapped(jnp.where(odd, left_edge, right_edge), -1)  1.05 us
  transfers between devices with their start and end apart: 6, of which 4 were waited for; matrix products, arithmetic and copies ran while one was open for 0% of the time, Pallas kernels for 4%

profile of v8, /device:TPU:0, one launch (start us, length us, event | category | flops | bytes accessed | tf_op | source)
XLA Modules:
  0.0 46.7 jit_solution(5575391341793351299)
XLA Ops:
  0.6 1.0 %broadcast_select_fusion = (bf16[32,4,256]{2,1,0:T(4,128)(2,1)S(1)}, bf16[32,4,256]{2,1,0:T(4,128)(2,1)S(1)}) fusion(pred[]{:T(512)S(6)} %eq.5, bf16[32,64,256]{2,1,0:T(8,128)(2,1)} %image.1), kind=kLoop, calls=%fused_computation.4 | loop fusion | flops 65536 | bytes 262145 | tf_op jit(solution)/shard_map/jit(_where)/select_n | solution.py:466
  1.7 0.1 collective-permute-start.1
  1.8 8.9 %collective-permute-start = (bf16[32,4,256]{2,1,0:T(4,128)(2,1)S(1)}, bf16[32,4,256]{2,1,0:T(4,128)(2,1)S(1)}, u32[]{:S(2)}, u32[]{:S(2)}) collective-permute-start(bf16[32,4,256]{2,1,0:T(4,128)(2,1)S(1)} %get-tuple-element.40), channel_id=1, source_target_pairs={{0,255},{1,2},{2,1},{3,4},{4,3},{5,6},{6,5},{7,8},{8,7},{9,10},{10... | collective-permute-start | bytes 196616 | tf_op jit(solution)/shard_map/ppermute | solution.py:454
  10.7 1.8 %prepare.1 = (bf16[34,72,256]{2,1,0:T(8,128)(2,1)S(1)}, bf16[9,256,256]{2,1,0:T(8,128)(2,1)S(1)}, bf16[1536,256]{1,0:T(8,128)(2,1)S(1)}, bf16[128,256]{1,0:T(8,1...) custom-call(s32[1]{0:T(128)} %bitcast.me_ref, ...), custom_call_target="tpu_custom_call" | custom-call | flops 100000000 | bytes 8388608 | tf_op jit(solution)/shard_map/prepare/pallas_call | solution.py:140
  12.5 0.0 collective-permute-done.1.beside
  12.5 0.1 collective-permute-done.crossed
  12.6 11.4 %front.1 = (bf16[34,72,256]{2,1,0:T(8,128)(2,1)S(1)}, bf16[2048,256]{1,0:T(8,128)(2,1)S(1)}, bf16[2048,256]{1,0:T(8,128)(2,1)S(1)}, f32[256,256]{1,0:T(8,128)S(1...) custom-call(s32[1]{0:T(128)} %bitcast.me_ref, ...), custom_call_target="tpu_custom_call", output_to_operand_aliasing={{0}: (1, {})} | custom-call | tf_op jit(solution)/shard_map/front/pallas_call | solution.py:285
  24.0 0.1 collective-permute-start.2
  24.2 1.4 %collective-permute-done.2.partner = bf16[22,16,256]{2,1,0:T(8,128)(2,1)S(1)} collective-permute-done((bf16[22,16,256]{2,1,0:T(8,128)(2,1)S(1)}, bf16[22,16,256]{2,1,0:T(8,128)(2,1)S(1)}, u32[]{:S(2)}, u32[]{:S(2)}) %collective-permute-start.2) | collective-permute-done | bytes 180256 | tf_op jit(solution)/shard_map/ppermute | solution.py:454
  25.6 7.3 %collective-permute-start.3 = (bf16[18,16,256]{2,1,0:T(8,128)(2,1)S(1)}, bf16[18,16,256]{2,1,0:T(8,128)(2,1)S(1)}, u32[]{:S(2)}, u32[]{:S(2)}) collective-permute-start(bf16[18,16,256]{2,1,0:T(8,128)(2,1)S(1)} %constant_dynamic-update-slice_fusion), channel_id=1, source_target_pairs={{0,255},{1,2},{2,1},{3,4},{4,3},{5,6},{6,5},{7,8},{8,7},{9,10},{10... | collective-permute-start | bytes 442376 | tf_op jit(solution)/shard_map/ppermute | solution.py:454
  32.9 0.9 %collective-permute-start.5 = (bf16[8,16,256]{2,1,0:T(8,128)(2,1)S(1)}, bf16[8,16,256]{2,1,0:T(8,128)(2,1)S(1)}, u32[]{:S(2)}, u32[]{:S(2)}) collective-permute-start(bf16[8,16,256]{2,1,0:T(8,128)(2,1)S(1)} %pad_maximum_fusion.1), channel_id=1, source_target_pairs={{0,253},{1,4},{2,255},{3,6},{4,1},{5,8},{6,3},{7,10},{8,5},{9,12},... | collective-permute-start | bytes 196616 | tf_op jit(solution)/shard_map/ppermute | solution.py:454
  33.8 1.9 %collective-permute-done.3.crossed = bf16[18,16,256]{2,1,0:T(8,128)(2,1)S(1)} collective-permute-done((bf16[18,16,256]{2,1,0:T(8,128)(2,1)S(1)}, bf16[18,16,256]{2,1,0:T(8,128)(2,1)S(1)}, u32[]{:S(2)}, u32[]{:S(2)}) %collective-permute-start.3) | collective-permute-done | bytes 147488 | tf_op jit(solution)/shard_map/ppermute | solution.py:454
  35.8 0.1 collective-permute-start.4
  35.9 5.2 %collective-permute-done.5 = bf16[8,16,256]{2,1,0:T(8,128)(2,1)S(1)} collective-permute-done((bf16[8,16,256]{2,1,0:T(8,128)(2,1)S(1)}, bf16[8,16,256]{2,1,0:T(8,128)(2,1)S(1)}, u32[]{:S(2)}, u32[]{:S(2)}) %collective-permute-start.5) | collective-permute-done | bytes 65568 | tf_op jit(solution)/shard_map/ppermute | solution.py:454
  41.1 0.0 collective-permute-done.4.relayed
  41.1 5.6 %back.1 = (bf16[16,4,256]{2,1,0:T(4,128)(2,1)}, bf16[32,64,256]{2,1,0:T(8,128)(2,1)}, bf16[64,128]{1,0:T(8,128)(2,1)}) custom-call(s32[1]{0:T(128)} %bitcast.me_ref, f32[256,256]{1,0:T(8,128)S(1)} %get-tuple-element.27.lifted, bf16[22,16,256]{2,1,0:T(8,128)(2,1)S(1)} %get-tuple-element.28.note, bf16[22,16,256]{2,1,0:T(8,128)(2,1)S(1)} %collective-permute-done.2.partner, ...), custom_call_target="tpu_custom_call" | custom-call | tf_op jit(solution)/shard_map/back/pallas_call | solution.py:430
  (13 shorter events, 0.1 us)
Async XLA Ops:
  1.7 10.8 %collective-permute-start.1 = (bf16[32,4,256]{2,1,0:T(4,128)(2,1)S(1)}, bf16[32,4,256]{2,1,0:T(4,128)(2,1)S(1)}, u32[]{:S(2)}, u32[]{:S(2)}) collective-permute-start(bf16[32,4,256]{2,1,0:T(4,128)(2,1)S(1)} %get-tuple-element.39), channel_id=1, source_target_pairs={{0,1},{1,0},{2,3},{3,2},{4,5},{5,4},{6,7},{7,6},{8,9},{9,8},{10,11... | collective-permute-start | bytes 196616 | tf_op jit(solution)/shard_map/ppermute | solution.py:454
  1.8 10.8 %collective-permute-start = (bf16[32,4,256]{2,1,0:T(4,128)(2,1)S(1)}, bf16[32,4,256]{2,1,0:T(4,128)(2,1)S(1)}, u32[]{:S(2)}, u32[]{:S(2)}) collective-permute-start(bf16[32,4,256]{2,1,0:T(4,128)(2,1)S(1)} %get-tuple-element.40), channel_id=1, source_target_pairs={{0,255},{1,2},{2,1},{3,4},{4,3},{5,6},{6,5},{7,8},{8,7},{9,10},{10... | collective-permute-start | bytes 196616 | tf_op jit(solution)/shard_map/ppermute | solution.py:454
  24.0 1.5 %collective-permute-start.2 = (bf16[22,16,256]{2,1,0:T(8,128)(2,1)S(1)}, bf16[22,16,256]{2,1,0:T(8,128)(2,1)S(1)}, u32[]{:S(2)}, u32[]{:S(2)}) collective-permute-start(bf16[22,16,256]{2,1,0:T(8,128)(2,1)S(1)} %get-tuple-element.28.note), channel_id=1, source_target_pairs={{0,1},{1,0},{2,3},{3,2},{4,5},{5,4},{6,7},{7,6},{8,9},{9,8},{10,11... | collective-permute-start | bytes 540680 | tf_op jit(solution)/shard_map/ppermute | solution.py:454
  25.6 10.1 %collective-permute-start.3 = (bf16[18,16,256]{2,1,0:T(8,128)(2,1)S(1)}, bf16[18,16,256]{2,1,0:T(8,128)(2,1)S(1)}, u32[]{:S(2)}, u32[]{:S(2)}) collective-permute-start(bf16[18,16,256]{2,1,0:T(8,128)(2,1)S(1)} %constant_dynamic-update-slice_fusion), channel_id=1, source_target_pairs={{0,255},{1,2},{2,1},{3,4},{4,3},{5,6},{6,5},{7,8},{8,7},{9,10},{10... | collective-permute-start | bytes 442376 | tf_op jit(solution)/shard_map/ppermute | solution.py:454
  32.9 8.2 %collective-permute-start.5 = (bf16[8,16,256]{2,1,0:T(8,128)(2,1)S(1)}, bf16[8,16,256]{2,1,0:T(8,128)(2,1)S(1)}, u32[]{:S(2)}, u32[]{:S(2)}) collective-permute-start(bf16[8,16,256]{2,1,0:T(8,128)(2,1)S(1)} %pad_maximum_fusion.1), channel_id=1, source_target_pairs={{0,253},{1,4},{2,255},{3,6},{4,1},{5,8},{6,3},{7,10},{8,5},{9,12},... | collective-permute-start | bytes 196616 | tf_op jit(solution)/shard_map/ppermute | solution.py:454
  35.8 5.3 %collective-permute-start.4 = (bf16[8,16,256]{2,1,0:T(8,128)(2,1)S(1)}, bf16[8,16,256]{2,1,0:T(8,128)(2,1)S(1)}, u32[]{:S(2)}, u32[]{:S(2)}) collective-permute-start(bf16[8,16,256]{2,1,0:T(8,128)(2,1)S(1)} %pad_maximum_fusion), channel_id=1, source_target_pairs={{0,1},{1,0},{2,3},{3,2},{4,5},{5,4},{6,7},{7,6},{8,9},{9,8},{10,11... | collective-permute-start | bytes 196616 | tf_op jit(solution)/shard_map/ppermute | solution.py:454
